TPU v7x, 128 devices: a whole 4x4x4 slice. The times are simulated.
128 devices in a mesh: illum: 2 (over y_hi), slab: 64 (over z, y_lo, x, core).
Axes of the slice: x: 4, y: 4 (y_hi: 2, y_lo: 2; y = y_hi * 2 + y_lo), z: 4, core: 2. Of those that a mesh axis runs over, the one named last changes fastest.
Arguments:
- incident: bfloat16 [2, 2, 256, 256, 128], P('illum', None, 'slab'), may hold values from -6 to 6
- field_now: float32 [2, 2, 256, 256, 128], P('illum', None, 'slab'), may hold values from -6 to 6
- contrast: float32 [256, 256, 128], P('slab'), may hold values from 0 to 0.5
- green_spectrum: float32 [2, 256, 256, 128], P(None, None, 'slab'), may hold values from -6 to 6
- detector_data: float32 [2, 2, 256, 128], P('illum', None, 'slab'), may hold values from -6 to 6
Outputs:
- field_next: float32 [2, 2, 256, 256, 128], P('illum', None, 'slab')
- misfit: float32 [2, 2, 256, 128], P('illum', None, 'slab')
- contrast_next: float32 [256, 256, 128], P('slab')
All inputs are finite; a program needn't handle non-finite values.
Results may differ from a plain program's by a relative error of at most 0.0003.
Values sent between devices are 32-bit elements; how exact they have to be, the bound alone decides.
No kernel may reach another device: no remote copies, remote signals or barrier semaphores. Data moves between devices by JAX's collectives and lax.ppermute only.
A program may use at most 64 MiB of HBM per device.

v0:
```python
import math

import jax
import jax.numpy as jnp
import ml_dtypes
import numpy as np
from jax import lax
from jax.experimental import pallas as pl
from jax.experimental.pallas import tpu as pltpu
from jax.sharding import PartitionSpec as P

wave_number = 1.2
step_size = 2.0
diffusion = 0.02
edge_scale = 0.25
f32 = jnp.float32
bf16 = jnp.bfloat16
PASSES = 4


def halves(table):
    high = table.astype(ml_dtypes.bfloat16)
    low = (table - high.astype(np.float64)).astype(ml_dtypes.bfloat16)
    return high, low


def circle(length):
    counter = np.arange(length)
    angle = (counter[:, None] * counter[None, :] % length) * (2.0 * math.pi / length)
    scale = 1.0 / math.sqrt(length)
    return np.cos(angle) * scale, np.sin(angle) * scale


def tall(cosine, sine):
    return halves(np.concatenate([cosine, sine], 0))


def split(value):
    high = value.astype(bf16)
    return high, (value - high.astype(f32)).astype(bf16)


def product(left, right):
    left_high, left_low = left
    right_high, right_low = right
    small = jnp.dot(left_high, right_low, preferred_element_type=f32)
    small += jnp.dot(left_low, right_high, preferred_element_type=f32)
    return jnp.dot(left_high, right_high, preferred_element_type=f32) + small


def mix_rows(table, wide, sign):
    both = product(table, split(wide))
    rows, lanes = wide.shape[0], wide.shape[1] // 2
    cos_re, cos_im = both[:rows, :lanes], both[:rows, lanes:]
    sin_re, sin_im = both[rows:, :lanes], both[rows:, lanes:]
    if sign < 0:
        return cos_re + sin_im, cos_im - sin_re
    return cos_re - sin_im, cos_im + sin_re


def forward_kernel(local, block, slabs, field, contrast, xh, xl, yh, yl, out):
    plane = pl.program_id(0)
    value = contrast[0]
    wide = jnp.concatenate([field[0, 0] * value, field[1, 0] * value], 1)
    wide = product(split(wide), (yh[...], yl[...]))
    parts = mix_rows((xh[...], xl[...]), wide, -1.0)
    for part in range(2):
        for row in range(block):
            spot = plane * (2 * block) + part * block + row
            out[pl.ds(spot, slabs, stride=local * 2 * block), :] = parts[part][
                row * slabs : (row + 1) * slabs
            ]


def detect_kernel(depth, slabs, root_depth, columns, steps, measured, out, spread):
    half = out.shape[0] // 2
    same, cross = steps[0], steps[1]
    same_far, cross_far = steps[2], steps[3]
    run = 16
    groups = depth // run
    totals = [None] * groups
    for inner in range(run):
        for group in range(groups):
            value = columns[pl.ds((group * run + inner) * 2 * half, 2 * half), :]
            if inner > 0:
                value = value + totals[group]
            totals[group] = value * same + pltpu.roll(value, half, 0) * cross
    total = totals[0]
    for group in range(1, groups):
        total = total * same_far + pltpu.roll(total, half, 0) * cross_far + totals[group]
    miss = total * (1.0 / root_depth) - measured[...]
    out[...] = miss
    for slab in range(slabs):
        spread[slab] = miss


def depth_kernel(depth, block, columns, green, zh, zl, out):
    row = pl.program_id(0)
    table = (zh[...], zl[...])
    stride = 2 * block
    wide = jnp.concatenate(
        [columns[pl.ds(part * block + row, depth, stride=stride), :] for part in range(2)], 1
    )
    deep_real, deep_imag = mix_rows(table, wide, -1.0)
    green_real = green[pl.ds(row, depth, stride=block), :]
    green_imag = green[pl.ds(depth * block + row, depth, stride=block), :]
    wide = jnp.concatenate(
        [
            green_real * deep_real - green_imag * deep_imag,
            green_real * deep_imag + green_imag * deep_real,
        ],
        1,
    )
    parts = mix_rows(table, wide, 1.0)
    for part in range(2):
        out[pl.ds(part * block + row, depth, stride=stride), :] = parts[part]


def gradient_kernel(
    block, slabs, root_depth, gathered, prop, step, field, xh, xl, yh, yl, out, hold
):
    @pl.when(pl.program_id(0) == 0)
    def _():
        hold[...] = prop[...]

    miss = [
        jnp.concatenate(
            [
                gathered[pl.ds(part * block + row, slabs, stride=2 * block), :]
                for row in range(block)
            ],
            0,
        )
        for part in range(2)
    ]
    real, imag = hold[0], hold[1]
    wide = jnp.concatenate(
        [real * miss[0] + imag * miss[1], real * miss[1] - imag * miss[0]], 1
    ) * (1.0 / root_depth)
    wide = jnp.concatenate(mix_rows((xh[...], xl[...]), wide, 1.0), 1)
    wide = product(split(wide), (yh[...], yl[...]))
    lanes = wide.shape[1] // 2
    out[0] = field[0, 0] * wide[:, :lanes] + field[1, 0] * wide[:, lanes:]
    hold[0] = real * step[0] - imag * step[1]
    hold[1] = real * step[1] + imag * step[0]


def field_kernel(local, block, slabs, volume, incident, xh, xl, yh, yl, out):
    plane = pl.program_id(0)
    stride = local * 2 * block
    wide = jnp.concatenate(
        [
            jnp.concatenate(
                [
                    volume[
                        pl.ds(plane * (2 * block) + part * block + row, slabs, stride=stride), :
                    ]
                    for row in range(block)
                ],
                0,
            )
            for part in range(2)
        ],
        1,
    )
    wide = jnp.concatenate(mix_rows((xh[...], xl[...]), wide, 1.0), 1)
    wide = product(split(wide), (yh[...], yl[...]))
    lanes = wide.shape[1] // 2
    out[0, 0] = incident[0, 0].astype(f32) + wide[:, :lanes]
    out[1, 0] = incident[1, 0].astype(f32) + wide[:, lanes:]


def smooth_kernel(depth, limits, before, own, after, out, ping, pong):
    local, rows, lanes = own.shape
    total = local + 2 * PASSES
    ping[:PASSES] = before[...]
    ping[PASSES : PASSES + local] = own[...]
    ping[PASSES + local :] = after[...]
    last_row = lax.broadcasted_iota(jnp.int32, (rows, lanes), 0) == rows - 1
    last_lane = lax.broadcasted_iota(jnp.int32, (rows, lanes), 1) == lanes - 1
    first = limits[0]
    source, target = ping, pong
    for repeat in range(PASSES):
        final = repeat == PASSES - 1

        def inside(plane):
            spot = first + plane
            return jnp.where((spot >= 0) & (spot <= depth - 2), 1.0, 0.0).astype(f32)

        def body(plane, carry, source=source, target=target, final=final):
            core = source[plane]
            slope_depth = (source[plane + 1] - core) * inside(plane)
            slope_rows = jnp.where(last_row, 0.0, pltpu.roll(core, rows - 1, 0) - core)
            slope_lanes = jnp.where(last_lane, 0.0, pltpu.roll(core, lanes - 1, 1) - core)
            scale = lax.rsqrt(
                slope_depth * slope_depth
                + slope_rows * slope_rows
                + slope_lanes * slope_lanes
                + edge_scale**2
            )
            flux_depth = slope_depth * scale
            flux_rows = slope_rows * scale
            flux_lanes = slope_lanes * scale
            spread = (
                (flux_depth - carry)
                + (flux_rows - pltpu.roll(flux_rows, 1, 0))
                + (flux_lanes - pltpu.roll(flux_lanes, 1, 1))
            )
            value = core + diffusion * spread
            if final:
                out[plane - PASSES] = value
            else:
                target[plane] = value
            return flux_depth

        low, high = repeat + 1, total - 1 - repeat
        core = source[low - 1]
        slope_depth = (source[low] - core) * inside(low - 1)
        slope_rows = jnp.where(last_row, 0.0, pltpu.roll(core, rows - 1, 0) - core)
        slope_lanes = jnp.where(last_lane, 0.0, pltpu.roll(core, lanes - 1, 1) - core)
        carry = slope_depth * lax.rsqrt(
            slope_depth * slope_depth
            + slope_rows * slope_rows
            + slope_lanes * slope_lanes
            + edge_scale**2
        )
        lax.fori_loop(low, high, body, carry)
        source, target = target, source


def frequency(index, length):
    shifted = jnp.where(index < length // 2, index, index - length)
    return shifted.astype(f32) * (2.0 * math.pi / length)


def propagator(distance, row_index, width_x, width_y):
    along_x = frequency(row_index, width_x)
    along_y = frequency(jnp.arange(width_y, dtype=jnp.int32), width_y)
    squared = wave_number**2 - along_x[:, None] ** 2 - along_y[None, :] ** 2
    root = jnp.sqrt(jnp.abs(squared))
    moving = squared > 0.0
    amplitude = jnp.where(moving, 1.0, jnp.exp(-root * distance))
    phase = jnp.where(moving, root * distance, 0.0)
    return amplitude * jnp.cos(phase), amplitude * jnp.sin(phase)


def whole(shape):
    return pl.BlockSpec(shape, lambda i: (0,) * len(shape))


def params():
    return pltpu.CompilerParams(vmem_limit_bytes=48 * 2**20)


def shards(incident, field_now, contrast, green_spectrum, detector_data):
    slabs = lax.axis_size("slab")
    place = lax.axis_index("slab")
    local, width_x, width_y = contrast.shape
    depth = local * slabs
    block = width_x // slabs
    root_depth = math.sqrt(depth)
    chunk = local * 2 * block
    lines = slabs * chunk

    order = np.arange(width_x)
    order = block * (order % slabs) + order // slabs
    cos_x, sin_x = circle(width_x)
    cos_y, sin_y = circle(width_y)
    ahead_x = tall(cos_x[order], sin_x[order])
    back_x = tall(cos_x[:, order], sin_x[:, order])
    ahead_z = tall(*circle(depth))
    ahead_y = halves(np.block([[cos_y, -sin_y], [sin_y, cos_y]]))
    back_y = halves(np.block([[cos_y, sin_y], [-sin_y, cos_y]]))
    x_spec, y_spec = whole((2 * width_x, width_x)), whole((2 * width_y, 2 * width_y))
    table_specs = [x_spec, x_spec, y_spec, y_spec]

    field = field_now[0]
    plane_spec = pl.BlockSpec((1, width_x, width_y), lambda i: (i, 0, 0))
    pair_spec = pl.BlockSpec((2, 1, width_x, width_y), lambda i: (0, i, 0, 0))

    packed = pl.pallas_call(
        lambda *refs: forward_kernel(local, block, slabs, *refs),
        out_shape=jax.ShapeDtypeStruct((lines, width_y), f32),
        grid=(local,),
        in_specs=[pair_spec, plane_spec] + table_specs,
        out_specs=whole((lines, width_y)),
        compiler_params=params(),
        name="forward",
    )(field, contrast, *ahead_x, *ahead_y)
    columns = lax.all_to_all(packed.reshape(slabs, chunk, width_y), "slab", 0, 0, tiled=True)
    columns = columns.reshape(lines, width_y)

    mine = place * block + jnp.arange(block, dtype=jnp.int32)
    steps = []
    for distance in (1.0, 16.0):
        real, imag = propagator(distance, mine, width_x, width_y)
        steps += [jnp.concatenate([real, real]), jnp.concatenate([-imag, imag])]
    steps = jnp.stack(steps)
    miss, spread = pl.pallas_call(
        lambda *refs: detect_kernel(depth, slabs, root_depth, *refs),
        out_shape=(
            jax.ShapeDtypeStruct((2 * block, width_y), f32),
            jax.ShapeDtypeStruct((slabs, 2 * block, width_y), f32),
        ),
        compiler_params=params(),
        name="detect",
    )(columns, steps, detector_data.reshape(2 * block, width_y))
    gathered = lax.all_to_all(spread, "slab", 0, 0, tiled=True)

    z_spec = whole((2 * depth, depth))
    volume = pl.pallas_call(
        lambda *refs: depth_kernel(depth, block, *refs),
        out_shape=jax.ShapeDtypeStruct((lines, width_y), f32),
        grid=(block,),
        in_specs=[whole((lines, width_y)), whole((lines, width_y)), z_spec, z_spec],
        out_specs=whole((lines, width_y)),
        compiler_params=params(),
        name="depth",
    )(columns, green_spectrum.reshape(lines, width_y), *ahead_z)
    volume = lax.all_to_all(volume.reshape(slabs, chunk, width_y), "slab", 0, 0, tiled=True)

    row_index = jnp.arange(width_x, dtype=jnp.int32)
    row_index = block * (row_index % slabs) + row_index // slabs
    nearest = (depth - place * local - (local - 1)).astype(f32)
    prop = jnp.stack(propagator(nearest, row_index, width_x, width_y))
    step = jnp.stack(propagator(1.0, row_index, width_x, width_y))
    terms = pl.pallas_call(
        lambda *refs: gradient_kernel(block, slabs, root_depth, *refs),
        out_shape=jax.ShapeDtypeStruct((local, width_x, width_y), f32),
        grid=(local,),
        in_specs=[
            whole((slabs * 2 * block, width_y)),
            whole((2, width_x, width_y)),
            whole((2, width_x, width_y)),
            pl.BlockSpec((2, 1, width_x, width_y), lambda i: (0, local - 1 - i, 0, 0)),
        ]
        + table_specs,
        out_specs=pl.BlockSpec((1, width_x, width_y), lambda i: (local - 1 - i, 0, 0)),
        scratch_shapes=[pltpu.VMEM((2, width_x, width_y), f32)],
        compiler_params=params(),
        name="gradient",
    )(gathered.reshape(slabs * 2 * block, width_y), prop, step, field, *back_x, *back_y)
    terms = terms + lax.ppermute(terms, "illum", [(0, 1), (1, 0)])
    updated = contrast - step_size * terms

    up = [(i, i + 1) for i in range(slabs - 1)]
    before = lax.ppermute(updated, "slab", up)
    after = lax.ppermute(updated, "slab", [(j, i) for i, j in up])

    field_next = pl.pallas_call(
        lambda *refs: field_kernel(local, block, slabs, *refs),
        out_shape=jax.ShapeDtypeStruct((2, local, width_x, width_y), f32),
        grid=(local,),
        in_specs=[whole((lines, width_y)), pair_spec] + table_specs,
        out_specs=pair_spec,
        compiler_params=params(),
        name="field",
    )(volume.reshape(lines, width_y), incident[0], *back_x, *back_y)

    limits = (place * local - PASSES).astype(jnp.int32).reshape(1)
    work = pltpu.VMEM((local + 2 * PASSES, width_x, width_y), f32)
    vmem = pl.BlockSpec(memory_space=pltpu.VMEM)
    smoothed = pl.pallas_call(
        lambda *refs: smooth_kernel(depth, *refs),
        out_shape=jax.ShapeDtypeStruct((local, width_x, width_y), f32),
        in_specs=[pl.BlockSpec(memory_space=pltpu.SMEM), vmem, vmem, vmem],
        out_specs=vmem,
        scratch_shapes=[work, work],
        compiler_params=params(),
        name="smooth",
    )(limits, before, updated, after)
    return (field_next[None], miss.reshape(1, 2, block, width_y), smoothed)


def solution(mesh):
    placed = (
        P("illum", None, "slab", None, None),
        P("illum", None, "slab", None, None),
        P("slab", None, None),
        P(None, None, "slab", None),
        P("illum", None, "slab", None),
    )
    return jax.shard_map(
        shards,
        mesh=mesh,
        in_specs=placed,
        out_specs=(
            P("illum", None, "slab", None, None),
            P("illum", None, "slab", None),
            P("slab", None, None),
        ),
        check_vma=False,
    )
```

profile of v0, /device:TPU:1, one launch (start us, length us, event | category | flops | bytes accessed | tf_op | source)
XLA Modules:
  0.0 105.1 jit_solution(16682299278022640882)
XLA Ops:
  0.6 0.0 copy-start
  0.6 1.2 %copy-done = f32[1,2,4,256,128]{4,3,2,1,0:T(8,128)S(1)} copy-done((f32[1,2,4,256,128]{4,3,2,1,0:T(8,128)S(1)}, f32[1,2,4,256,128]{4,3,2,1,0:T(8,128)}, u32[]{:S(2)}) %copy-start) | copy-done | bytes 1048600
  1.9 0.0 copy-start.2
  1.9 1.0 copy-done.2
  2.9 0.0 copy-start.15
  2.9 0.9 copy-done.15
  3.9 0.0 copy-start.16
  3.9 0.9 copy-done.16
  4.8 0.0 copy-start.17
  4.8 0.9 copy-done.17
  5.7 0.0 copy-start.18
  5.7 0.9 copy-done.18
  6.6 4.8 %forward.1 = f32[2048,128]{1,0:T(8,128)} custom-call(f32[2,4,256,128]{3,2,1,0:T(8,128)S(1)} %bitcast.22, f32[4,256,128]{2,1,0:T(8,128)S(1)} %copy-done.2, bf16[512,256]{1,0:T(8,128)(2,1)S(1)} %copy-done.16, bf16[512,256]{1,0:T(8,128)(2,1)S(1)} %copy-done.15, bf16[256,256]{1,0:T(8,128)(2,1)S(1)} %copy-done.18, bf16[256,256]{1,0:T(8,128)(2,1)S(1)} %copy-done.17), custom_call_target="tpu_custom_call" | custom-call | tf_op jit(solution)/shard_map/forward/pallas_call | solution.py:281
  11.4 10.8 %all-to-all-start = ((f32[64,32,128]{2,1,0:T(8,128)}), f32[64,32,128]{2,1,0:T(8,128)S(1)}, u32[]{:S(2)}, u32[]{:S(2)}) async-start(f32[64,32,128]{2,1,0:T(8,128)} %bitcast.1), calls=%async_computation | async-start | bytes 2097152 | tf_op jit(solution)/shard_map/all_to_all | solution.py:290
  22.3 0.1 cosine_multiply_fusion.1
  22.4 0.0 copy-start.19
  22.5 17.8 %all-to-all-done = f32[64,32,128]{2,1,0:T(8,128)S(1)} async-done(((f32[64,32,128]{2,1,0:T(8,128)}), f32[64,32,128]{2,1,0:T(8,128)S(1)}, u32[]{:S(2)}, u32[]{:S(2)}) %all-to-all-start) | async-done | bytes 1048608 | tf_op jit(solution)/shard_map/all_to_all | solution.py:290
  40.3 0.0 copy-done.19
  40.3 0.9 detect.1
  41.2 0.0 copy-start.1
  41.2 4.9 %all-to-all-start.2 = ((f32[64,8,128]{2,1,0:T(8,128)}), f32[64,8,128]{2,1,0:T(8,128)S(1)}, u32[]{:S(2)}, u32[]{:S(2)}) async-start(f32[64,8,128]{2,1,0:T(8,128)} %get-tuple-element.6), calls=%async_computation.2 | async-start | bytes 524288 | tf_op jit(solution)/shard_map/all_to_all | solution.py:308
  46.0 1.1 %fusion.11 = (f32[1,256,128]{2,1,0:T(8,128)S(1)}, f32[1,256,128]{2,1,0:T(8,128)S(1)}, f32[1,256,128]{2,1,0:T(8,128)S(1)}, f32[1,256,128]{2,1,0:T(8,128)S(1)}) fusion(f32[128]{0:T(128)S(1)} %fusion.42, f32[256]{0:T(256)S(1)} %fusion.35, f32[]{:T(128)S(6)} %convert_element_type.54), kind=kLoop, calls=%fused_computation.16 | loop fusion | flops 458752 | bytes 525828 | tf_op jit(solution)/shard_map/mul | solution.py:244
  47.1 0.0 copy-start.10
  47.2 8.6 %all-to-all-done.2 = f32[64,8,128]{2,1,0:T(8,128)S(1)} async-done(((f32[64,8,128]{2,1,0:T(8,128)}), f32[64,8,128]{2,1,0:T(8,128)S(1)}, u32[]{:S(2)}, u32[]{:S(2)}) %all-to-all-start.2) | async-done | bytes 262176 | tf_op jit(solution)/shard_map/all_to_all | solution.py:308
  55.8 0.0 copy-done.1
  55.8 0.0 copy-done.10
  55.8 0.0 copy-start.5
  55.8 0.9 copy-done.5
  56.8 0.0 copy-start.7
  56.8 0.9 copy-done.7
  57.8 0.0 copy-start.11
  57.8 0.9 copy-done.11
  58.7 0.0 copy-start.4
  58.7 0.0 copy-start.13
  58.7 0.0 copy-start.14
  58.7 3.2 %gradient.1 = f32[4,256,128]{2,1,0:T(8,128)S(1)} custom-call(f32[512,128]{1,0:T(8,128)S(1)} %bitcast.26, f32[2,256,128]{2,1,0:T(8,128)S(1)} %get-tuple-element.21.refs_1_, f32[2,256,128]{2,1,0:T(8,128)S(1)} %get-tuple-element.22.refs_2_, f32[2,4,256,128]{3,2,1,0:T(8,128)S(1)} %bitcast.23, bf16[512,256]{1,0:T(8,128)(2,1)S(1)} %copy-done.7, ...), custom_call_target="tpu_custom_call" | custom-call | tf_op jit(solution)/shard_map/gradient/pallas_call | solution.py:327
  61.9 2.7 %collective-permute-start = (f32[4,256,128]{2,1,0:T(8,128)S(1)}, f32[4,256,128]{2,1,0:T(8,128)}, u32[]{:S(2)}, u32[]{:S(2)}) collective-permute-start(f32[4,256,128]{2,1,0:T(8,128)S(1)} %gradient.1), channel_id=1, source_target_pairs={{0,64},{64,0},{1,65},{65,1},{2,66},{66,2},{3,67},{67,3},{4,68},{68... | collective-permute-start | bytes 1572872 | tf_op jit(solution)/shard_map/ppermute | solution.py:343
  64.6 0.0 copy-done.4
  64.6 0.0 copy-done.13
  64.6 0.0 copy-done.14
  64.6 5.4 %depth.1 = f32[2048,128]{1,0:T(8,128)} custom-call(f32[2048,128]{1,0:T(8,128)S(1)} %bitcast.21, f32[2048,128]{1,0:T(8,128)S(1)} %bitcast.25, bf16[512,256]{1,0:T(8,128)(2,1)S(1)} %copy-done.14, bf16[512,256]{1,0:T(8,128)(2,1)S(1)} %copy-done.13), custom_call_target="tpu_custom_call" | custom-call | tf_op jit(solution)/shard_map/depth/pallas_call | solution.py:311
  70.0 0.0 copy-start.3
  70.0 5.0 %all-to-all-start.1 = ((f32[64,32,128]{2,1,0:T(8,128)}), f32[64,32,128]{2,1,0:T(8,128)S(1)}, u32[]{:S(2)}, u32[]{:S(2)}) async-start(f32[64,32,128]{2,1,0:T(8,128)} %bitcast.4), calls=%async_computation.1 | async-start | bytes 2097152 | tf_op jit(solution)/shard_map/all_to_all | solution.py:320
  75.0 0.0 copy-start.6
  75.0 0.0 copy-start.8
  75.0 0.0 copy-start.12
  75.0 1.7 %collective-permute-done = f32[4,256,128]{2,1,0:T(8,128)} collective-permute-done((f32[4,256,128]{2,1,0:T(8,128)S(1)}, f32[4,256,128]{2,1,0:T(8,128)}, u32[]{:S(2)}, u32[]{:S(2)}) %collective-permute-start) | collective-permute-done | bytes 524320 | tf_op jit(solution)/shard_map/ppermute | solution.py:343
  76.7 0.0 copy-done.3
  76.7 1.1 %multiply_subtract_fusion.refs_2_ = f32[4,256,128]{2,1,0:T(8,128)S(1)} fusion(f32[4,256,128]{2,1,0:T(8,128)S(1)} %copy-done.3, f32[4,256,128]{2,1,0:T(8,128)S(1)} %gradient.1, f32[4,256,128]{2,1,0:T(8,128)} %collective-permute-done), kind=kLoop, calls=%fused_computation | loop fusion | flops 393216 | bytes 2097152 | tf_op jit(solution)/shard_map/sub | solution.py:344
  77.8 3.9 %collective-permute-start.2 = (f32[4,256,128]{2,1,0:T(8,128)S(1)}, f32[4,256,128]{2,1,0:T(8,128)S(1)}, u32[]{:S(2)}, u32[]{:S(2)}) collective-permute-start(f32[4,256,128]{2,1,0:T(8,128)S(1)} %multiply_subtract_fusion.refs_2_), channel_id=1, source_target_pairs={{1,0},{2,1},{3,2},{4,3},{5,4},{6,5},{7,6},{8,7},{9,8},{10,9},{11,1... | collective-permute-start | bytes 1572872 | tf_op jit(solution)/shard_map/ppermute | solution.py:348
  81.7 1.9 %collective-permute-start.1 = (f32[4,256,128]{2,1,0:T(8,128)S(1)}, f32[4,256,128]{2,1,0:T(8,128)S(1)}, u32[]{:S(2)}, u32[]{:S(2)}) collective-permute-start(f32[4,256,128]{2,1,0:T(8,128)S(1)} %multiply_subtract_fusion.refs_2_), channel_id=1, source_target_pairs={{0,1},{1,2},{2,3},{3,4},{4,5},{5,6},{6,7},{7,8},{8,9},{9,10},{10,1... | collective-permute-start | bytes 1572872 | tf_op jit(solution)/shard_map/ppermute | solution.py:347
  83.6 9.8 %all-to-all-done.1 = f32[64,32,128]{2,1,0:T(8,128)S(1)} async-done(((f32[64,32,128]{2,1,0:T(8,128)}), f32[64,32,128]{2,1,0:T(8,128)S(1)}, u32[]{:S(2)}, u32[]{:S(2)}) %all-to-all-start.1) | async-done | bytes 1048608 | tf_op jit(solution)/shard_map/all_to_all | solution.py:320
  93.4 0.0 copy-done.6
  93.4 0.0 copy-done.8
  93.4 0.0 copy-done.12
  93.4 0.0 copy-start.9
  93.4 1.0 copy-done.9
  94.4 4.1 %field.1 = f32[2,4,256,128]{3,2,1,0:T(8,128)} custom-call(f32[2048,128]{1,0:T(8,128)S(1)} %bitcast.24, bf16[2,4,256,128]{3,2,1,0:T(8,128)(2,1)S(1)} %bitcast.27, bf16[512,256]{1,0:T(8,128)(2,1)S(1)} %copy-done.8, bf16[512,256]{1,0:T(8,128)(2,1)S(1)} %copy-done.6, bf16[256,256]{1,0:T(8,128)(2,1)S(1)} %copy-done.12, bf16[256,256]{1,0:T(8,128)(2,1)S(1)} %copy-done.10), custom_call_target="tpu_custom_call" | custom-call | tf_op jit(solution)/shard_map/field/pallas_call | solution.py:350
  98.6 0.0 collective-permute-done.2.refs_3_
  98.6 0.0 collective-permute-done.1.refs_1_
  98.6 6.5 %smooth.1 = f32[4,256,128]{2,1,0:T(8,128)} custom-call(s32[1]{0:T(128)} %bitcast.14.refs_0_, f32[4,256,128]{2,1,0:T(8,128)S(1)} %collective-permute-done.1.refs_1_, f32[4,256,128]{2,1,0:T(8,128)S(1)} %multiply_subtract_fusion.refs_2_, f32[4,256,128]{2,1,0:T(8,128)S(1)} %collective-permute-done.2.refs_3_), custom_call_target="tpu_custom_call" | custom-call | tf_op jit(solution)/shard_map/smooth/pallas_call | solution.py:363
  (7 shorter events, 0.1 us)
Async XLA Ops:
  0.6 1.2 %copy-start = (f32[1,2,4,256,128]{4,3,2,1,0:T(8,128)S(1)}, f32[1,2,4,256,128]{4,3,2,1,0:T(8,128)}, u32[]{:S(2)}) copy-start(f32[1,2,4,256,128]{4,3,2,1,0:T(8,128)} %param.16) | copy-start | bytes 3145732
  1.9 1.0 copy-start.2
  2.9 0.9 copy-start.15
  3.9 0.9 copy-start.16
  4.8 0.9 copy-start.17
  5.7 0.9 copy-start.18
  11.4 28.9 %all-to-all-start = ((f32[64,32,128]{2,1,0:T(8,128)}), f32[64,32,128]{2,1,0:T(8,128)S(1)}, u32[]{:S(2)}, u32[]{:S(2)}) async-start(f32[64,32,128]{2,1,0:T(8,128)} %bitcast.1), calls=%async_computation | async-start | bytes 2097152 | tf_op jit(solution)/shard_map/all_to_all | solution.py:290
  22.4 17.8 %copy-start.19 = (f32[1,2,4,128]{3,2,1,0:T(4,128)S(1)}, f32[1,2,4,128]{3,2,1,0:T(4,128)}, u32[]{:S(2)}) copy-start(f32[1,2,4,128]{3,2,1,0:T(4,128)} %param.19) | copy-start | bytes 12292
  41.2 14.7 %copy-start.1 = (f32[1,2,4,256,128]{4,3,2,1,0:T(8,128)S(1)}, f32[1,2,4,256,128]{4,3,2,1,0:T(8,128)}, u32[]{:S(2)}) copy-start(f32[1,2,4,256,128]{4,3,2,1,0:T(8,128)} %param.16) | copy-start | bytes 3145732
  41.2 14.7 %all-to-all-start.2 = ((f32[64,8,128]{2,1,0:T(8,128)}), f32[64,8,128]{2,1,0:T(8,128)S(1)}, u32[]{:S(2)}, u32[]{:S(2)}) async-start(f32[64,8,128]{2,1,0:T(8,128)} %get-tuple-element.6), calls=%async_computation.2 | async-start | bytes 524288 | tf_op jit(solution)/shard_map/all_to_all | solution.py:308
  47.1 8.7 %copy-start.10 = (bf16[256,256]{1,0:T(8,128)(2,1)S(1)}, bf16[256,256]{1,0:T(8,128)(2,1)}, u32[]{:S(2)}) copy-start(bf16[256,256]{1,0:T(8,128)(2,1)} %constant.104.clone.refs_5_.refs_7_) | copy-start | bytes 393220
  55.8 1.0 copy-start.5
  56.8 0.9 copy-start.7
  57.8 0.9 copy-start.11
  58.7 5.9 %copy-start.4 = (f32[2,256,4,128]{3,2,1,0:T(4,128)S(1)}, f32[2,256,4,128]{3,2,1,0:T(4,128)}, u32[]{:S(2)}) copy-start(f32[2,256,4,128]{3,2,1,0:T(4,128)} %param.18) | copy-start | bytes 3145732
  58.7 5.9 %copy-start.13 = (bf16[512,256]{1,0:T(8,128)(2,1)S(1)}, bf16[512,256]{1,0:T(8,128)(2,1)}, u32[]{:S(2)}) copy-start(bf16[512,256]{1,0:T(8,128)(2,1)} %constant.100.clone.refs_3_) | copy-start | bytes 786436
  58.7 5.9 %copy-start.14 = (bf16[512,256]{1,0:T(8,128)(2,1)S(1)}, bf16[512,256]{1,0:T(8,128)(2,1)}, u32[]{:S(2)}) copy-start(bf16[512,256]{1,0:T(8,128)(2,1)} %constant.99.clone.refs_2_) | copy-start | bytes 786436
  61.9 14.8 %collective-permute-start = (f32[4,256,128]{2,1,0:T(8,128)S(1)}, f32[4,256,128]{2,1,0:T(8,128)}, u32[]{:S(2)}, u32[]{:S(2)}) collective-permute-start(f32[4,256,128]{2,1,0:T(8,128)S(1)} %gradient.1), channel_id=1, source_target_pairs={{0,64},{64,0},{1,65},{65,1},{2,66},{66,2},{3,67},{67,3},{4,68},{68... | collective-permute-start | bytes 1572872 | tf_op jit(solution)/shard_map/ppermute | solution.py:343
  70.0 6.7 %copy-start.3 = (f32[4,256,128]{2,1,0:T(8,128)S(1)}, f32[4,256,128]{2,1,0:T(8,128)}, u32[]{:S(2)}) copy-start(f32[4,256,128]{2,1,0:T(8,128)} %refs_1_.1) | copy-start | bytes 1572868
  70.0 23.4 %all-to-all-start.1 = ((f32[64,32,128]{2,1,0:T(8,128)}), f32[64,32,128]{2,1,0:T(8,128)S(1)}, u32[]{:S(2)}, u32[]{:S(2)}) async-start(f32[64,32,128]{2,1,0:T(8,128)} %bitcast.4), calls=%async_computation.1 | async-start | bytes 2097152 | tf_op jit(solution)/shard_map/all_to_all | solution.py:320
  75.0 18.4 %copy-start.6 = (bf16[512,256]{1,0:T(8,128)(2,1)S(1)}, bf16[512,256]{1,0:T(8,128)(2,1)}, u32[]{:S(2)}) copy-start(bf16[512,256]{1,0:T(8,128)(2,1)} %constant.102.clone.refs_3_.refs_5_) | copy-start | bytes 786436
  75.0 18.4 %copy-start.8 = (bf16[512,256]{1,0:T(8,128)(2,1)S(1)}, bf16[512,256]{1,0:T(8,128)(2,1)}, u32[]{:S(2)}) copy-start(bf16[512,256]{1,0:T(8,128)(2,1)} %constant.101.clone.refs_2_.refs_4_) | copy-start | bytes 786436
  75.0 18.4 %copy-start.12 = (bf16[256,256]{1,0:T(8,128)(2,1)S(1)}, bf16[256,256]{1,0:T(8,128)(2,1)}, u32[]{:S(2)}) copy-start(bf16[256,256]{1,0:T(8,128)(2,1)} %constant.103.clone.refs_4_.refs_6_) | copy-start | bytes 393220
  77.8 20.8 %collective-permute-start.2 = (f32[4,256,128]{2,1,0:T(8,128)S(1)}, f32[4,256,128]{2,1,0:T(8,128)S(1)}, u32[]{:S(2)}, u32[]{:S(2)}) collective-permute-start(f32[4,256,128]{2,1,0:T(8,128)S(1)} %multiply_subtract_fusion.refs_2_), channel_id=1, source_target_pairs={{1,0},{2,1},{3,2},{4,3},{5,4},{6,5},{7,6},{8,7},{9,8},{10,9},{11,1... | collective-permute-start | bytes 1572872 | tf_op jit(solution)/shard_map/ppermute | solution.py:348
  81.7 16.9 %collective-permute-start.1 = (f32[4,256,128]{2,1,0:T(8,128)S(1)}, f32[4,256,128]{2,1,0:T(8,128)S(1)}, u32[]{:S(2)}, u32[]{:S(2)}) collective-permute-start(f32[4,256,128]{2,1,0:T(8,128)S(1)} %multiply_subtract_fusion.refs_2_), channel_id=1, source_target_pairs={{0,1},{1,2},{2,3},{3,4},{4,5},{5,6},{6,7},{7,8},{8,9},{9,10},{10,1... | collective-permute-start | bytes 1572872 | tf_op jit(solution)/shard_map/ppermute | solution.py:347
  93.4 1.0 copy-start.9
where the time goes:
time: 106 us; the launch traced here: 105 us
  waiting for transfers between devices  37.9 us (36%)
  starting transfers between devices  29.1 us (27%)
  Pallas kernels  24.9 us (23%)
  local copies, waits for them, and re-layouts  9.86 us (9%)
  other arithmetic  2.42 us (2%)
    all_to_all x1, waiting for transfers between devices, shards(): lax.all_to_all(packed.reshape(slabs, chunk, width_y), 'slab', 0, 0, tiled...  17.8 us
    all_to_all x1, starting transfers between devices, shards(): lax.all_to_all(packed.reshape(slabs, chunk, width_y), 'slab', 0, 0, tiled...  10.8 us
    unnamed x40, local copies, waits for them, and re-layouts  9.86 us
    all_to_all x1, waiting for transfers between devices, shards(): lax.all_to_all(volume.reshape(slabs, chunk, width_y), 'slab', 0, 0, tiled...  9.77 us
    all_to_all x1, waiting for transfers between devices, shards(): gathered = lax.all_to_all(spread, 'slab', 0, 0, tiled=True)  8.64 us
    pallas_call x1, Pallas kernels, shards(): pl.pallas_call(lambda *refs: smooth_kernel(depth, *refs), out_shape=jax.S...  6.51 us
    pallas_call x1, Pallas kernels, shards(): pl.pallas_call(lambda *refs: depth_kernel(depth, block, *refs), out_shape...  5.38 us
    all_to_all x1, starting transfers between devices, shards(): lax.all_to_all(volume.reshape(slabs, chunk, width_y), 'slab', 0, 0, tiled...  4.96 us
  transfers between devices with their start and end apart: 6, of which 4 were waited for; matrix products, arithmetic and copies ran while one was open for 2% of the time, Pallas kernels for 9%

commit v1 on v0

v1 whole, which is shorter than its diff:
```python
import math

import jax
import jax.numpy as jnp
import ml_dtypes
import numpy as np
from jax import lax
from jax.experimental import pallas as pl
from jax.experimental.pallas import tpu as pltpu
from jax.sharding import PartitionSpec as P

wave_number = 1.2
step_size = 2.0
diffusion = 0.02
edge_scale = 0.25
f32 = jnp.float32
bf16 = jnp.bfloat16
PASSES = 4


def halves(table):
    high = table.astype(ml_dtypes.bfloat16)
    low = (table - high.astype(np.float64)).astype(ml_dtypes.bfloat16)
    return high, low


def circle(length):
    counter = np.arange(length)
    angle = (counter[:, None] * counter[None, :] % length) * (2.0 * math.pi / length)
    scale = 1.0 / math.sqrt(length)
    return np.cos(angle) * scale, np.sin(angle) * scale


def tall(cosine, sine):
    return halves(np.concatenate([cosine, sine], 0))


def split(value):
    high = value.astype(bf16)
    return high, (value - high.astype(f32)).astype(bf16)


def product(left, right):
    left_high, left_low = left
    right_high, right_low = right
    small = jnp.dot(left_high, right_low, preferred_element_type=f32)
    small += jnp.dot(left_low, right_high, preferred_element_type=f32)
    return jnp.dot(left_high, right_high, preferred_element_type=f32) + small


def mix_rows(table, wide, sign):
    both = product(table, split(wide))
    rows, lanes = wide.shape[0], wide.shape[1] // 2
    cos_re, cos_im = both[:rows, :lanes], both[:rows, lanes:]
    sin_re, sin_im = both[rows:, :lanes], both[rows:, lanes:]
    if sign < 0:
        return cos_re + sin_im, cos_im - sin_re
    return cos_re - sin_im, cos_im + sin_re


def fetch(sources, targets, sems):
    copies = [
        pltpu.make_async_copy(source, target, sems.at[i])
        for i, (source, target) in enumerate(zip(sources, targets, strict=True))
    ]
    for copy in copies:
        copy.start()
    return copies


def forward_kernel(
    local, block, slabs, field, contrast, xh, xl, yh, yl, out, fv, cv, xhv, xlv, yhv, ylv, sems
):
    sources, targets = [], []
    for plane in range(local):
        sources += [field.at[:, plane], contrast.at[plane]]
        targets += [fv.at[plane], cv.at[plane]]
        if plane == 0:
            sources += [yh, yl, xh, xl]
            targets += [yhv, ylv, xhv, xlv]
    copies = fetch(sources, targets, sems)
    for plane in range(local):
        spot = 0 if plane == 0 else 4 + 2 * plane
        for copy in copies[spot : spot + (4 if plane == 0 else 2)]:
            copy.wait()
        value = cv[plane]
        wide = jnp.concatenate([fv[plane, 0] * value, fv[plane, 1] * value], 1)
        wide = product(split(wide), (yhv[...], ylv[...]))
        if plane == 0:
            for copy in copies[4:6]:
                copy.wait()
        parts = mix_rows((xhv[...], xlv[...]), wide, -1.0)
        for part in range(2):
            for row in range(block):
                spot = plane * (2 * block) + part * block + row
                out[pl.ds(spot, slabs, stride=local * 2 * block), :] = parts[part][
                    row * slabs : (row + 1) * slabs
                ]


def detect_kernel(depth, slabs, root_depth, columns, steps, measured, out, spread):
    half = out.shape[0] // 2
    same, cross = steps[0], steps[1]
    same_far, cross_far = steps[2], steps[3]
    run = 16
    groups = depth // run
    totals = [None] * groups
    for inner in range(run):
        for group in range(groups):
            value = columns[pl.ds((group * run + inner) * 2 * half, 2 * half), :]
            if inner > 0:
                value = value + totals[group]
            totals[group] = value * same + pltpu.roll(value, half, 0) * cross
    total = totals[0]
    for group in range(1, groups):
        total = total * same_far + pltpu.roll(total, half, 0) * cross_far + totals[group]
    miss = total * (1.0 / root_depth) - measured[...]
    out[...] = miss
    for slab in range(slabs):
        spread[slab] = miss


def depth_kernel(depth, block, columns, green, zh, zl, out, gv, zhv, zlv, sems):
    copies = fetch([zh, zl, green], [zhv, zlv, gv], sems)
    stride = 2 * block
    for copy in copies[:2]:
        copy.wait()
    table = (zhv[...], zlv[...])
    for row in range(block):
        wide = jnp.concatenate(
            [columns[pl.ds(part * block + row, depth, stride=stride), :] for part in range(2)],
            1,
        )
        deep_real, deep_imag = mix_rows(table, wide, -1.0)
        if row == 0:
            copies[2].wait()
        green_real = gv[pl.ds(row, depth, stride=block), :]
        green_imag = gv[pl.ds(depth * block + row, depth, stride=block), :]
        wide = jnp.concatenate(
            [
                green_real * deep_real - green_imag * deep_imag,
                green_real * deep_imag + green_imag * deep_real,
            ],
            1,
        )
        parts = mix_rows(table, wide, 1.0)
        for part in range(2):
            out[pl.ds(part * block + row, depth, stride=stride), :] = parts[part]


def gradient_kernel(
    block,
    slabs,
    root_depth,
    gathered,
    prop,
    step,
    field,
    contrast,
    xh,
    xl,
    yh,
    yl,
    out,
    fv,
    cv,
    xhv,
    xlv,
    yhv,
    ylv,
    sems,
):
    local = cv.shape[0]
    sources, targets = [xh, xl, yh, yl], [xhv, xlv, yhv, ylv]
    for plane in range(local - 1, -1, -1):
        sources += [field.at[:, plane], contrast.at[plane]]
        targets += [fv.at[plane], cv.at[plane]]
    copies = fetch(sources, targets, sems)
    miss = [
        jnp.concatenate(
            [
                gathered[pl.ds(part * block + row, slabs, stride=2 * block), :]
                for row in range(block)
            ],
            0,
        )
        * (1.0 / root_depth)
        for part in range(2)
    ]
    real, imag = prop[0], prop[1]
    for plane in range(local - 1, -1, -1):
        wide = jnp.concatenate(
            [real * miss[0] + imag * miss[1], real * miss[1] - imag * miss[0]], 1
        )
        if plane == local - 1:
            for copy in copies[:2]:
                copy.wait()
        wide = jnp.concatenate(mix_rows((xhv[...], xlv[...]), wide, 1.0), 1)
        if plane == local - 1:
            for copy in copies[2:4]:
                copy.wait()
        wide = product(split(wide), (yhv[...], ylv[...]))
        lanes = wide.shape[1] // 2
        spot = 4 + 2 * (local - 1 - plane)
        for copy in copies[spot : spot + 2]:
            copy.wait()
        terms = fv[plane, 0] * wide[:, :lanes] + fv[plane, 1] * wide[:, lanes:]
        out[plane] = 0.5 * cv[plane] - step_size * terms
        if plane > 0:
            real, imag = (
                real * step[0] - imag * step[1],
                real * step[1] + imag * step[0],
            )


def field_kernel(
    local,
    block,
    slabs,
    volume,
    incident,
    xh,
    xl,
    yh,
    yl,
    out,
    iv,
    stage,
    xhv,
    xlv,
    yhv,
    ylv,
    sems,
    out_sems,
):
    fetched = fetch([xh, xl, yh, yl, incident], [xhv, xlv, yhv, ylv, iv], sems)
    stride = local * 2 * block
    copies = []
    for plane in range(local):
        wide = jnp.concatenate(
            [
                jnp.concatenate(
                    [
                        volume[
                            pl.ds(
                                plane * (2 * block) + part * block + row, slabs, stride=stride
                            ),
                            :,
                        ]
                        for row in range(block)
                    ],
                    0,
                )
                for part in range(2)
            ],
            1,
        )
        if plane == 0:
            for copy in fetched:
                copy.wait()
        wide = jnp.concatenate(mix_rows((xhv[...], xlv[...]), wide, 1.0), 1)
        wide = product(split(wide), (yhv[...], ylv[...]))
        lanes = wide.shape[1] // 2
        stage[plane, 0] = iv[0, plane].astype(f32) + wide[:, :lanes]
        stage[plane, 1] = iv[1, plane].astype(f32) + wide[:, lanes:]
        copy = pltpu.make_async_copy(stage.at[plane], out.at[:, plane], out_sems.at[plane])
        copy.start()
        copies.append(copy)
    for copy in copies:
        copy.wait()


def smooth_kernel(depth, limits, before, own, after, out, ping, pong, flux, stage, sems):
    local, rows, lanes = own.shape
    total = local + 2 * PASSES
    size = 64
    ping[:PASSES, :rows] = before[...]
    ping[PASSES : PASSES + local, :rows] = own[...]
    ping[PASSES + local :, :rows] = after[...]
    for plane in range(total):
        ping[plane, rows:] = jnp.broadcast_to(ping[plane, rows - 1 : rows], (8, lanes))
    last_lane = lax.broadcasted_iota(jnp.int32, (size, lanes), 1) == lanes - 1
    first_row = lax.broadcasted_iota(jnp.int32, (size, lanes), 0) == 0
    first = limits[0]

    def inside(plane):
        spot = first + plane
        return jnp.where((spot >= 0) & (spot <= depth - 2), 1.0, 0.0).astype(f32)

    def slopes(source, plane, start, gate):
        core = source[plane, start : start + size]
        slope_depth = (source[plane + 1, start : start + size] - core) * gate
        slope_rows = source[plane, start + 1 : start + size + 1] - core
        slope_lanes = jnp.where(last_lane, 0.0, pltpu.roll(core, lanes - 1, 1) - core)
        scale = lax.rsqrt(
            slope_depth * slope_depth
            + slope_rows * slope_rows
            + (slope_lanes * slope_lanes + edge_scale**2)
        )
        return core, slope_depth * scale, slope_rows * scale, slope_lanes * scale

    source, target = ping, pong
    for repeat in range(PASSES):
        final = repeat == PASSES - 1
        low, high = repeat + 1, total - 1 - repeat
        gate = inside(low - 1)
        for start in range(0, rows, size):
            flux[start : start + size] = slopes(source, low - 1, start, gate)[1]

        def body(plane, carry, source=source, target=target, final=final):
            gate = inside(plane)
            above = jnp.zeros((1, lanes), f32)
            for start in range(0, rows, size):
                here = slice(start, start + size)
                core, flux_depth, flux_rows, flux_lanes = slopes(source, plane, start, gate)
                shifted = jnp.where(first_row, above, pltpu.roll(flux_rows, 1, 0))
                above = flux_rows[size - 1 : size]
                spread = (
                    (flux_depth - flux[here])
                    + (flux_rows - shifted)
                    + (flux_lanes - pltpu.roll(flux_lanes, 1, 1))
                )
                flux[here] = flux_depth
                value = core + diffusion * spread
                if final:
                    stage[plane - PASSES, here] = value
                else:
                    target[plane, here] = value
                    if start + size == rows:
                        target[plane, rows:] = jnp.broadcast_to(
                            value[size - 1 : size], (8, lanes)
                        )
            return carry

        if final:
            copies = []
            for plane in range(low, high):
                body(plane, 0)
                spot = plane - PASSES
                copy = pltpu.make_async_copy(stage.at[spot], out.at[spot], sems.at[spot])
                copy.start()
                copies.append(copy)
            for copy in copies:
                copy.wait()
        else:
            lax.fori_loop(low, high, body, 0)
        source, target = target, source


def frequency(index, length):
    shifted = jnp.where(index < length // 2, index, index - length)
    return shifted.astype(f32) * (2.0 * math.pi / length)


def propagator(distance, row_index, width_x, width_y):
    along_x = frequency(row_index, width_x)
    along_y = frequency(jnp.arange(width_y, dtype=jnp.int32), width_y)
    squared = wave_number**2 - along_x[:, None] ** 2 - along_y[None, :] ** 2
    root = jnp.sqrt(jnp.abs(squared))
    moving = squared > 0.0
    amplitude = jnp.where(moving, 1.0, jnp.exp(-root * distance))
    phase = jnp.where(moving, root * distance, 0.0)
    return amplitude * jnp.cos(phase), amplitude * jnp.sin(phase)


def params():
    return pltpu.CompilerParams(vmem_limit_bytes=10 * 2**20)


def shards(incident, field_now, contrast, green_spectrum, detector_data):
    slabs = lax.axis_size("slab")
    place = lax.axis_index("slab")
    local, width_x, width_y = contrast.shape
    depth = local * slabs
    block = width_x // slabs
    root_depth = math.sqrt(depth)
    chunk = local * 2 * block
    lines = slabs * chunk

    order = np.arange(width_x)
    order = block * (order % slabs) + order // slabs
    cos_x, sin_x = circle(width_x)
    cos_y, sin_y = circle(width_y)
    ahead_x = tall(cos_x[order], sin_x[order])
    back_x = tall(cos_x[:, order], sin_x[:, order])
    ahead_z = tall(*circle(depth))
    ahead_y = halves(np.block([[cos_y, -sin_y], [sin_y, cos_y]]))
    back_y = halves(np.block([[cos_y, sin_y], [-sin_y, cos_y]]))
    x_table = pltpu.VMEM((2 * width_x, width_x), bf16)
    y_table = pltpu.VMEM((2 * width_y, 2 * width_y), bf16)
    z_table = pltpu.VMEM((2 * depth, depth), bf16)
    hbm = pl.BlockSpec(memory_space=pltpu.HBM)
    vmem = pl.BlockSpec(memory_space=pltpu.VMEM)
    sem = pltpu.SemaphoreType.DMA
    far = lambda x: pltpu.with_memory_space_constraint(jnp.asarray(x), pltpu.HBM)
    field, contrast, incident = far(field_now[0]), far(contrast), far(incident[0])
    ahead_x, ahead_y, back_x, back_y, ahead_z = (
        [far(half) for half in pair] for pair in (ahead_x, ahead_y, back_x, back_y, ahead_z)
    )
    green = far(green_spectrum.reshape(lines, width_y))

    packed = pl.pallas_call(
        lambda *refs: forward_kernel(local, block, slabs, *refs),
        out_shape=jax.ShapeDtypeStruct((lines, width_y), f32),
        in_specs=[hbm] * 6,
        out_specs=vmem,
        scratch_shapes=[
            pltpu.VMEM((local, 2, width_x, width_y), f32),
            pltpu.VMEM((local, width_x, width_y), f32),
            x_table,
            x_table,
            y_table,
            y_table,
            sem((2 * local + 4,)),
        ],
        compiler_params=params(),
        name="forward",
    )(field, contrast, *ahead_x, *ahead_y)
    columns = lax.all_to_all(packed.reshape(slabs, chunk, width_y), "slab", 0, 0, tiled=True)
    columns = columns.reshape(lines, width_y)

    mine = place * block + jnp.arange(block, dtype=jnp.int32)
    steps = []
    for distance in (1.0, 16.0):
        real, imag = propagator(distance, mine, width_x, width_y)
        steps += [jnp.concatenate([real, real]), jnp.concatenate([-imag, imag])]
    steps = jnp.stack(steps)
    row_index = jnp.arange(width_x, dtype=jnp.int32)
    row_index = block * (row_index % slabs) + row_index // slabs
    nearest = (depth - place * local - (local - 1)).astype(f32)
    prop = jnp.stack(propagator(nearest, row_index, width_x, width_y))
    step = jnp.stack(propagator(1.0, row_index, width_x, width_y))
    columns, prop, step = lax.optimization_barrier((columns, prop, step))

    miss, spread = pl.pallas_call(
        lambda *refs: detect_kernel(depth, slabs, root_depth, *refs),
        out_shape=(
            jax.ShapeDtypeStruct((2 * block, width_y), f32),
            jax.ShapeDtypeStruct((slabs, 2 * block, width_y), f32),
        ),
        compiler_params=params(),
        name="detect",
    )(columns, steps, detector_data.reshape(2 * block, width_y))
    gathered = lax.all_to_all(spread, "slab", 0, 0, tiled=True)

    volume = pl.pallas_call(
        lambda *refs: depth_kernel(depth, block, *refs),
        out_shape=jax.ShapeDtypeStruct((lines, width_y), f32),
        in_specs=[vmem] + [hbm] * 3,
        out_specs=vmem,
        scratch_shapes=[pltpu.VMEM((lines, width_y), f32), z_table, z_table, sem((3,))],
        compiler_params=params(),
        name="depth",
    )(columns, green, *ahead_z)
    gathered, volume = lax.optimization_barrier((gathered, volume))

    tables = [x_table, x_table, y_table, y_table]
    terms = pl.pallas_call(
        lambda *refs: gradient_kernel(block, slabs, root_depth, *refs),
        out_shape=jax.ShapeDtypeStruct((local, width_x, width_y), f32),
        in_specs=[vmem] * 3 + [hbm] * 6,
        out_specs=vmem,
        scratch_shapes=[
            pltpu.VMEM((local, 2, width_x, width_y), f32),
            pltpu.VMEM((local, width_x, width_y), f32),
            *tables,
            sem((2 * local + 4,)),
        ],
        compiler_params=params(),
        name="gradient",
    )(
        gathered.reshape(slabs * 2 * block, width_y),
        prop,
        step,
        field,
        contrast,
        *back_x,
        *back_y,
    )
    volume = lax.all_to_all(volume.reshape(slabs, chunk, width_y), "slab", 0, 0, tiled=True)
    updated = terms + lax.ppermute(terms, "illum", [(0, 1), (1, 0)])

    up = [(i, i + 1) for i in range(slabs - 1)]
    before = lax.ppermute(updated, "slab", up)
    after = lax.ppermute(updated, "slab", [(j, i) for i, j in up])

    field_next = pl.pallas_call(
        lambda *refs: field_kernel(local, block, slabs, *refs),
        out_shape=jax.ShapeDtypeStruct((2, local, width_x, width_y), f32),
        in_specs=[vmem] + [hbm] * 5,
        out_specs=hbm,
        scratch_shapes=[
            pltpu.VMEM((2, local, width_x, width_y), incident.dtype),
            pltpu.VMEM((local, 2, width_x, width_y), f32),
            *tables,
            sem((5,)),
            sem((local,)),
        ],
        compiler_params=params(),
        name="field",
    )(volume.reshape(lines, width_y), incident, *back_x, *back_y)

    limits = (place * local - PASSES).astype(jnp.int32).reshape(1)
    work = pltpu.VMEM((local + 2 * PASSES, width_x + 8, width_y), f32)
    smoothed = pl.pallas_call(
        lambda *refs: smooth_kernel(depth, *refs),
        out_shape=jax.ShapeDtypeStruct((local, width_x, width_y), f32),
        in_specs=[pl.BlockSpec(memory_space=pltpu.SMEM), vmem, vmem, vmem],
        out_specs=hbm,
        scratch_shapes=[
            work,
            work,
            pltpu.VMEM((width_x, width_y), f32),
            pltpu.VMEM((local, width_x, width_y), f32),
            sem((local,)),
        ],
        compiler_params=params(),
        name="smooth",
    )(limits, before, updated, after)
    return (field_next[None], miss.reshape(1, 2, block, width_y), smoothed)


def solution(mesh):
    placed = (
        P("illum", None, "slab", None, None),
        P("illum", None, "slab", None, None),
        P("slab", None, None),
        P(None, None, "slab", None),
        P("illum", None, "slab", None),
    )
    return jax.shard_map(
        shards,
        mesh=mesh,
        in_specs=placed,
        out_specs=(
            P("illum", None, "slab", None, None),
            P("illum", None, "slab", None),
            P("slab", None, None),
        ),
        check_vma=False,
    )
```

time: 106 us -> 101 us (0.953)
  the two profiles are of different devices: /device:TPU:1 before, /device:TPU:32 now
where the time goes in v1:
time: 101 us; the launch traced here: 100 us
  waiting for transfers between devices  41.8 us (41%)
  starting transfers between devices  28.3 us (28%)
  Pallas kernels  28 us (28%)
  other arithmetic  1.36 us (1%)
    ppermute x1, waiting for transfers between devices, shards(): updated = terms + lax.ppermute(terms, 'illum', [(0, 1), (1, 0)])  16.1 us
    all_to_all x1, waiting for transfers between devices, shards(): lax.all_to_all(packed.reshape(slabs, chunk, width_y), 'slab', 0, 0, tiled...  15.7 us
    all_to_all x1, starting transfers between devices, shards(): lax.all_to_all(packed.reshape(slabs, chunk, width_y), 'slab', 0, 0, tiled...  9.47 us
    pallas_call x1, Pallas kernels, shards(): pl.pallas_call(lambda *refs: smooth_kernel(depth, *refs), out_shape=jax.S...  6.62 us
    pallas_call x1, Pallas kernels, shards(): pl.pallas_call(lambda *refs: forward_kernel(local, block, slabs, *refs),...  6.1 us
    ppermute x1, waiting for transfers between devices, shards(): before = lax.ppermute(updated, 'slab', up)  5.87 us
    all_to_all x1, starting transfers between devices, shards(): lax.all_to_all(volume.reshape(slabs, chunk, width_y), 'slab', 0, 0, tiled...  5.7 us
    all_to_all x1, starting transfers between devices, shards(): gathered = lax.all_to_all(spread, 'slab', 0, 0, tiled=True)  5.69 us
  transfers between devices with their start and end apart: 6, of which 4 were waited for; matrix products, arithmetic and copies ran while one was open for 1% of the time, Pallas kernels for 10%

profile of v1, /device:TPU:32, one launch (start us, length us, event | category | flops | bytes accessed | tf_op | source)
XLA Modules:
  0.0 100.4 jit_solution(17212950727894730064)
XLA Ops:
  0.6 6.1 %forward.1 = f32[2048,128]{1,0:T(8,128)} custom-call(f32[2,4,256,128]{3,2,1,0:T(8,128)} %bitcast.25, f32[4,256,128]{2,1,0:T(8,128)} %refs_4_.3, bf16[512,256]{1,0:T(8,128)(2,1)} %constant.93.clone.refs_2_, bf16[512,256]{1,0:T(8,128)(2,1)} %constant.94.clone.refs_3_, bf16[256,256]{1,0:T(8,128)(2,1)} %constant.95.clone.refs_4_, ...), custom_call_target="tpu_custom_call" | custom-call | tf_op jit(solution)/shard_map/forward/pallas_call | solution.py:402
  6.7 9.5 %all-to-all-start = ((f32[64,32,128]{2,1,0:T(8,128)}), f32[64,32,128]{2,1,0:T(8,128)S(1)}, u32[]{:S(2)}, u32[]{:S(2)}) async-start(f32[64,32,128]{2,1,0:T(8,128)} %bitcast.1), calls=%async_computation | async-start | bytes 2097152 | tf_op jit(solution)/shard_map/all_to_all | solution.py:419
  16.3 0.1 cosine_multiply_fusion.1
  16.5 1.1 %fusion.11 = (f32[1,256,128]{2,1,0:T(8,128)S(1)}, f32[1,256,128]{2,1,0:T(8,128)S(1)}, f32[1,256,128]{2,1,0:T(8,128)S(1)}, f32[1,256,128]{2,1,0:T(8,128)S(1)}) fusion(f32[128]{0:T(128)S(1)} %fusion.38, f32[256]{0:T(256)S(1)} %fusion.35, f32[]{:T(128)S(6)} %convert_element_type.53), kind=kLoop, calls=%fused_computation.15 | loop fusion | flops 458752 | bytes 525828 | tf_op jit(solution)/shard_map/mul | solution.py:363
  17.6 0.0 copy-start
  17.6 15.7 %all-to-all-done = f32[64,32,128]{2,1,0:T(8,128)S(1)} async-done(((f32[64,32,128]{2,1,0:T(8,128)}), f32[64,32,128]{2,1,0:T(8,128)S(1)}, u32[]{:S(2)}, u32[]{:S(2)}) %all-to-all-start) | async-done | bytes 1048608 | tf_op jit(solution)/shard_map/all_to_all | solution.py:419
  33.3 0.0 copy-done
  33.3 0.9 detect.1
  34.2 5.7 %all-to-all-start.1 = ((f32[64,8,128]{2,1,0:T(8,128)}), f32[64,8,128]{2,1,0:T(8,128)S(1)}, u32[]{:S(2)}, u32[]{:S(2)}) async-start(f32[64,8,128]{2,1,0:T(8,128)} %get-tuple-element.11), calls=%async_computation.1 | async-start | bytes 524288 | tf_op jit(solution)/shard_map/all_to_all | solution.py:444
  39.9 4.6 %depth.1 = f32[2048,128]{1,0:T(8,128)} custom-call(f32[2048,128]{1,0:T(8,128)S(1)} %bitcast.21, f32[2048,128]{1,0:T(8,128)} %bitcast.27, bf16[512,256]{1,0:T(8,128)(2,1)} %constant.101.clone.refs_2_, bf16[512,256]{1,0:T(8,128)(2,1)} %constant.102.clone.refs_3_), custom_call_target="tpu_custom_call" | custom-call | tf_op jit(solution)/shard_map/depth/pallas_call | solution.py:446
  44.5 4.1 %all-to-all-done.1 = f32[64,8,128]{2,1,0:T(8,128)S(1)} async-done(((f32[64,8,128]{2,1,0:T(8,128)}), f32[64,8,128]{2,1,0:T(8,128)S(1)}, u32[]{:S(2)}, u32[]{:S(2)}) %all-to-all-start.1) | async-done | bytes 262176 | tf_op jit(solution)/shard_map/all_to_all | solution.py:444
  48.6 4.7 %gradient.1 = f32[4,256,128]{2,1,0:T(8,128)S(1)} custom-call(f32[512,128]{1,0:T(8,128)S(1)} %bitcast.23, f32[2,256,128]{2,1,0:T(8,128)S(1)} %get-tuple-element.15.refs_1_, f32[2,256,128]{2,1,0:T(8,128)S(1)} %get-tuple-element.16.refs_2_, f32[2,4,256,128]{3,2,1,0:T(8,128)} %bitcast.26, f32[4,256,128]{2,1,0:T(8,128)} %refs_4_.3, ...), custom_call_target="tpu_custom_call" | custom-call | tf_op jit(solution)/shard_map/gradient/pallas_call | solution.py:458
  53.3 3.0 %collective-permute-start = (f32[4,256,128]{2,1,0:T(8,128)S(1)}, f32[4,256,128]{2,1,0:T(8,128)S(1)}, u32[]{:S(2)}, u32[]{:S(2)}) collective-permute-start(f32[4,256,128]{2,1,0:T(8,128)S(1)} %gradient.1), channel_id=1, source_target_pairs={{0,64},{64,0},{1,65},{65,1},{2,66},{66,2},{3,67},{67,3},{4,68},{68... | collective-permute-start | bytes 1572872 | tf_op jit(solution)/shard_map/ppermute | solution.py:481
  56.3 5.7 %all-to-all-start.2 = ((f32[64,32,128]{2,1,0:T(8,128)}), f32[64,32,128]{2,1,0:T(8,128)S(1)}, u32[]{:S(2)}, u32[]{:S(2)}) async-start(f32[64,32,128]{2,1,0:T(8,128)} %bitcast.9), calls=%async_computation.2 | async-start | bytes 2097152 | tf_op jit(solution)/shard_map/all_to_all | solution.py:480
  62.0 16.1 %collective-permute-done = f32[4,256,128]{2,1,0:T(8,128)S(1)} collective-permute-done((f32[4,256,128]{2,1,0:T(8,128)S(1)}, f32[4,256,128]{2,1,0:T(8,128)S(1)}, u32[]{:S(2)}, u32[]{:S(2)}) %collective-permute-start) | collective-permute-done | bytes 524320 | tf_op jit(solution)/shard_map/ppermute | solution.py:481
  78.1 0.1 add.77.refs_2_
  78.2 1.9 %collective-permute-start.2 = (f32[4,256,128]{2,1,0:T(8,128)S(1)}, f32[4,256,128]{2,1,0:T(8,128)S(1)}, u32[]{:S(2)}, u32[]{:S(2)}) collective-permute-start(f32[4,256,128]{2,1,0:T(8,128)S(1)} %add.77.refs_2_), channel_id=1, source_target_pairs={{1,0},{2,1},{3,2},{4,3},{5,4},{6,5},{7,6},{8,7},{9,8},{10,9},{11,1... | collective-permute-start | bytes 1572872 | tf_op jit(solution)/shard_map/ppermute | solution.py:485
  80.1 2.6 %collective-permute-start.1 = (f32[4,256,128]{2,1,0:T(8,128)S(1)}, f32[4,256,128]{2,1,0:T(8,128)S(1)}, u32[]{:S(2)}, u32[]{:S(2)}) collective-permute-start(f32[4,256,128]{2,1,0:T(8,128)S(1)} %add.77.refs_2_), channel_id=1, source_target_pairs={{0,1},{1,2},{2,3},{3,4},{4,5},{5,6},{6,7},{7,8},{8,9},{9,10},{10,1... | collective-permute-start | bytes 1572872 | tf_op jit(solution)/shard_map/ppermute | solution.py:484
  82.7 0.0 all-to-all-done.2
  82.7 5.0 %field.1 = f32[2,4,256,128]{3,2,1,0:T(8,128)} custom-call(f32[2048,128]{1,0:T(8,128)S(1)} %bitcast.22, bf16[2,4,256,128]{3,2,1,0:T(8,128)(2,1)} %bitcast.29, bf16[512,256]{1,0:T(8,128)(2,1)} %constant.97.clone.refs_2_.refs_5_, bf16[512,256]{1,0:T(8,128)(2,1)} %constant.98.clone.refs_3_.refs_6_, bf16[256,256]{1,0:T(8,128)(2,1)} %constant.99.clone.refs_4_.refs_7_, ...), custom_call_target="tpu_custom_call" | custom-call | tf_op jit(solution)/shard_map/field/pallas_call | solution.py:487
  87.7 0.0 collective-permute-done.2.refs_3_
  87.7 5.9 %collective-permute-done.1.refs_1_ = f32[4,256,128]{2,1,0:T(8,128)S(1)} collective-permute-done((f32[4,256,128]{2,1,0:T(8,128)S(1)}, f32[4,256,128]{2,1,0:T(8,128)S(1)}, u32[]{:S(2)}, u32[]{:S(2)}) %collective-permute-start.1) | collective-permute-done | bytes 524320 | tf_op jit(solution)/shard_map/ppermute | solution.py:484
  93.6 6.6 %smooth.1 = f32[4,256,128]{2,1,0:T(8,128)} custom-call(s32[1]{0:T(128)} %bitcast.14.refs_0_, f32[4,256,128]{2,1,0:T(8,128)S(1)} %collective-permute-done.1.refs_1_, f32[4,256,128]{2,1,0:T(8,128)S(1)} %add.77.refs_2_, f32[4,256,128]{2,1,0:T(8,128)S(1)} %collective-permute-done.2.refs_3_), custom_call_target="tpu_custom_call" | custom-call | tf_op jit(solution)/shard_map/smooth/pallas_call | solution.py:505
  (7 shorter events, 0.1 us)
Async XLA Ops:
  6.7 26.6 %all-to-all-start = ((f32[64,32,128]{2,1,0:T(8,128)}), f32[64,32,128]{2,1,0:T(8,128)S(1)}, u32[]{:S(2)}, u32[]{:S(2)}) async-start(f32[64,32,128]{2,1,0:T(8,128)} %bitcast.1), calls=%async_computation | async-start | bytes 2097152 | tf_op jit(solution)/shard_map/all_to_all | solution.py:419
  17.6 15.7 %copy-start = (f32[1,2,4,128]{3,2,1,0:T(4,128)S(1)}, f32[1,2,4,128]{3,2,1,0:T(4,128)}, u32[]{:S(2)}) copy-start(f32[1,2,4,128]{3,2,1,0:T(4,128)} %param.19) | copy-start | bytes 12292
  34.2 14.4 %all-to-all-start.1 = ((f32[64,8,128]{2,1,0:T(8,128)}), f32[64,8,128]{2,1,0:T(8,128)S(1)}, u32[]{:S(2)}, u32[]{:S(2)}) async-start(f32[64,8,128]{2,1,0:T(8,128)} %get-tuple-element.11), calls=%async_computation.1 | async-start | bytes 524288 | tf_op jit(solution)/shard_map/all_to_all | solution.py:444
  53.3 24.8 %collective-permute-start = (f32[4,256,128]{2,1,0:T(8,128)S(1)}, f32[4,256,128]{2,1,0:T(8,128)S(1)}, u32[]{:S(2)}, u32[]{:S(2)}) collective-permute-start(f32[4,256,128]{2,1,0:T(8,128)S(1)} %gradient.1), channel_id=1, source_target_pairs={{0,64},{64,0},{1,65},{65,1},{2,66},{66,2},{3,67},{67,3},{4,68},{68... | collective-permute-start | bytes 1572872 | tf_op jit(solution)/shard_map/ppermute | solution.py:481
  56.3 26.4 %all-to-all-start.2 = ((f32[64,32,128]{2,1,0:T(8,128)}), f32[64,32,128]{2,1,0:T(8,128)S(1)}, u32[]{:S(2)}, u32[]{:S(2)}) async-start(f32[64,32,128]{2,1,0:T(8,128)} %bitcast.9), calls=%async_computation.2 | async-start | bytes 2097152 | tf_op jit(solution)/shard_map/all_to_all | solution.py:480
  78.2 9.6 %collective-permute-start.2 = (f32[4,256,128]{2,1,0:T(8,128)S(1)}, f32[4,256,128]{2,1,0:T(8,128)S(1)}, u32[]{:S(2)}, u32[]{:S(2)}) collective-permute-start(f32[4,256,128]{2,1,0:T(8,128)S(1)} %add.77.refs_2_), channel_id=1, source_target_pairs={{1,0},{2,1},{3,2},{4,3},{5,4},{6,5},{7,6},{8,7},{9,8},{10,9},{11,1... | collective-permute-start | bytes 1572872 | tf_op jit(solution)/shard_map/ppermute | solution.py:485
  80.1 13.5 %collective-permute-start.1 = (f32[4,256,128]{2,1,0:T(8,128)S(1)}, f32[4,256,128]{2,1,0:T(8,128)S(1)}, u32[]{:S(2)}, u32[]{:S(2)}) collective-permute-start(f32[4,256,128]{2,1,0:T(8,128)S(1)} %add.77.refs_2_), channel_id=1, source_target_pairs={{0,1},{1,2},{2,3},{3,4},{4,5},{5,6},{6,7},{7,8},{8,9},{9,10},{10,1... | collective-permute-start | bytes 1572872 | tf_op jit(solution)/shard_map/ppermute | solution.py:484

commit v2 on v1

--- a/solution.py
+++ b/solution.py
@@ -69,8 +69,26 @@
 
 
 def forward_kernel(
-    local, block, slabs, field, contrast, xh, xl, yh, yl, out, fv, cv, xhv, xlv, yhv, ylv, sems
+    block,
+    slabs,
+    field,
+    contrast,
+    xh,
+    xl,
+    yh,
+    yl,
+    out,
+    fv,
+    cv,
+    xhv,
+    xlv,
+    yhv,
+    ylv,
+    stage,
+    sems,
+    out_sems,
 ):
+    local = cv.shape[0]
     sources, targets = [], []
     for plane in range(local):
         sources += [field.at[:, plane], contrast.at[plane]]
@@ -79,6 +97,7 @@
             sources += [yh, yl, xh, xl]
             targets += [yhv, ylv, xhv, xlv]
     copies = fetch(sources, targets, sems)
+    sent = []
     for plane in range(local):
         spot = 0 if plane == 0 else 4 + 2 * plane
         for copy in copies[spot : spot + (4 if plane == 0 else 2)]:
@@ -92,10 +111,14 @@
         parts = mix_rows((xhv[...], xlv[...]), wide, -1.0)
         for part in range(2):
             for row in range(block):
-                spot = plane * (2 * block) + part * block + row
-                out[pl.ds(spot, slabs, stride=local * 2 * block), :] = parts[part][
+                stage[plane, :, part * block + row, :] = parts[part][
                     row * slabs : (row + 1) * slabs
                 ]
+        copy = pltpu.make_async_copy(stage.at[plane], out.at[:, plane], out_sems.at[plane])
+        copy.start()
+        sent.append(copy)
+    for copy in sent:
+        copy.wait()
 
 
 def detect_kernel(depth, slabs, root_depth, columns, steps, measured, out, spread):
@@ -148,6 +171,11 @@
             out[pl.ds(part * block + row, depth, stride=stride), :] = parts[part]
 
 
+def bring_kernel(count, *refs):
+    for copy in fetch(refs[:count], refs[count : 2 * count], refs[2 * count]):
+        copy.wait()
+
+
 def gradient_kernel(
     block,
     slabs,
@@ -155,23 +183,19 @@
     gathered,
     prop,
     step,
-    field,
-    contrast,
     xh,
     xl,
     yh,
     yl,
+    field,
+    contrast,
     out,
     fv,
     cv,
-    xhv,
-    xlv,
-    yhv,
-    ylv,
     sems,
 ):
     local = cv.shape[0]
-    sources, targets = [xh, xl, yh, yl], [xhv, xlv, yhv, ylv]
+    sources, targets = [], []
     for plane in range(local - 1, -1, -1):
         sources += [field.at[:, plane], contrast.at[plane]]
         targets += [fv.at[plane], cv.at[plane]]
@@ -192,16 +216,10 @@
         wide = jnp.concatenate(
             [real * miss[0] + imag * miss[1], real * miss[1] - imag * miss[0]], 1
         )
-        if plane == local - 1:
-            for copy in copies[:2]:
-                copy.wait()
-        wide = jnp.concatenate(mix_rows((xhv[...], xlv[...]), wide, 1.0), 1)
-        if plane == local - 1:
-            for copy in copies[2:4]:
-                copy.wait()
-        wide = product(split(wide), (yhv[...], ylv[...]))
+        wide = jnp.concatenate(mix_rows((xh[...], xl[...]), wide, 1.0), 1)
+        wide = product(split(wide), (yh[...], yl[...]))
         lanes = wide.shape[1] // 2
-        spot = 4 + 2 * (local - 1 - plane)
+        spot = 2 * (local - 1 - plane)
         for copy in copies[spot : spot + 2]:
             copy.wait()
         terms = fv[plane, 0] * wide[:, :lanes] + fv[plane, 1] * wide[:, lanes:]
@@ -400,10 +418,10 @@
     green = far(green_spectrum.reshape(lines, width_y))
 
     packed = pl.pallas_call(
-        lambda *refs: forward_kernel(local, block, slabs, *refs),
-        out_shape=jax.ShapeDtypeStruct((lines, width_y), f32),
+        lambda *refs: forward_kernel(block, slabs, *refs),
+        out_shape=jax.ShapeDtypeStruct((slabs, local, 2 * block, width_y), f32),
         in_specs=[hbm] * 6,
-        out_specs=vmem,
+        out_specs=hbm,
         scratch_shapes=[
             pltpu.VMEM((local, 2, width_x, width_y), f32),
             pltpu.VMEM((local, width_x, width_y), f32),
@@ -411,7 +429,9 @@
             x_table,
             y_table,
             y_table,
+            pltpu.VMEM((local, slabs, 2 * block, width_y), f32),
             sem((2 * local + 4,)),
+            sem((local,)),
         ],
         compiler_params=params(),
         name="forward",
@@ -443,6 +463,30 @@
     )(columns, steps, detector_data.reshape(2 * block, width_y))
     gathered = lax.all_to_all(spread, "slab", 0, 0, tiled=True)
 
+    brought = [*back_x, *back_y]
+    near = pl.pallas_call(
+        lambda *refs: bring_kernel(len(brought), *refs),
+        out_shape=[jax.ShapeDtypeStruct(x.shape, x.dtype) for x in brought],
+        in_specs=[hbm] * len(brought),
+        out_specs=[vmem] * len(brought),
+        scratch_shapes=[sem((len(brought),))],
+        compiler_params=params(),
+        name="bring",
+    )(*brought)
+    terms = pl.pallas_call(
+        lambda *refs: gradient_kernel(block, slabs, root_depth, *refs),
+        out_shape=jax.ShapeDtypeStruct((local, width_x, width_y), f32),
+        in_specs=[vmem] * 7 + [hbm] * 2,
+        out_specs=vmem,
+        scratch_shapes=[
+            pltpu.VMEM((local, 2, width_x, width_y), f32),
+            pltpu.VMEM((local, width_x, width_y), f32),
+            sem((2 * local,)),
+        ],
+        compiler_params=params(),
+        name="gradient",
+    )(gathered.reshape(slabs * 2 * block, width_y), prop, step, *near, field, contrast)
+    swapped = lax.ppermute(terms, "illum", [(0, 1), (1, 0)])
     volume = pl.pallas_call(
         lambda *refs: depth_kernel(depth, block, *refs),
         out_shape=jax.ShapeDtypeStruct((lines, width_y), f32),
@@ -452,33 +496,9 @@
         compiler_params=params(),
         name="depth",
     )(columns, green, *ahead_z)
-    gathered, volume = lax.optimization_barrier((gathered, volume))
-
+    volume = lax.all_to_all(volume.reshape(slabs, chunk, width_y), "slab", 0, 0, tiled=True)
     tables = [x_table, x_table, y_table, y_table]
-    terms = pl.pallas_call(
-        lambda *refs: gradient_kernel(block, slabs, root_depth, *refs),
-        out_shape=jax.ShapeDtypeStruct((local, width_x, width_y), f32),
-        in_specs=[vmem] * 3 + [hbm] * 6,
-        out_specs=vmem,
-        scratch_shapes=[
-            pltpu.VMEM((local, 2, width_x, width_y), f32),
-            pltpu.VMEM((local, width_x, width_y), f32),
-            *tables,
-            sem((2 * local + 4,)),
-        ],
-        compiler_params=params(),
-        name="gradient",
-    )(
-        gathered.reshape(slabs * 2 * block, width_y),
-        prop,
-        step,
-        field,
-        contrast,
-        *back_x,
-        *back_y,
-    )
-    volume = lax.all_to_all(volume.reshape(slabs, chunk, width_y), "slab", 0, 0, tiled=True)
-    updated = terms + lax.ppermute(terms, "illum", [(0, 1), (1, 0)])
+    updated = terms + swapped
 
     up = [(i, i + 1) for i in range(slabs - 1)]
     before = lax.ppermute(updated, "slab", up)
@@ -528,6 +548,7 @@
         P(None, None, "slab", None),
         P("illum", None, "slab", None),
     )
+
     return jax.shard_map(
         shards,
         mesh=mesh,

time: 101 us -> 97.4 us (0.964)
  the two profiles are of different devices: /device:TPU:32 before, /device:TPU:1 now
where the time goes in v2:
time: 97.4 us; the launch traced here: 96.9 us
  waiting for transfers between devices  36.1 us (37%)
  starting transfers between devices  30.7 us (32%)
  Pallas kernels  27.8 us (29%)
  other arithmetic  1.36 us (1%)
    all_to_all x1, waiting for transfers between devices, shards(): lax.all_to_all(packed.reshape(slabs, chunk, width_y), 'slab', 0, 0, tiled...  16.7 us
    all_to_all x1, starting transfers between devices, shards(): lax.all_to_all(packed.reshape(slabs, chunk, width_y), 'slab', 0, 0, tiled...  10.9 us
    all_to_all x1, waiting for transfers between devices, shards(): gathered = lax.all_to_all(spread, 'slab', 0, 0, tiled=True)  8.65 us
    all_to_all x1, waiting for transfers between devices, shards(): lax.all_to_all(volume.reshape(slabs, chunk, width_y), 'slab', 0, 0, tiled...  8.23 us
    pallas_call x1, Pallas kernels, shards(): pl.pallas_call(lambda *refs: smooth_kernel(depth, *refs), out_shape=jax.S...  6.63 us
    pallas_call x1, Pallas kernels, shards(): pl.pallas_call(lambda *refs: forward_kernel(block, slabs, *refs), out_sha...  5.68 us
    ppermute x1, starting transfers between devices, shards(): before = lax.ppermute(updated, 'slab', up)  5.48 us
    pallas_call x1, Pallas kernels, shards(): pl.pallas_call(lambda *refs: field_kernel(local, block, slabs, *refs), ou...  5.01 us
  transfers between devices with their start and end apart: 6, of which 4 were waited for; matrix products, arithmetic and copies ran while one was open for 1% of the time, Pallas kernels for 11%

profile of v2, /device:TPU:1, one launch (start us, length us, event | category | flops | bytes accessed | tf_op | source)
XLA Modules:
  0.0 96.9 jit_solution(8888974960174502404)
XLA Ops:
  0.6 5.7 %forward.1 = f32[64,4,8,128]{3,2,1,0:T(8,128)} custom-call(f32[2,4,256,128]{3,2,1,0:T(8,128)} %bitcast.25, f32[4,256,128]{2,1,0:T(8,128)} %refs_8_.1, bf16[512,256]{1,0:T(8,128)(2,1)} %constant.93.clone.refs_2_, bf16[512,256]{1,0:T(8,128)(2,1)} %constant.94.clone.refs_3_, bf16[256,256]{1,0:T(8,128)(2,1)} %constant.95.clone.refs_4_, ...), custom_call_target="tpu_custom_call" | custom-call | tf_op jit(solution)/shard_map/forward/pallas_call | solution.py:420
  6.3 10.9 %all-to-all-start = ((f32[64,32,128]{2,1,0:T(8,128)}), f32[64,32,128]{2,1,0:T(8,128)S(1)}, u32[]{:S(2)}, u32[]{:S(2)}) async-start(f32[64,32,128]{2,1,0:T(8,128)} %bitcast.1), calls=%async_computation | async-start | bytes 2097152 | tf_op jit(solution)/shard_map/all_to_all | solution.py:439
  17.2 0.1 cosine_multiply_fusion.1
  17.4 1.1 %fusion.11 = (f32[1,256,128]{2,1,0:T(8,128)S(1)}, f32[1,256,128]{2,1,0:T(8,128)S(1)}, f32[1,256,128]{2,1,0:T(8,128)S(1)}, f32[1,256,128]{2,1,0:T(8,128)S(1)}) fusion(f32[128]{0:T(128)S(1)} %fusion.38, f32[256]{0:T(256)S(1)} %fusion.35, f32[]{:T(128)S(6)} %convert_element_type.53), kind=kLoop, calls=%fused_computation.15 | loop fusion | flops 458752 | bytes 525828 | tf_op jit(solution)/shard_map/mul | solution.py:381
  18.6 0.0 copy-start
  18.6 16.7 %all-to-all-done = f32[64,32,128]{2,1,0:T(8,128)S(1)} async-done(((f32[64,32,128]{2,1,0:T(8,128)}), f32[64,32,128]{2,1,0:T(8,128)S(1)}, u32[]{:S(2)}, u32[]{:S(2)}) %all-to-all-start) | async-done | bytes 1048608 | tf_op jit(solution)/shard_map/all_to_all | solution.py:439
  35.2 0.0 copy-done
  35.2 0.9 detect.1
  36.1 4.7 %all-to-all-start.2 = ((f32[64,8,128]{2,1,0:T(8,128)}), f32[64,8,128]{2,1,0:T(8,128)S(1)}, u32[]{:S(2)}, u32[]{:S(2)}) async-start(f32[64,8,128]{2,1,0:T(8,128)} %get-tuple-element.14), calls=%async_computation.2 | async-start | bytes 524288 | tf_op jit(solution)/shard_map/all_to_all | solution.py:464
  40.9 1.1 %bring.1 = (bf16[512,256]{1,0:T(8,128)(2,1)S(1)}, bf16[512,256]{1,0:T(8,128)(2,1)S(1)}, bf16[256,256]{1,0:T(8,128)(2,1)S(1)}, bf16[256,256]{1,0:T(8,128)(2,1)S(1)}) custom-call(bf16[512,256]{1,0:T(8,128)(2,1)} %constant.97.clone.refs_2_.refs_0_, bf16[512,256]{1,0:T(8,128)(2,1)} %constant.98.clone.refs_3_.refs_1_, ...), custom_call_target="tpu_custom_call" | custom-call | tf_op jit(solution)/shard_map/bring/pallas_call | solution.py:467
  42.0 8.6 %all-to-all-done.2 = f32[64,8,128]{2,1,0:T(8,128)S(1)} async-done(((f32[64,8,128]{2,1,0:T(8,128)}), f32[64,8,128]{2,1,0:T(8,128)S(1)}, u32[]{:S(2)}, u32[]{:S(2)}) %all-to-all-start.2) | async-done | bytes 262176 | tf_op jit(solution)/shard_map/all_to_all | solution.py:464
  50.7 3.8 %gradient.1 = f32[4,256,128]{2,1,0:T(8,128)S(1)} custom-call(f32[512,128]{1,0:T(8,128)S(1)} %bitcast.23, f32[2,256,128]{2,1,0:T(8,128)S(1)} %get-tuple-element.15.refs_1_, f32[2,256,128]{2,1,0:T(8,128)S(1)} %get-tuple-element.16.refs_2_, bf16[512,256]{1,0:T(8,128)(2,1)S(1)} %get-tuple-element.17.refs_3_, bf16[512,256]{1,0:T(8,128)(2,1)S(1)} %get-tuple-element.18.refs_4_, ...), custom_call_target="tpu_custom_call" | custom-call | tf_op jit(solution)/shard_map/gradient/pallas_call | solution.py:476
  54.5 2.7 %collective-permute-start = (f32[4,256,128]{2,1,0:T(8,128)S(1)}, f32[4,256,128]{2,1,0:T(8,128)S(1)}, u32[]{:S(2)}, u32[]{:S(2)}) collective-permute-start(f32[4,256,128]{2,1,0:T(8,128)S(1)} %gradient.1), channel_id=1, source_target_pairs={{0,64},{64,0},{1,65},{65,1},{2,66},{66,2},{3,67},{67,3},{4,68},{68... | collective-permute-start | bytes 1572872 | tf_op jit(solution)/shard_map/ppermute | solution.py:489
  57.2 4.6 %depth.1 = f32[2048,128]{1,0:T(8,128)} custom-call(f32[2048,128]{1,0:T(8,128)S(1)} %bitcast.21, f32[2048,128]{1,0:T(8,128)} %bitcast.27, bf16[512,256]{1,0:T(8,128)(2,1)} %constant.101.clone.refs_2_, bf16[512,256]{1,0:T(8,128)(2,1)} %constant.102.clone.refs_3_), custom_call_target="tpu_custom_call" | custom-call | tf_op jit(solution)/shard_map/depth/pallas_call | solution.py:490
  61.8 4.8 %all-to-all-start.1 = ((f32[64,32,128]{2,1,0:T(8,128)}), f32[64,32,128]{2,1,0:T(8,128)S(1)}, u32[]{:S(2)}, u32[]{:S(2)}) async-start(f32[64,32,128]{2,1,0:T(8,128)} %bitcast.4), calls=%async_computation.1 | async-start | bytes 2097152 | tf_op jit(solution)/shard_map/all_to_all | solution.py:499
  66.6 2.5 %collective-permute-done = f32[4,256,128]{2,1,0:T(8,128)S(1)} collective-permute-done((f32[4,256,128]{2,1,0:T(8,128)S(1)}, f32[4,256,128]{2,1,0:T(8,128)S(1)}, u32[]{:S(2)}, u32[]{:S(2)}) %collective-permute-start) | collective-permute-done | bytes 524320 | tf_op jit(solution)/shard_map/ppermute | solution.py:489
  69.1 0.1 add.77.refs_2_
  69.2 5.5 %collective-permute-start.1 = (f32[4,256,128]{2,1,0:T(8,128)S(1)}, f32[4,256,128]{2,1,0:T(8,128)S(1)}, u32[]{:S(2)}, u32[]{:S(2)}) collective-permute-start(f32[4,256,128]{2,1,0:T(8,128)S(1)} %add.77.refs_2_), channel_id=1, source_target_pairs={{0,1},{1,2},{2,3},{3,4},{4,5},{5,6},{6,7},{7,8},{8,9},{9,10},{10,1... | collective-permute-start | bytes 1572872 | tf_op jit(solution)/shard_map/ppermute | solution.py:504
  74.7 2.1 %collective-permute-start.2 = (f32[4,256,128]{2,1,0:T(8,128)S(1)}, f32[4,256,128]{2,1,0:T(8,128)S(1)}, u32[]{:S(2)}, u32[]{:S(2)}) collective-permute-start(f32[4,256,128]{2,1,0:T(8,128)S(1)} %add.77.refs_2_), channel_id=1, source_target_pairs={{1,0},{2,1},{3,2},{4,3},{5,4},{6,5},{7,6},{8,7},{9,8},{10,9},{11,1... | collective-permute-start | bytes 1572872 | tf_op jit(solution)/shard_map/ppermute | solution.py:505
  76.8 8.2 %all-to-all-done.1 = f32[64,32,128]{2,1,0:T(8,128)S(1)} async-done(((f32[64,32,128]{2,1,0:T(8,128)}), f32[64,32,128]{2,1,0:T(8,128)S(1)}, u32[]{:S(2)}, u32[]{:S(2)}) %all-to-all-start.1) | async-done | bytes 1048608 | tf_op jit(solution)/shard_map/all_to_all | solution.py:499
  85.0 5.0 %field.1 = f32[2,4,256,128]{3,2,1,0:T(8,128)} custom-call(f32[2048,128]{1,0:T(8,128)S(1)} %bitcast.22, bf16[2,4,256,128]{3,2,1,0:T(8,128)(2,1)} %bitcast.29, bf16[512,256]{1,0:T(8,128)(2,1)} %constant.97.clone.refs_2_.refs_0_, bf16[512,256]{1,0:T(8,128)(2,1)} %constant.98.clone.refs_3_.refs_1_, bf16[256,256]{1,0:T(8,128)(2,1)} %constant.99.clone.refs_4_.refs_2_, ...), custom_call_target="tpu_custom_call" | custom-call | tf_op jit(solution)/shard_map/field/pallas_call | solution.py:507
  90.1 0.0 collective-permute-done.1.refs_1_
  90.1 0.0 collective-permute-done.2.refs_3_
  90.1 6.6 %smooth.1 = f32[4,256,128]{2,1,0:T(8,128)} custom-call(s32[1]{0:T(128)} %bitcast.14.refs_0_, f32[4,256,128]{2,1,0:T(8,128)S(1)} %collective-permute-done.1.refs_1_, f32[4,256,128]{2,1,0:T(8,128)S(1)} %add.77.refs_2_, f32[4,256,128]{2,1,0:T(8,128)S(1)} %collective-permute-done.2.refs_3_), custom_call_target="tpu_custom_call" | custom-call | tf_op jit(solution)/shard_map/smooth/pallas_call | solution.py:525
  (7 shorter events, 0.1 us)
Async XLA Ops:
  6.3 28.9 %all-to-all-start = ((f32[64,32,128]{2,1,0:T(8,128)}), f32[64,32,128]{2,1,0:T(8,128)S(1)}, u32[]{:S(2)}, u32[]{:S(2)}) async-start(f32[64,32,128]{2,1,0:T(8,128)} %bitcast.1), calls=%async_computation | async-start | bytes 2097152 | tf_op jit(solution)/shard_map/all_to_all | solution.py:439
  18.6 16.7 %copy-start = (f32[1,2,4,128]{3,2,1,0:T(4,128)S(1)}, f32[1,2,4,128]{3,2,1,0:T(4,128)}, u32[]{:S(2)}) copy-start(f32[1,2,4,128]{3,2,1,0:T(4,128)} %param.19) | copy-start | bytes 12292
  36.1 14.5 %all-to-all-start.2 = ((f32[64,8,128]{2,1,0:T(8,128)}), f32[64,8,128]{2,1,0:T(8,128)S(1)}, u32[]{:S(2)}, u32[]{:S(2)}) async-start(f32[64,8,128]{2,1,0:T(8,128)} %get-tuple-element.14), calls=%async_computation.2 | async-start | bytes 524288 | tf_op jit(solution)/shard_map/all_to_all | solution.py:464
  54.5 14.7 %collective-permute-start = (f32[4,256,128]{2,1,0:T(8,128)S(1)}, f32[4,256,128]{2,1,0:T(8,128)S(1)}, u32[]{:S(2)}, u32[]{:S(2)}) collective-permute-start(f32[4,256,128]{2,1,0:T(8,128)S(1)} %gradient.1), channel_id=1, source_target_pairs={{0,64},{64,0},{1,65},{65,1},{2,66},{66,2},{3,67},{67,3},{4,68},{68... | collective-permute-start | bytes 1572872 | tf_op jit(solution)/shard_map/ppermute | solution.py:489
  61.8 23.3 %all-to-all-start.1 = ((f32[64,32,128]{2,1,0:T(8,128)}), f32[64,32,128]{2,1,0:T(8,128)S(1)}, u32[]{:S(2)}, u32[]{:S(2)}) async-start(f32[64,32,128]{2,1,0:T(8,128)} %bitcast.4), calls=%async_computation.1 | async-start | bytes 2097152 | tf_op jit(solution)/shard_map/all_to_all | solution.py:499
  69.2 20.9 %collective-permute-start.1 = (f32[4,256,128]{2,1,0:T(8,128)S(1)}, f32[4,256,128]{2,1,0:T(8,128)S(1)}, u32[]{:S(2)}, u32[]{:S(2)}) collective-permute-start(f32[4,256,128]{2,1,0:T(8,128)S(1)} %add.77.refs_2_), channel_id=1, source_target_pairs={{0,1},{1,2},{2,3},{3,4},{4,5},{5,6},{6,7},{7,8},{8,9},{9,10},{10,1... | collective-permute-start | bytes 1572872 | tf_op jit(solution)/shard_map/ppermute | solution.py:504
  74.7 15.4 %collective-permute-start.2 = (f32[4,256,128]{2,1,0:T(8,128)S(1)}, f32[4,256,128]{2,1,0:T(8,128)S(1)}, u32[]{:S(2)}, u32[]{:S(2)}) collective-permute-start(f32[4,256,128]{2,1,0:T(8,128)S(1)} %add.77.refs_2_), channel_id=1, source_target_pairs={{1,0},{2,1},{3,2},{4,3},{5,4},{6,5},{7,6},{8,7},{9,8},{10,9},{11,1... | collective-permute-start | bytes 1572872 | tf_op jit(solution)/shard_map/ppermute | solution.py:505

commit v3 on v2

--- a/solution.py
+++ b/solution.py
@@ -31,8 +31,15 @@
     return np.cos(angle) * scale, np.sin(angle) * scale
 
 
-def tall(cosine, sine):
-    return halves(np.concatenate([cosine, sine], 0))
+def half_tables(length, block, slabs):
+    cosine, sine = circle(length)
+    half = length // 2
+    slot = np.arange(half)
+    slot = block * (slot % (slabs // 2)) + slot // (slabs // 2)
+    sine = sine[slot]
+    sine[0] = cosine[half]
+    ahead = np.concatenate([cosine[slot], sine], 0)
+    return halves(ahead), halves(ahead.T)
 
 
 def split(value):
@@ -48,14 +55,49 @@
     return jnp.dot(left_high, right_high, preferred_element_type=f32) + small
 
 
-def mix_rows(table, wide, sign):
-    both = product(table, split(wide))
-    rows, lanes = wide.shape[0], wide.shape[1] // 2
-    cos_re, cos_im = both[:rows, :lanes], both[:rows, lanes:]
-    sin_re, sin_im = both[rows:, :lanes], both[rows:, lanes:]
-    if sign < 0:
-        return cos_re + sin_im, cos_im - sin_re
-    return cos_re - sin_im, cos_im + sin_re
+def flip_rows(value):
+    index = 7 - lax.broadcasted_iota(jnp.int32, (8, value.shape[1]), 0)
+    tiles = [value[start : start + 8] for start in range(0, value.shape[0], 8)]
+    return jnp.concatenate([jnp.take_along_axis(x, index, axis=0) for x in tiles[::-1]], 0)
+
+
+def align(natural):
+    head = pltpu.roll(flip_rows(natural[0]), 1, 0)
+    return [head] + [flip_rows(x) for x in natural[:0:-1]]
+
+
+def unalign(mirrored):
+    head = flip_rows(pltpu.roll(mirrored[0], mirrored[0].shape[0] - 1, 0))
+    return [head] + [flip_rows(x) for x in mirrored[:0:-1]]
+
+
+def first_row(special, value):
+    row = lax.broadcasted_iota(jnp.int32, (8, value.shape[1]), 0)
+    return jnp.concatenate([jnp.where(row == 0, special[:8], value[:8]), value[8:]], 0)
+
+
+def unfold(both):
+    half, lanes = both.shape[0] // 2, both.shape[1] // 2
+    cos_re, cos_im = both[:half, :lanes], both[:half, lanes:]
+    sin_re, sin_im = both[half:, :lanes], both[half:, lanes:]
+    lower = (first_row(cos_re, cos_re + sin_im), first_row(cos_im, cos_im - sin_re))
+    upper = (first_row(sin_re, cos_re - sin_im), first_row(sin_im, cos_im + sin_re))
+    return lower, upper
+
+
+def fold(lower, upper):
+    even = [first_row(a, a + b) for a, b in zip(lower, upper, strict=True)]
+    odd = [first_row(upper[0], upper[1] - lower[1]), first_row(upper[1], lower[0] - upper[0])]
+    return jnp.concatenate([jnp.concatenate(even, 1), jnp.concatenate(odd, 1)], 0)
+
+
+def gather_rows(ref, starts, slabs, stride):
+    lower, upper = [], []
+    for part in starts:
+        blocks = [ref[pl.ds(start, slabs, stride=stride), :] for start in part]
+        lower.append(jnp.concatenate([x[: slabs // 2] for x in blocks], 0))
+        upper.append(jnp.concatenate(align([x[slabs // 2 :] for x in blocks]), 0))
+    return fold(lower, upper)
 
 
 def fetch(sources, targets, sems):
@@ -108,12 +150,14 @@
         if plane == 0:
             for copy in copies[4:6]:
                 copy.wait()
-        parts = mix_rows((xhv[...], xlv[...]), wide, -1.0)
+        lower, upper = unfold(product((xhv[...], xlv[...]), split(wide)))
+        size = slabs // 2
         for part in range(2):
+            mirrored = unalign([upper[part][row * size : (row + 1) * size] for row in range(block)])
             for row in range(block):
-                stage[plane, :, part * block + row, :] = parts[part][
-                    row * slabs : (row + 1) * slabs
-                ]
+                spot = part * block + row
+                stage[plane, :size, spot, :] = lower[part][row * size : (row + 1) * size]
+                stage[plane, size:, spot, :] = mirrored[row]
         copy = pltpu.make_async_copy(stage.at[plane], out.at[:, plane], out_sems.at[plane])
         copy.start()
         sent.append(copy)
@@ -143,32 +187,41 @@
         spread[slab] = miss
 
 
-def depth_kernel(depth, block, columns, green, zh, zl, out, gv, zhv, zlv, sems):
-    copies = fetch([zh, zl, green], [zhv, zlv, gv], sems)
+def depth_kernel(depth, block, columns, green, ah, al, bh, bl, out, gv, *rest):
+    tables, sems = rest[:4], rest[4]
+    copies = fetch([ah, al, green, bh, bl], [*tables[:2], gv, *tables[2:]], sems)
     stride = 2 * block
+    half = depth // 2
     for copy in copies[:2]:
         copy.wait()
-    table = (zhv[...], zlv[...])
     for row in range(block):
         wide = jnp.concatenate(
             [columns[pl.ds(part * block + row, depth, stride=stride), :] for part in range(2)],
             1,
         )
-        deep_real, deep_imag = mix_rows(table, wide, -1.0)
+        lower, upper = unfold(product((tables[0][...], tables[1][...]), split(wide)))
         if row == 0:
-            copies[2].wait()
-        green_real = gv[pl.ds(row, depth, stride=block), :]
-        green_imag = gv[pl.ds(depth * block + row, depth, stride=block), :]
-        wide = jnp.concatenate(
-            [
-                green_real * deep_real - green_imag * deep_imag,
-                green_real * deep_imag + green_imag * deep_real,
-            ],
-            1,
-        )
-        parts = mix_rows(table, wide, 1.0)
+            for copy in copies[2:]:
+                copy.wait()
+        pieces = []
+        for side, deep in enumerate((lower, upper)):
+            green_part = [
+                gv[pl.ds((part * depth + side * half) * block + row, half, stride=block), :]
+                for part in range(2)
+            ]
+            if side == 1:
+                green_part = [align([x])[0] for x in green_part]
+            pieces.append(
+                (
+                    green_part[0] * deep[0] - green_part[1] * deep[1],
+                    green_part[0] * deep[1] + green_part[1] * deep[0],
+                )
+            )
+        wide = product((tables[2][...], tables[3][...]), split(fold(*pieces)))
         for part in range(2):
-            out[pl.ds(part * block + row, depth, stride=stride), :] = parts[part]
+            out[pl.ds(part * block + row, depth, stride=stride), :] = wide[
+                :, part * wide.shape[1] // 2 : (part + 1) * wide.shape[1] // 2
+            ]
 
 
 def bring_kernel(count, *refs):
@@ -200,25 +253,17 @@
         sources += [field.at[:, plane], contrast.at[plane]]
         targets += [fv.at[plane], cv.at[plane]]
     copies = fetch(sources, targets, sems)
-    miss = [
-        jnp.concatenate(
-            [
-                gathered[pl.ds(part * block + row, slabs, stride=2 * block), :]
-                for row in range(block)
-            ],
-            0,
-        )
-        * (1.0 / root_depth)
-        for part in range(2)
-    ]
+    starts = [[part * block + row for row in range(block)] for part in range(2)]
+    miss = gather_rows(gathered, starts, slabs, 2 * block) * (1.0 / root_depth)
+    lanes = miss.shape[1] // 2
+    miss = (miss[:, :lanes], miss[:, lanes:])
     real, imag = prop[0], prop[1]
     for plane in range(local - 1, -1, -1):
         wide = jnp.concatenate(
             [real * miss[0] + imag * miss[1], real * miss[1] - imag * miss[0]], 1
         )
-        wide = jnp.concatenate(mix_rows((xh[...], xl[...]), wide, 1.0), 1)
+        wide = product((xh[...], xl[...]), split(wide))
         wide = product(split(wide), (yh[...], yl[...]))
-        lanes = wide.shape[1] // 2
         spot = 2 * (local - 1 - plane)
         for copy in copies[spot : spot + 2]:
             copy.wait()
@@ -255,28 +300,15 @@
     stride = local * 2 * block
     copies = []
     for plane in range(local):
-        wide = jnp.concatenate(
-            [
-                jnp.concatenate(
-                    [
-                        volume[
-                            pl.ds(
-                                plane * (2 * block) + part * block + row, slabs, stride=stride
-                            ),
-                            :,
-                        ]
-                        for row in range(block)
-                    ],
-                    0,
-                )
-                for part in range(2)
-            ],
-            1,
-        )
+        starts = [
+            [plane * (2 * block) + part * block + row for row in range(block)]
+            for part in range(2)
+        ]
+        wide = gather_rows(volume, starts, slabs, stride)
         if plane == 0:
             for copy in fetched:
                 copy.wait()
-        wide = jnp.concatenate(mix_rows((xhv[...], xlv[...]), wide, 1.0), 1)
+        wide = product((xhv[...], xlv[...]), split(wide))
         wide = product(split(wide), (yhv[...], ylv[...]))
         lanes = wide.shape[1] // 2
         stage[plane, 0] = iv[0, plane].astype(f32) + wide[:, :lanes]
@@ -395,25 +427,22 @@
     chunk = local * 2 * block
     lines = slabs * chunk
 
-    order = np.arange(width_x)
-    order = block * (order % slabs) + order // slabs
-    cos_x, sin_x = circle(width_x)
+    ahead_x, back_x = half_tables(width_x, block, slabs)
+    ahead_z, back_z = half_tables(depth, 1, depth)
     cos_y, sin_y = circle(width_y)
-    ahead_x = tall(cos_x[order], sin_x[order])
-    back_x = tall(cos_x[:, order], sin_x[:, order])
-    ahead_z = tall(*circle(depth))
     ahead_y = halves(np.block([[cos_y, -sin_y], [sin_y, cos_y]]))
     back_y = halves(np.block([[cos_y, sin_y], [-sin_y, cos_y]]))
-    x_table = pltpu.VMEM((2 * width_x, width_x), bf16)
+    x_table = pltpu.VMEM((width_x, width_x), bf16)
     y_table = pltpu.VMEM((2 * width_y, 2 * width_y), bf16)
-    z_table = pltpu.VMEM((2 * depth, depth), bf16)
+    z_table = pltpu.VMEM((depth, depth), bf16)
     hbm = pl.BlockSpec(memory_space=pltpu.HBM)
     vmem = pl.BlockSpec(memory_space=pltpu.VMEM)
     sem = pltpu.SemaphoreType.DMA
     far = lambda x: pltpu.with_memory_space_constraint(jnp.asarray(x), pltpu.HBM)
     field, contrast, incident = far(field_now[0]), far(contrast), far(incident[0])
-    ahead_x, ahead_y, back_x, back_y, ahead_z = (
-        [far(half) for half in pair] for pair in (ahead_x, ahead_y, back_x, back_y, ahead_z)
+    ahead_x, ahead_y, back_x, back_y, ahead_z, back_z = (
+        [far(half) for half in pair]
+        for pair in (ahead_x, ahead_y, back_x, back_y, ahead_z, back_z)
     )
     green = far(green_spectrum.reshape(lines, width_y))
 
@@ -445,8 +474,10 @@
         real, imag = propagator(distance, mine, width_x, width_y)
         steps += [jnp.concatenate([real, real]), jnp.concatenate([-imag, imag])]
     steps = jnp.stack(steps)
-    row_index = jnp.arange(width_x, dtype=jnp.int32)
-    row_index = block * (row_index % slabs) + row_index // slabs
+    slot = jnp.arange(width_x, dtype=jnp.int32)
+    row_index = slot % (width_x // 2)
+    row_index = block * (row_index % (slabs // 2)) + row_index // (slabs // 2)
+    row_index = jnp.where(slot == width_x // 2, width_x // 2, row_index)
     nearest = (depth - place * local - (local - 1)).astype(f32)
     prop = jnp.stack(propagator(nearest, row_index, width_x, width_y))
     step = jnp.stack(propagator(1.0, row_index, width_x, width_y))
@@ -490,12 +521,12 @@
     volume = pl.pallas_call(
         lambda *refs: depth_kernel(depth, block, *refs),
         out_shape=jax.ShapeDtypeStruct((lines, width_y), f32),
-        in_specs=[vmem] + [hbm] * 3,
+        in_specs=[vmem] + [hbm] * 5,
         out_specs=vmem,
-        scratch_shapes=[pltpu.VMEM((lines, width_y), f32), z_table, z_table, sem((3,))],
+        scratch_shapes=[pltpu.VMEM((lines, width_y), f32)] + [z_table] * 4 + [sem((5,))],
         compiler_params=params(),
         name="depth",
-    )(columns, green, *ahead_z)
+    )(columns, green, *ahead_z, *back_z)
     volume = lax.all_to_all(volume.reshape(slabs, chunk, width_y), "slab", 0, 0, tiled=True)
     tables = [x_table, x_table, y_table, y_table]
     updated = terms + swapped

time: 97.4 us -> 95.7 us (0.983)
  starting transfers between devices: 30.7 us -> 34.7 us
  Pallas kernels: 27.8 us -> 24.3 us
  waiting for transfers between devices: 36.1 us -> 33.9 us
    all_to_all x1, waiting for transfers between devices: 8.23 us -> 2.95 us  [shards(): lax.all_to_all(volume.reshape(slabs, chunk, width_y), 'slab', 0, 0, tiled...]
    ppermute x1, starting transfers between devices: 5.48 us -> 9.46 us  [shards(): before = lax.ppermute(updated, 'slab', up)]
    ppermute x1, waiting for transfers between devices: 0.01 us -> 1.84 us  [shards(): after = lax.ppermute(updated, 'slab', [(j, i) for i, j in up])]
    pallas_call x1, Pallas kernels: 5.01 us -> 3.58 us  [shards(): pl.pallas_call(lambda *refs: field_kernel(local, block, slabs, *refs), ou...]
    ppermute x1, waiting for transfers between devices: 2.54 us -> 3.84 us  [shards(): swapped = lax.ppermute(terms, 'illum', [(0, 1), (1, 0)])]
  transfers between devices with their start and end apart: 6 -> 6, of which waited for: 4 -> 5; matrix products, arithmetic and copies ran while one was open for 1% -> 1% of each run, Pallas kernels for 11% -> 9%
where the time goes in v3:
time: 95.7 us; the launch traced here: 95.2 us
  starting transfers between devices  34.7 us (36%)
  waiting for transfers between devices  33.9 us (35%)
  Pallas kernels  24.3 us (25%)
  other arithmetic  1.36 us (1%)
  between operations  0.96 us (1%)
    all_to_all x1, waiting for transfers between devices, shards(): lax.all_to_all(packed.reshape(slabs, chunk, width_y), 'slab', 0, 0, tiled...  16.6 us
    all_to_all x1, starting transfers between devices, shards(): lax.all_to_all(packed.reshape(slabs, chunk, width_y), 'slab', 0, 0, tiled...  10.8 us
    ppermute x1, starting transfers between devices, shards(): before = lax.ppermute(updated, 'slab', up)  9.46 us
    all_to_all x1, waiting for transfers between devices, shards(): gathered = lax.all_to_all(spread, 'slab', 0, 0, tiled=True)  8.65 us
    pallas_call x1, Pallas kernels, shards(): pl.pallas_call(lambda *refs: smooth_kernel(depth, *refs), out_shape=jax.S...  6.62 us
    pallas_call x1, Pallas kernels, shards(): pl.pallas_call(lambda *refs: forward_kernel(block, slabs, *refs), out_sha...  5.19 us
    all_to_all x1, starting transfers between devices, shards(): lax.all_to_all(volume.reshape(slabs, chunk, width_y), 'slab', 0, 0, tiled...  4.84 us
    all_to_all x1, starting transfers between devices, shards(): gathered = lax.all_to_all(spread, 'slab', 0, 0, tiled=True)  4.73 us
  transfers between devices with their start and end apart: 6, of which 5 were waited for; matrix products, arithmetic and copies ran while one was open for 1% of the time, Pallas kernels for 9%

profile of v3, /device:TPU:1, one launch (start us, length us, event | category | flops | bytes accessed | tf_op | source)
XLA Modules:
  0.0 95.2 jit_solution(3873057263748834476)
XLA Ops:
  0.6 5.2 %forward.1 = f32[64,4,8,128]{3,2,1,0:T(8,128)} custom-call(f32[2,4,256,128]{3,2,1,0:T(8,128)} %bitcast.25, f32[4,256,128]{2,1,0:T(8,128)} %refs_8_.1, bf16[256,256]{1,0:T(8,128)(2,1)} %constant.106.clone.refs_2_, bf16[256,256]{1,0:T(8,128)(2,1)} %constant.107.clone.refs_3_, bf16[256,256]{1,0:T(8,128)(2,1)} %constant.108.clone.refs_4_, ...), custom_call_target="tpu_custom_call" | custom-call | tf_op jit(solution)/shard_map/forward/pallas_call | solution.py:449
  5.8 10.8 %all-to-all-start = ((f32[64,32,128]{2,1,0:T(8,128)}), f32[64,32,128]{2,1,0:T(8,128)S(1)}, u32[]{:S(2)}, u32[]{:S(2)}) async-start(f32[64,32,128]{2,1,0:T(8,128)} %bitcast.1), calls=%async_computation | async-start | bytes 2097152 | tf_op jit(solution)/shard_map/all_to_all | solution.py:468
  16.7 0.1 cosine_multiply_fusion.1
  16.9 1.1 %fusion.11 = (f32[1,256,128]{2,1,0:T(8,128)S(1)}, f32[1,256,128]{2,1,0:T(8,128)S(1)}, f32[1,256,128]{2,1,0:T(8,128)S(1)}, f32[1,256,128]{2,1,0:T(8,128)S(1)}) fusion(f32[128]{0:T(128)S(1)} %fusion.36, f32[256]{0:T(256)S(1)} %fusion.33, f32[]{:T(128)S(6)} %convert_element_type.53), kind=kLoop, calls=%fused_computation.15 | loop fusion | flops 458752 | bytes 525828 | tf_op jit(solution)/shard_map/mul | solution.py:413
  18.1 0.0 copy-start
  18.1 16.6 %all-to-all-done = f32[64,32,128]{2,1,0:T(8,128)S(1)} async-done(((f32[64,32,128]{2,1,0:T(8,128)}), f32[64,32,128]{2,1,0:T(8,128)S(1)}, u32[]{:S(2)}, u32[]{:S(2)}) %all-to-all-start) | async-done | bytes 1048608 | tf_op jit(solution)/shard_map/all_to_all | solution.py:468
  34.7 0.0 copy-done
  34.7 0.9 detect.1
  35.6 4.7 %all-to-all-start.2 = ((f32[64,8,128]{2,1,0:T(8,128)}), f32[64,8,128]{2,1,0:T(8,128)S(1)}, u32[]{:S(2)}, u32[]{:S(2)}) async-start(f32[64,8,128]{2,1,0:T(8,128)} %get-tuple-element.14), calls=%async_computation.2 | async-start | bytes 524288 | tf_op jit(solution)/shard_map/all_to_all | solution.py:495
  40.4 1.1 %bring.1 = (bf16[256,256]{1,0:T(8,128)(2,1)S(1)}, bf16[256,256]{1,0:T(8,128)(2,1)S(1)}, bf16[256,256]{1,0:T(8,128)(2,1)S(1)}, bf16[256,256]{1,0:T(8,128)(2,1)S(1)}) custom-call(bf16[256,256]{1,0:T(8,128)(2,1)} %constant.110.clone.refs_2_.refs_0_, bf16[256,256]{1,0:T(8,128)(2,1)} %constant.111.clone.refs_3_.refs_1_, ...), custom_call_target="tpu_custom_call" | custom-call | tf_op jit(solution)/shard_map/bring/pallas_call | solution.py:498
  41.5 8.7 %all-to-all-done.2 = f32[64,8,128]{2,1,0:T(8,128)S(1)} async-done(((f32[64,8,128]{2,1,0:T(8,128)}), f32[64,8,128]{2,1,0:T(8,128)S(1)}, u32[]{:S(2)}, u32[]{:S(2)}) %all-to-all-start.2) | async-done | bytes 262176 | tf_op jit(solution)/shard_map/all_to_all | solution.py:495
  50.2 3.2 %gradient.1 = f32[4,256,128]{2,1,0:T(8,128)S(1)} custom-call(f32[512,128]{1,0:T(8,128)S(1)} %bitcast.23, f32[2,256,128]{2,1,0:T(8,128)S(1)} %get-tuple-element.15.refs_1_, f32[2,256,128]{2,1,0:T(8,128)S(1)} %get-tuple-element.16.refs_2_, bf16[256,256]{1,0:T(8,128)(2,1)S(1)} %get-tuple-element.17.refs_3_, bf16[256,256]{1,0:T(8,128)(2,1)S(1)} %get-tuple-element.18.refs_4_, ...), custom_call_target="tpu_custom_call" | custom-call | tf_op jit(solution)/shard_map/gradient/pallas_call | solution.py:507
  53.4 2.7 %collective-permute-start = (f32[4,256,128]{2,1,0:T(8,128)S(1)}, f32[4,256,128]{2,1,0:T(8,128)S(1)}, u32[]{:S(2)}, u32[]{:S(2)}) collective-permute-start(f32[4,256,128]{2,1,0:T(8,128)S(1)} %gradient.1), channel_id=1, source_target_pairs={{0,64},{64,0},{1,65},{65,1},{2,66},{66,2},{3,67},{67,3},{4,68},{68... | collective-permute-start | bytes 1572872 | tf_op jit(solution)/shard_map/ppermute | solution.py:520
  56.1 3.6 %depth.1 = f32[2048,128]{1,0:T(8,128)} custom-call(f32[2048,128]{1,0:T(8,128)S(1)} %bitcast.21, f32[2048,128]{1,0:T(8,128)} %bitcast.27, bf16[256,256]{1,0:T(8,128)(2,1)} %constant.114.clone.refs_2_, bf16[256,256]{1,0:T(8,128)(2,1)} %constant.115.clone.refs_3_, bf16[256,256]{1,0:T(8,128)(2,1)} %constant.116.clone.refs_4_, ...), custom_call_target="tpu_custom_call" | custom-call | tf_op jit(solution)/shard_map/depth/pallas_call | solution.py:521
  59.7 4.8 %all-to-all-start.1 = ((f32[64,32,128]{2,1,0:T(8,128)}), f32[64,32,128]{2,1,0:T(8,128)S(1)}, u32[]{:S(2)}, u32[]{:S(2)}) async-start(f32[64,32,128]{2,1,0:T(8,128)} %bitcast.4), calls=%async_computation.1 | async-start | bytes 2097152 | tf_op jit(solution)/shard_map/all_to_all | solution.py:530
  64.6 3.8 %collective-permute-done = f32[4,256,128]{2,1,0:T(8,128)S(1)} collective-permute-done((f32[4,256,128]{2,1,0:T(8,128)S(1)}, f32[4,256,128]{2,1,0:T(8,128)S(1)}, u32[]{:S(2)}, u32[]{:S(2)}) %collective-permute-start) | collective-permute-done | bytes 524320 | tf_op jit(solution)/shard_map/ppermute | solution.py:520
  68.4 0.1 add.96.refs_2_
  68.5 9.5 %collective-permute-start.1 = (f32[4,256,128]{2,1,0:T(8,128)S(1)}, f32[4,256,128]{2,1,0:T(8,128)S(1)}, u32[]{:S(2)}, u32[]{:S(2)}) collective-permute-start(f32[4,256,128]{2,1,0:T(8,128)S(1)} %add.96.refs_2_), channel_id=1, source_target_pairs={{0,1},{1,2},{2,3},{3,4},{4,5},{5,6},{6,7},{7,8},{8,9},{9,10},{10,1... | collective-permute-start | bytes 1572872 | tf_op jit(solution)/shard_map/ppermute | solution.py:535
  77.9 2.1 %collective-permute-start.2 = (f32[4,256,128]{2,1,0:T(8,128)S(1)}, f32[4,256,128]{2,1,0:T(8,128)S(1)}, u32[]{:S(2)}, u32[]{:S(2)}) collective-permute-start(f32[4,256,128]{2,1,0:T(8,128)S(1)} %add.96.refs_2_), channel_id=1, source_target_pairs={{1,0},{2,1},{3,2},{4,3},{5,4},{6,5},{7,6},{8,7},{9,8},{10,9},{11,1... | collective-permute-start | bytes 1572872 | tf_op jit(solution)/shard_map/ppermute | solution.py:536
  80.0 3.0 %all-to-all-done.1 = f32[64,32,128]{2,1,0:T(8,128)S(1)} async-done(((f32[64,32,128]{2,1,0:T(8,128)}), f32[64,32,128]{2,1,0:T(8,128)S(1)}, u32[]{:S(2)}, u32[]{:S(2)}) %all-to-all-start.1) | async-done | bytes 1048608 | tf_op jit(solution)/shard_map/all_to_all | solution.py:530
  83.0 3.6 %field.1 = f32[2,4,256,128]{3,2,1,0:T(8,128)} custom-call(f32[2048,128]{1,0:T(8,128)S(1)} %bitcast.22, bf16[2,4,256,128]{3,2,1,0:T(8,128)(2,1)} %bitcast.29, bf16[256,256]{1,0:T(8,128)(2,1)} %constant.110.clone.refs_2_.refs_0_, bf16[256,256]{1,0:T(8,128)(2,1)} %constant.111.clone.refs_3_.refs_1_, bf16[256,256]{1,0:T(8,128)(2,1)} %constant.112.clone.refs_4_.refs_2_, ...), custom_call_target="tpu_custom_call" | custom-call | tf_op jit(solution)/shard_map/field/pallas_call | solution.py:538
  86.6 0.0 collective-permute-done.1.refs_1_
  86.6 1.8 %collective-permute-done.2.refs_3_ = f32[4,256,128]{2,1,0:T(8,128)S(1)} collective-permute-done((f32[4,256,128]{2,1,0:T(8,128)S(1)}, f32[4,256,128]{2,1,0:T(8,128)S(1)}, u32[]{:S(2)}, u32[]{:S(2)}) %collective-permute-start.2) | collective-permute-done | bytes 524320 | tf_op jit(solution)/shard_map/ppermute | solution.py:536
  88.4 6.6 %smooth.1 = f32[4,256,128]{2,1,0:T(8,128)} custom-call(s32[1]{0:T(128)} %bitcast.14.refs_0_, f32[4,256,128]{2,1,0:T(8,128)S(1)} %collective-permute-done.1.refs_1_, f32[4,256,128]{2,1,0:T(8,128)S(1)} %add.96.refs_2_, f32[4,256,128]{2,1,0:T(8,128)S(1)} %collective-permute-done.2.refs_3_), custom_call_target="tpu_custom_call" | custom-call | tf_op jit(solution)/shard_map/smooth/pallas_call | solution.py:556
  (7 shorter events, 0.1 us)
Async XLA Ops:
  5.8 28.9 %all-to-all-start = ((f32[64,32,128]{2,1,0:T(8,128)}), f32[64,32,128]{2,1,0:T(8,128)S(1)}, u32[]{:S(2)}, u32[]{:S(2)}) async-start(f32[64,32,128]{2,1,0:T(8,128)} %bitcast.1), calls=%async_computation | async-start | bytes 2097152 | tf_op jit(solution)/shard_map/all_to_all | solution.py:468
  18.1 16.7 %copy-start = (f32[1,2,4,128]{3,2,1,0:T(4,128)S(1)}, f32[1,2,4,128]{3,2,1,0:T(4,128)}, u32[]{:S(2)}) copy-start(f32[1,2,4,128]{3,2,1,0:T(4,128)} %param.21) | copy-start | bytes 12292
  35.6 14.5 %all-to-all-start.2 = ((f32[64,8,128]{2,1,0:T(8,128)}), f32[64,8,128]{2,1,0:T(8,128)S(1)}, u32[]{:S(2)}, u32[]{:S(2)}) async-start(f32[64,8,128]{2,1,0:T(8,128)} %get-tuple-element.14), calls=%async_computation.2 | async-start | bytes 524288 | tf_op jit(solution)/shard_map/all_to_all | solution.py:495
  53.4 15.0 %collective-permute-start = (f32[4,256,128]{2,1,0:T(8,128)S(1)}, f32[4,256,128]{2,1,0:T(8,128)S(1)}, u32[]{:S(2)}, u32[]{:S(2)}) collective-permute-start(f32[4,256,128]{2,1,0:T(8,128)S(1)} %gradient.1), channel_id=1, source_target_pairs={{0,64},{64,0},{1,65},{65,1},{2,66},{66,2},{3,67},{67,3},{4,68},{68... | collective-permute-start | bytes 1572872 | tf_op jit(solution)/shard_map/ppermute | solution.py:520
  59.7 23.3 %all-to-all-start.1 = ((f32[64,32,128]{2,1,0:T(8,128)}), f32[64,32,128]{2,1,0:T(8,128)S(1)}, u32[]{:S(2)}, u32[]{:S(2)}) async-start(f32[64,32,128]{2,1,0:T(8,128)} %bitcast.4), calls=%async_computation.1 | async-start | bytes 2097152 | tf_op jit(solution)/shard_map/all_to_all | solution.py:530
  68.5 18.1 %collective-permute-start.1 = (f32[4,256,128]{2,1,0:T(8,128)S(1)}, f32[4,256,128]{2,1,0:T(8,128)S(1)}, u32[]{:S(2)}, u32[]{:S(2)}) collective-permute-start(f32[4,256,128]{2,1,0:T(8,128)S(1)} %add.96.refs_2_), channel_id=1, source_target_pairs={{0,1},{1,2},{2,3},{3,4},{4,5},{5,6},{6,7},{7,8},{8,9},{9,10},{10,1... | collective-permute-start | bytes 1572872 | tf_op jit(solution)/shard_map/ppermute | solution.py:535
  77.9 10.5 %collective-permute-start.2 = (f32[4,256,128]{2,1,0:T(8,128)S(1)}, f32[4,256,128]{2,1,0:T(8,128)S(1)}, u32[]{:S(2)}, u32[]{:S(2)}) collective-permute-start(f32[4,256,128]{2,1,0:T(8,128)S(1)} %add.96.refs_2_), channel_id=1, source_target_pairs={{1,0},{2,1},{3,2},{4,3},{5,4},{6,5},{7,6},{8,7},{9,8},{10,9},{11,1... | collective-permute-start | bytes 1572872 | tf_op jit(solution)/shard_map/ppermute | solution.py:536

commit v4 on v3

--- a/solution.py
+++ b/solution.py
@@ -245,35 +245,44 @@
     out,
     fv,
     cv,
+    miss,
+    hold,
     sems,
 ):
     local = cv.shape[0]
-    sources, targets = [], []
+    lanes = out.shape[2]
+
+    def copies(plane):
+        return (
+            pltpu.make_async_copy(field.at[:, plane], fv.at[plane], sems.at[0, plane]),
+            pltpu.make_async_copy(contrast.at[plane], cv.at[plane], sems.at[1, plane]),
+        )
+
     for plane in range(local - 1, -1, -1):
-        sources += [field.at[:, plane], contrast.at[plane]]
-        targets += [fv.at[plane], cv.at[plane]]
-    copies = fetch(sources, targets, sems)
+        for copy in copies(plane):
+            copy.start()
     starts = [[part * block + row for row in range(block)] for part in range(2)]
-    miss = gather_rows(gathered, starts, slabs, 2 * block) * (1.0 / root_depth)
-    lanes = miss.shape[1] // 2
-    miss = (miss[:, :lanes], miss[:, lanes:])
-    real, imag = prop[0], prop[1]
-    for plane in range(local - 1, -1, -1):
+    miss[...] = gather_rows(gathered, starts, slabs, 2 * block) * (1.0 / root_depth)
+    hold[...] = prop[...]
+
+    def body(count, carry):
+        plane = local - 1 - count
+        real, imag = hold[0], hold[1]
+        miss_real, miss_imag = miss[:, :lanes], miss[:, lanes:]
         wide = jnp.concatenate(
-            [real * miss[0] + imag * miss[1], real * miss[1] - imag * miss[0]], 1
+            [real * miss_real + imag * miss_imag, real * miss_imag - imag * miss_real], 1
         )
+        hold[0] = real * step[0] - imag * step[1]
+        hold[1] = real * step[1] + imag * step[0]
         wide = product((xh[...], xl[...]), split(wide))
         wide = product(split(wide), (yh[...], yl[...]))
-        spot = 2 * (local - 1 - plane)
-        for copy in copies[spot : spot + 2]:
+        for copy in copies(plane):
             copy.wait()
         terms = fv[plane, 0] * wide[:, :lanes] + fv[plane, 1] * wide[:, lanes:]
-        out[plane] = 0.5 * cv[plane] - step_size * terms
-        if plane > 0:
-            real, imag = (
-                real * step[0] - imag * step[1],
-                real * step[1] + imag * step[0],
-            )
+        out[plane] = (0.5 / diffusion) * cv[plane] - (step_size / diffusion) * terms
+        return carry
+
+    lax.fori_loop(0, local, body, 0)
 
 
 def field_kernel(
@@ -320,32 +329,36 @@
         copy.wait()
 
 
-def smooth_kernel(depth, limits, before, own, after, out, ping, pong, flux, stage, sems):
+def smooth_kernel(depth, limits, before, own, after, out, ping, pong, flux, side, stage, sems):
     local, rows, lanes = own.shape
     total = local + 2 * PASSES
-    size = 64
+    floor = (edge_scale / diffusion) ** 2
+    size, together = 128, 2
     ping[:PASSES, :rows] = before[...]
     ping[PASSES : PASSES + local, :rows] = own[...]
     ping[PASSES + local :, :rows] = after[...]
     for plane in range(total):
         ping[plane, rows:] = jnp.broadcast_to(ping[plane, rows - 1 : rows], (8, lanes))
+    side[:, :8] = jnp.zeros((together, 8, lanes), f32)
     last_lane = lax.broadcasted_iota(jnp.int32, (size, lanes), 1) == lanes - 1
-    first_row = lax.broadcasted_iota(jnp.int32, (size, lanes), 0) == 0
-    first = limits[0]
-
-    def inside(plane):
-        spot = first + plane
-        return jnp.where((spot >= 0) & (spot <= depth - 2), 1.0, 0.0).astype(f32)
-
-    def slopes(source, plane, start, gate):
+
+    def close(ref):
+        @pl.when(limits[0] == 0)
+        def _():
+            ref[PASSES - 1] = ref[PASSES]
+
+        @pl.when(limits[0] == depth - local)
+        def _():
+            ref[PASSES + local] = ref[PASSES + local - 1]
+
+    def slopes(source, plane, start):
         core = source[plane, start : start + size]
-        slope_depth = (source[plane + 1, start : start + size] - core) * gate
+        slope_depth = source[plane + 1, start : start + size] - core
         slope_rows = source[plane, start + 1 : start + size + 1] - core
         slope_lanes = jnp.where(last_lane, 0.0, pltpu.roll(core, lanes - 1, 1) - core)
         scale = lax.rsqrt(
-            slope_depth * slope_depth
-            + slope_rows * slope_rows
-            + (slope_lanes * slope_lanes + edge_scale**2)
+            (slope_depth * slope_depth + slope_rows * slope_rows)
+            + (slope_lanes * slope_lanes + floor)
         )
         return core, slope_depth * scale, slope_rows * scale, slope_lanes * scale
 
@@ -353,48 +366,52 @@
     for repeat in range(PASSES):
         final = repeat == PASSES - 1
         low, high = repeat + 1, total - 1 - repeat
-        gate = inside(low - 1)
+        close(source)
         for start in range(0, rows, size):
-            flux[start : start + size] = slopes(source, low - 1, start, gate)[1]
-
-        def body(plane, carry, source=source, target=target, final=final):
-            gate = inside(plane)
-            above = jnp.zeros((1, lanes), f32)
+            flux[start : start + size] = slopes(source, low - 1, start)[1]
+
+        def body(plane, slot, source=source, target=target, final=final):
             for start in range(0, rows, size):
                 here = slice(start, start + size)
-                core, flux_depth, flux_rows, flux_lanes = slopes(source, plane, start, gate)
-                shifted = jnp.where(first_row, above, pltpu.roll(flux_rows, 1, 0))
-                above = flux_rows[size - 1 : size]
-                spread = (
+                core, flux_depth, flux_rows, flux_lanes = slopes(source, plane, start)
+                side[slot, 8 + start : 8 + start + size] = flux_rows
+                value = core + (
                     (flux_depth - flux[here])
-                    + (flux_rows - shifted)
                     + (flux_lanes - pltpu.roll(flux_lanes, 1, 1))
+                    + (flux_rows - side[slot, 7 + start : 7 + start + size])
                 )
                 flux[here] = flux_depth
-                value = core + diffusion * spread
                 if final:
-                    stage[plane - PASSES, here] = value
+                    stage[plane - PASSES, here] = value * diffusion
                 else:
                     target[plane, here] = value
                     if start + size == rows:
                         target[plane, rows:] = jnp.broadcast_to(
                             value[size - 1 : size], (8, lanes)
                         )
-            return carry
 
         if final:
-            copies = []
-            for plane in range(low, high):
-                body(plane, 0)
-                spot = plane - PASSES
-                copy = pltpu.make_async_copy(stage.at[spot], out.at[spot], sems.at[spot])
-                copy.start()
-                copies.append(copy)
-            for copy in copies:
-                copy.wait()
+
+            def ending(step, carry, body=body, low=low):
+                for slot in range(together):
+                    plane = low + step * together + slot
+                    body(plane, slot)
+                    spot = plane - PASSES
+                    pltpu.make_async_copy(stage.at[spot], out.at[spot], sems.at[spot]).start()
+                return carry
+
+            lax.fori_loop(0, (high - low) // together, ending, 0)
         else:
-            lax.fori_loop(low, high, body, 0)
+
+            def group(step, carry, body=body, low=low):
+                for slot in range(together):
+                    body(low + step * together + slot, slot)
+                return carry
+
+            lax.fori_loop(0, (high - low) // together, group, 0)
         source, target = target, source
+    for spot in range(local):
+        pltpu.make_async_copy(stage.at[spot], out.at[spot], sems.at[spot]).wait()
 
 
 def frequency(index, length):
@@ -512,7 +529,9 @@
         scratch_shapes=[
             pltpu.VMEM((local, 2, width_x, width_y), f32),
             pltpu.VMEM((local, width_x, width_y), f32),
-            sem((2 * local,)),
+            pltpu.VMEM((width_x, 2 * width_y), f32),
+            pltpu.VMEM((2, width_x, width_y), f32),
+            sem((2, local)),
         ],
         compiler_params=params(),
         name="gradient",
@@ -551,7 +570,7 @@
         name="field",
     )(volume.reshape(lines, width_y), incident, *back_x, *back_y)
 
-    limits = (place * local - PASSES).astype(jnp.int32).reshape(1)
+    limits = (place * local).astype(jnp.int32).reshape(1)
     work = pltpu.VMEM((local + 2 * PASSES, width_x + 8, width_y), f32)
     smoothed = pl.pallas_call(
         lambda *refs: smooth_kernel(depth, *refs),
@@ -562,6 +581,7 @@
             work,
             work,
             pltpu.VMEM((width_x, width_y), f32),
+            pltpu.VMEM((2, width_x + 8, width_y), f32),
             pltpu.VMEM((local, width_x, width_y), f32),
             sem((local,)),
         ],

time: 95.7 us -> 93.8 us (0.980)
  Pallas kernels: 24.3 us -> 22.5 us
    pallas_call x1, Pallas kernels: 6.62 us -> 4.92 us  [shards(): pl.pallas_call(lambda *refs: smooth_kernel(depth, *refs), out_shape=jax.S...]
where the time goes in v4:
time: 93.8 us; the launch traced here: 93.3 us
  starting transfers between devices  34.5 us (37%)
  waiting for transfers between devices  34.1 us (36%)
  Pallas kernels  22.5 us (24%)
  other arithmetic  1.36 us (1%)
    all_to_all x1, waiting for transfers between devices, shards(): lax.all_to_all(packed.reshape(slabs, chunk, width_y), 'slab', 0, 0, tiled...  16.6 us
    all_to_all x1, starting transfers between devices, shards(): lax.all_to_all(packed.reshape(slabs, chunk, width_y), 'slab', 0, 0, tiled...  10.8 us
    ppermute x1, starting transfers between devices, shards(): before = lax.ppermute(updated, 'slab', up)  9.46 us
    all_to_all x1, waiting for transfers between devices, shards(): gathered = lax.all_to_all(spread, 'slab', 0, 0, tiled=True)  8.65 us
    pallas_call x1, Pallas kernels, shards(): pl.pallas_call(lambda *refs: forward_kernel(block, slabs, *refs), out_sha...  5.19 us
    pallas_call x1, Pallas kernels, shards(): pl.pallas_call(lambda *refs: smooth_kernel(depth, *refs), out_shape=jax.S...  4.92 us
    all_to_all x1, starting transfers between devices, shards(): lax.all_to_all(volume.reshape(slabs, chunk, width_y), 'slab', 0, 0, tiled...  4.84 us
    all_to_all x1, starting transfers between devices, shards(): gathered = lax.all_to_all(spread, 'slab', 0, 0, tiled=True)  4.73 us
  transfers between devices with their start and end apart: 6, of which 5 were waited for; matrix products, arithmetic and copies ran while one was open for 1% of the time, Pallas kernels for 9%

profile of v4, /device:TPU:1, one launch (start us, length us, event | category | flops | bytes accessed | tf_op | source)
XLA Modules:
  0.0 93.3 jit_solution(519842089768502680)
XLA Ops:
  0.6 5.2 %forward.1 = f32[64,4,8,128]{3,2,1,0:T(8,128)} custom-call(f32[2,4,256,128]{3,2,1,0:T(8,128)} %bitcast.25, f32[4,256,128]{2,1,0:T(8,128)} %refs_8_.1, bf16[256,256]{1,0:T(8,128)(2,1)} %constant.104.clone.refs_2_, bf16[256,256]{1,0:T(8,128)(2,1)} %constant.105.clone.refs_3_, bf16[256,256]{1,0:T(8,128)(2,1)} %constant.106.clone.refs_4_, ...), custom_call_target="tpu_custom_call" | custom-call | tf_op jit(solution)/shard_map/forward/pallas_call | solution.py:466
  5.8 10.8 %all-to-all-start = ((f32[64,32,128]{2,1,0:T(8,128)}), f32[64,32,128]{2,1,0:T(8,128)S(1)}, u32[]{:S(2)}, u32[]{:S(2)}) async-start(f32[64,32,128]{2,1,0:T(8,128)} %bitcast.1), calls=%async_computation | async-start | bytes 2097152 | tf_op jit(solution)/shard_map/all_to_all | solution.py:485
  16.7 0.1 cosine_multiply_fusion.1
  16.9 1.1 %fusion.11 = (f32[1,256,128]{2,1,0:T(8,128)S(1)}, f32[1,256,128]{2,1,0:T(8,128)S(1)}, f32[1,256,128]{2,1,0:T(8,128)S(1)}, f32[1,256,128]{2,1,0:T(8,128)S(1)}) fusion(f32[128]{0:T(128)S(1)} %fusion.36, f32[256]{0:T(256)S(1)} %fusion.33, f32[]{:T(128)S(6)} %convert_element_type.53), kind=kLoop, calls=%fused_computation.15 | loop fusion | flops 458752 | bytes 525828 | tf_op jit(solution)/shard_map/mul | solution.py:430
  18.1 0.0 copy-start
  18.1 16.6 %all-to-all-done = f32[64,32,128]{2,1,0:T(8,128)S(1)} async-done(((f32[64,32,128]{2,1,0:T(8,128)}), f32[64,32,128]{2,1,0:T(8,128)S(1)}, u32[]{:S(2)}, u32[]{:S(2)}) %all-to-all-start) | async-done | bytes 1048608 | tf_op jit(solution)/shard_map/all_to_all | solution.py:485
  34.7 0.0 copy-done
  34.7 0.9 detect.1
  35.6 4.7 %all-to-all-start.2 = ((f32[64,8,128]{2,1,0:T(8,128)}), f32[64,8,128]{2,1,0:T(8,128)S(1)}, u32[]{:S(2)}, u32[]{:S(2)}) async-start(f32[64,8,128]{2,1,0:T(8,128)} %get-tuple-element.14), calls=%async_computation.2 | async-start | bytes 524288 | tf_op jit(solution)/shard_map/all_to_all | solution.py:512
  40.4 1.1 %bring.1 = (bf16[256,256]{1,0:T(8,128)(2,1)S(1)}, bf16[256,256]{1,0:T(8,128)(2,1)S(1)}, bf16[256,256]{1,0:T(8,128)(2,1)S(1)}, bf16[256,256]{1,0:T(8,128)(2,1)S(1)}) custom-call(bf16[256,256]{1,0:T(8,128)(2,1)} %constant.108.clone.refs_2_.refs_0_, bf16[256,256]{1,0:T(8,128)(2,1)} %constant.109.clone.refs_3_.refs_1_, ...), custom_call_target="tpu_custom_call" | custom-call | tf_op jit(solution)/shard_map/bring/pallas_call | solution.py:515
  41.5 8.7 %all-to-all-done.2 = f32[64,8,128]{2,1,0:T(8,128)S(1)} async-done(((f32[64,8,128]{2,1,0:T(8,128)}), f32[64,8,128]{2,1,0:T(8,128)S(1)}, u32[]{:S(2)}, u32[]{:S(2)}) %all-to-all-start.2) | async-done | bytes 262176 | tf_op jit(solution)/shard_map/all_to_all | solution.py:512
  50.2 3.1 %gradient.1 = f32[4,256,128]{2,1,0:T(8,128)S(1)} custom-call(f32[512,128]{1,0:T(8,128)S(1)} %bitcast.23, f32[2,256,128]{2,1,0:T(8,128)S(1)} %get-tuple-element.15.refs_1_, f32[2,256,128]{2,1,0:T(8,128)S(1)} %get-tuple-element.16.refs_2_, bf16[256,256]{1,0:T(8,128)(2,1)S(1)} %get-tuple-element.17.refs_3_, bf16[256,256]{1,0:T(8,128)(2,1)S(1)} %get-tuple-element.18.refs_4_, ...), custom_call_target="tpu_custom_call" | custom-call | tf_op jit(solution)/shard_map/gradient/pallas_call | solution.py:524
  53.3 2.7 %collective-permute-start = (f32[4,256,128]{2,1,0:T(8,128)S(1)}, f32[4,256,128]{2,1,0:T(8,128)S(1)}, u32[]{:S(2)}, u32[]{:S(2)}) collective-permute-start(f32[4,256,128]{2,1,0:T(8,128)S(1)} %gradient.1), channel_id=1, source_target_pairs={{0,64},{64,0},{1,65},{65,1},{2,66},{66,2},{3,67},{67,3},{4,68},{68... | collective-permute-start | bytes 1572872 | tf_op jit(solution)/shard_map/ppermute | solution.py:539
  56.0 3.6 %depth.1 = f32[2048,128]{1,0:T(8,128)} custom-call(f32[2048,128]{1,0:T(8,128)S(1)} %bitcast.21, f32[2048,128]{1,0:T(8,128)} %bitcast.27, bf16[256,256]{1,0:T(8,128)(2,1)} %constant.112.clone.refs_2_, bf16[256,256]{1,0:T(8,128)(2,1)} %constant.113.clone.refs_3_, bf16[256,256]{1,0:T(8,128)(2,1)} %constant.114.clone.refs_4_, ...), custom_call_target="tpu_custom_call" | custom-call | tf_op jit(solution)/shard_map/depth/pallas_call | solution.py:540
  59.6 4.8 %all-to-all-start.1 = ((f32[64,32,128]{2,1,0:T(8,128)}), f32[64,32,128]{2,1,0:T(8,128)S(1)}, u32[]{:S(2)}, u32[]{:S(2)}) async-start(f32[64,32,128]{2,1,0:T(8,128)} %bitcast.4), calls=%async_computation.1 | async-start | bytes 2097152 | tf_op jit(solution)/shard_map/all_to_all | solution.py:549
  64.5 3.8 %collective-permute-done = f32[4,256,128]{2,1,0:T(8,128)S(1)} collective-permute-done((f32[4,256,128]{2,1,0:T(8,128)S(1)}, f32[4,256,128]{2,1,0:T(8,128)S(1)}, u32[]{:S(2)}, u32[]{:S(2)}) %collective-permute-start) | collective-permute-done | bytes 524320 | tf_op jit(solution)/shard_map/ppermute | solution.py:539
  68.3 0.1 add.95.refs_2_
  68.4 9.5 %collective-permute-start.1 = (f32[4,256,128]{2,1,0:T(8,128)S(1)}, f32[4,256,128]{2,1,0:T(8,128)S(1)}, u32[]{:S(2)}, u32[]{:S(2)}) collective-permute-start(f32[4,256,128]{2,1,0:T(8,128)S(1)} %add.95.refs_2_), channel_id=1, source_target_pairs={{0,1},{1,2},{2,3},{3,4},{4,5},{5,6},{6,7},{7,8},{8,9},{9,10},{10,1... | collective-permute-start | bytes 1572872 | tf_op jit(solution)/shard_map/ppermute | solution.py:554
  77.8 1.9 %collective-permute-start.2 = (f32[4,256,128]{2,1,0:T(8,128)S(1)}, f32[4,256,128]{2,1,0:T(8,128)S(1)}, u32[]{:S(2)}, u32[]{:S(2)}) collective-permute-start(f32[4,256,128]{2,1,0:T(8,128)S(1)} %add.95.refs_2_), channel_id=1, source_target_pairs={{1,0},{2,1},{3,2},{4,3},{5,4},{6,5},{7,6},{8,7},{9,8},{10,9},{11,1... | collective-permute-start | bytes 1572872 | tf_op jit(solution)/shard_map/ppermute | solution.py:555
  79.8 3.1 %all-to-all-done.1 = f32[64,32,128]{2,1,0:T(8,128)S(1)} async-done(((f32[64,32,128]{2,1,0:T(8,128)}), f32[64,32,128]{2,1,0:T(8,128)S(1)}, u32[]{:S(2)}, u32[]{:S(2)}) %all-to-all-start.1) | async-done | bytes 1048608 | tf_op jit(solution)/shard_map/all_to_all | solution.py:549
  82.9 3.6 %field.1 = f32[2,4,256,128]{3,2,1,0:T(8,128)} custom-call(f32[2048,128]{1,0:T(8,128)S(1)} %bitcast.22, bf16[2,4,256,128]{3,2,1,0:T(8,128)(2,1)} %bitcast.29, bf16[256,256]{1,0:T(8,128)(2,1)} %constant.108.clone.refs_2_.refs_0_, bf16[256,256]{1,0:T(8,128)(2,1)} %constant.109.clone.refs_3_.refs_1_, bf16[256,256]{1,0:T(8,128)(2,1)} %constant.110.clone.refs_4_.refs_2_, ...), custom_call_target="tpu_custom_call" | custom-call | tf_op jit(solution)/shard_map/field/pallas_call | solution.py:557
  86.5 0.0 collective-permute-done.1.refs_1_
  86.5 1.8 %collective-permute-done.2.refs_3_ = f32[4,256,128]{2,1,0:T(8,128)S(1)} collective-permute-done((f32[4,256,128]{2,1,0:T(8,128)S(1)}, f32[4,256,128]{2,1,0:T(8,128)S(1)}, u32[]{:S(2)}, u32[]{:S(2)}) %collective-permute-start.2) | collective-permute-done | bytes 524320 | tf_op jit(solution)/shard_map/ppermute | solution.py:555
  88.3 4.9 %smooth.1 = f32[4,256,128]{2,1,0:T(8,128)} custom-call(s32[1]{0:T(128)} %bitcast.14.refs_0_, f32[4,256,128]{2,1,0:T(8,128)S(1)} %collective-permute-done.1.refs_1_, f32[4,256,128]{2,1,0:T(8,128)S(1)} %add.95.refs_2_, f32[4,256,128]{2,1,0:T(8,128)S(1)} %collective-permute-done.2.refs_3_), custom_call_target="tpu_custom_call" | custom-call | tf_op jit(solution)/shard_map/smooth/pallas_call | solution.py:575
  (7 shorter events, 0.1 us)
Async XLA Ops:
  5.8 28.9 %all-to-all-start = ((f32[64,32,128]{2,1,0:T(8,128)}), f32[64,32,128]{2,1,0:T(8,128)S(1)}, u32[]{:S(2)}, u32[]{:S(2)}) async-start(f32[64,32,128]{2,1,0:T(8,128)} %bitcast.1), calls=%async_computation | async-start | bytes 2097152 | tf_op jit(solution)/shard_map/all_to_all | solution.py:485
  18.1 16.7 %copy-start = (f32[1,2,4,128]{3,2,1,0:T(4,128)S(1)}, f32[1,2,4,128]{3,2,1,0:T(4,128)}, u32[]{:S(2)}) copy-start(f32[1,2,4,128]{3,2,1,0:T(4,128)} %param.21) | copy-start | bytes 12292
  35.6 14.5 %all-to-all-start.2 = ((f32[64,8,128]{2,1,0:T(8,128)}), f32[64,8,128]{2,1,0:T(8,128)S(1)}, u32[]{:S(2)}, u32[]{:S(2)}) async-start(f32[64,8,128]{2,1,0:T(8,128)} %get-tuple-element.14), calls=%async_computation.2 | async-start | bytes 524288 | tf_op jit(solution)/shard_map/all_to_all | solution.py:512
  53.3 15.0 %collective-permute-start = (f32[4,256,128]{2,1,0:T(8,128)S(1)}, f32[4,256,128]{2,1,0:T(8,128)S(1)}, u32[]{:S(2)}, u32[]{:S(2)}) collective-permute-start(f32[4,256,128]{2,1,0:T(8,128)S(1)} %gradient.1), channel_id=1, source_target_pairs={{0,64},{64,0},{1,65},{65,1},{2,66},{66,2},{3,67},{67,3},{4,68},{68... | collective-permute-start | bytes 1572872 | tf_op jit(solution)/shard_map/ppermute | solution.py:539
  59.6 23.3 %all-to-all-start.1 = ((f32[64,32,128]{2,1,0:T(8,128)}), f32[64,32,128]{2,1,0:T(8,128)S(1)}, u32[]{:S(2)}, u32[]{:S(2)}) async-start(f32[64,32,128]{2,1,0:T(8,128)} %bitcast.4), calls=%async_computation.1 | async-start | bytes 2097152 | tf_op jit(solution)/shard_map/all_to_all | solution.py:549
  68.4 18.1 %collective-permute-start.1 = (f32[4,256,128]{2,1,0:T(8,128)S(1)}, f32[4,256,128]{2,1,0:T(8,128)S(1)}, u32[]{:S(2)}, u32[]{:S(2)}) collective-permute-start(f32[4,256,128]{2,1,0:T(8,128)S(1)} %add.95.refs_2_), channel_id=1, source_target_pairs={{0,1},{1,2},{2,3},{3,4},{4,5},{5,6},{6,7},{7,8},{8,9},{9,10},{10,1... | collective-permute-start | bytes 1572872 | tf_op jit(solution)/shard_map/ppermute | solution.py:554
  77.8 10.5 %collective-permute-start.2 = (f32[4,256,128]{2,1,0:T(8,128)S(1)}, f32[4,256,128]{2,1,0:T(8,128)S(1)}, u32[]{:S(2)}, u32[]{:S(2)}) collective-permute-start(f32[4,256,128]{2,1,0:T(8,128)S(1)} %add.95.refs_2_), channel_id=1, source_target_pairs={{1,0},{2,1},{3,2},{4,3},{5,4},{6,5},{7,6},{8,7},{9,8},{10,9},{11,1... | collective-permute-start | bytes 1572872 | tf_op jit(solution)/shard_map/ppermute | solution.py:555

commit v5 on v4

--- a/solution.py
+++ b/solution.py
@@ -298,14 +298,10 @@
     out,
     iv,
     stage,
-    xhv,
-    xlv,
-    yhv,
-    ylv,
     sems,
     out_sems,
 ):
-    fetched = fetch([xh, xl, yh, yl, incident], [xhv, xlv, yhv, ylv, iv], sems)
+    fetched = fetch([incident], [iv], sems)
     stride = local * 2 * block
     copies = []
     for plane in range(local):
@@ -314,11 +310,11 @@
             for part in range(2)
         ]
         wide = gather_rows(volume, starts, slabs, stride)
+        wide = product((xh[...], xl[...]), split(wide))
+        wide = product(split(wide), (yh[...], yl[...]))
         if plane == 0:
             for copy in fetched:
                 copy.wait()
-        wide = product((xhv[...], xlv[...]), split(wide))
-        wide = product(split(wide), (yhv[...], ylv[...]))
         lanes = wide.shape[1] // 2
         stage[plane, 0] = iv[0, plane].astype(f32) + wide[:, :lanes]
         stage[plane, 1] = iv[1, plane].astype(f32) + wide[:, lanes:]
@@ -547,7 +543,16 @@
         name="depth",
     )(columns, green, *ahead_z, *back_z)
     volume = lax.all_to_all(volume.reshape(slabs, chunk, width_y), "slab", 0, 0, tiled=True)
-    tables = [x_table, x_table, y_table, y_table]
+    brought = [*back_y, *back_x]
+    nearer = pl.pallas_call(
+        lambda *refs: bring_kernel(len(brought), *refs),
+        out_shape=[jax.ShapeDtypeStruct(x.shape, x.dtype) for x in brought],
+        in_specs=[hbm] * len(brought),
+        out_specs=[vmem] * len(brought),
+        scratch_shapes=[sem((len(brought),))],
+        compiler_params=params(),
+        name="again",
+    )(*brought)
     updated = terms + swapped
 
     up = [(i, i + 1) for i in range(slabs - 1)]
@@ -557,18 +562,17 @@
     field_next = pl.pallas_call(
         lambda *refs: field_kernel(local, block, slabs, *refs),
         out_shape=jax.ShapeDtypeStruct((2, local, width_x, width_y), f32),
-        in_specs=[vmem] + [hbm] * 5,
+        in_specs=[vmem, hbm] + [vmem] * 4,
         out_specs=hbm,
         scratch_shapes=[
             pltpu.VMEM((2, local, width_x, width_y), incident.dtype),
             pltpu.VMEM((local, 2, width_x, width_y), f32),
-            *tables,
-            sem((5,)),
+            sem((1,)),
             sem((local,)),
         ],
         compiler_params=params(),
         name="field",
-    )(volume.reshape(lines, width_y), incident, *back_x, *back_y)
+    )(volume.reshape(lines, width_y), incident, *nearer[2:], *nearer[:2])
 
     limits = (place * local).astype(jnp.int32).reshape(1)
     work = pltpu.VMEM((local + 2 * PASSES, width_x + 8, width_y), f32)

time: 93.8 us -> 93.8 us (level)
    all_to_all x1, waiting for transfers between devices: 3.13 us -> 1.99 us  [shards(): lax.all_to_all(volume.reshape(slabs, chunk, width_y), 'slab', 0, 0, tiled...]
    pallas_call x1 -> x2, Pallas kernels: 1.13 us -> 2.27 us  [shards(): pl.pallas_call(lambda *refs: bring_kernel(len(brought), *refs), out_shape...]
  transfers between devices with their start and end apart: 6 -> 6, of which waited for: 5 -> 5; matrix products, arithmetic and copies ran while one was open for 1% -> 1% of each run, Pallas kernels for 9% -> 10%
where the time goes in v5:
time: 93.8 us; the launch traced here: 93.3 us
  starting transfers between devices  34.5 us (37%)
  waiting for transfers between devices  33.4 us (36%)
  Pallas kernels  23.2 us (25%)
  other arithmetic  1.36 us (1%)
    all_to_all x1, waiting for transfers between devices, shards(): lax.all_to_all(packed.reshape(slabs, chunk, width_y), 'slab', 0, 0, tiled...  16.6 us
    all_to_all x1, starting transfers between devices, shards(): lax.all_to_all(packed.reshape(slabs, chunk, width_y), 'slab', 0, 0, tiled...  10.8 us
    ppermute x1, starting transfers between devices, shards(): before = lax.ppermute(updated, 'slab', up)  9.46 us
    all_to_all x1, waiting for transfers between devices, shards(): gathered = lax.all_to_all(spread, 'slab', 0, 0, tiled=True)  8.65 us
    pallas_call x1, Pallas kernels, shards(): pl.pallas_call(lambda *refs: forward_kernel(block, slabs, *refs), out_sha...  5.19 us
    pallas_call x1, Pallas kernels, shards(): pl.pallas_call(lambda *refs: smooth_kernel(depth, *refs), out_shape=jax.S...  4.92 us
    all_to_all x1, starting transfers between devices, shards(): lax.all_to_all(volume.reshape(slabs, chunk, width_y), 'slab', 0, 0, tiled...  4.84 us
    all_to_all x1, starting transfers between devices, shards(): gathered = lax.all_to_all(spread, 'slab', 0, 0, tiled=True)  4.73 us
  transfers between devices with their start and end apart: 6, of which 5 were waited for; matrix products, arithmetic and copies ran while one was open for 1% of the time, Pallas kernels for 10%

profile of v5, /device:TPU:1, one launch (start us, length us, event | category | flops | bytes accessed | tf_op | source)
XLA Modules:
  0.0 93.3 jit_solution(1501558419330057303)
XLA Ops:
  0.6 5.2 %forward.1 = f32[64,4,8,128]{3,2,1,0:T(8,128)} custom-call(f32[2,4,256,128]{3,2,1,0:T(8,128)} %bitcast.25, f32[4,256,128]{2,1,0:T(8,128)} %refs_8_.1, bf16[256,256]{1,0:T(8,128)(2,1)} %constant.104.clone.refs_2_, bf16[256,256]{1,0:T(8,128)(2,1)} %constant.105.clone.refs_3_, bf16[256,256]{1,0:T(8,128)(2,1)} %constant.106.clone.refs_4_, ...), custom_call_target="tpu_custom_call" | custom-call | tf_op jit(solution)/shard_map/forward/pallas_call | solution.py:462
  5.8 10.8 %all-to-all-start = ((f32[64,32,128]{2,1,0:T(8,128)}), f32[64,32,128]{2,1,0:T(8,128)S(1)}, u32[]{:S(2)}, u32[]{:S(2)}) async-start(f32[64,32,128]{2,1,0:T(8,128)} %bitcast.1), calls=%async_computation | async-start | bytes 2097152 | tf_op jit(solution)/shard_map/all_to_all | solution.py:481
  16.7 0.1 cosine_multiply_fusion.1
  16.9 1.1 %fusion.11 = (f32[1,256,128]{2,1,0:T(8,128)S(1)}, f32[1,256,128]{2,1,0:T(8,128)S(1)}, f32[1,256,128]{2,1,0:T(8,128)S(1)}, f32[1,256,128]{2,1,0:T(8,128)S(1)}) fusion(f32[128]{0:T(128)S(1)} %fusion.36, f32[256]{0:T(256)S(1)} %fusion.33, f32[]{:T(128)S(6)} %convert_element_type.53), kind=kLoop, calls=%fused_computation.15 | loop fusion | flops 458752 | bytes 525828 | tf_op jit(solution)/shard_map/mul | solution.py:426
  18.1 0.0 copy-start
  18.1 16.6 %all-to-all-done = f32[64,32,128]{2,1,0:T(8,128)S(1)} async-done(((f32[64,32,128]{2,1,0:T(8,128)}), f32[64,32,128]{2,1,0:T(8,128)S(1)}, u32[]{:S(2)}, u32[]{:S(2)}) %all-to-all-start) | async-done | bytes 1048608 | tf_op jit(solution)/shard_map/all_to_all | solution.py:481
  34.7 0.0 copy-done
  34.7 0.9 detect.1
  35.6 4.7 %all-to-all-start.2 = ((f32[64,8,128]{2,1,0:T(8,128)}), f32[64,8,128]{2,1,0:T(8,128)S(1)}, u32[]{:S(2)}, u32[]{:S(2)}) async-start(f32[64,8,128]{2,1,0:T(8,128)} %get-tuple-element.22), calls=%async_computation.2 | async-start | bytes 524288 | tf_op jit(solution)/shard_map/all_to_all | solution.py:508
  40.4 1.1 %bring.1 = (bf16[256,256]{1,0:T(8,128)(2,1)S(1)}, bf16[256,256]{1,0:T(8,128)(2,1)S(1)}, bf16[256,256]{1,0:T(8,128)(2,1)S(1)}, bf16[256,256]{1,0:T(8,128)(2,1)S(1)}) custom-call(bf16[256,256]{1,0:T(8,128)(2,1)} %constant.108.clone.refs_2_.refs_0_, bf16[256,256]{1,0:T(8,128)(2,1)} %constant.109.clone.refs_3_.refs_1_, ...), custom_call_target="tpu_custom_call" | custom-call | tf_op jit(solution)/shard_map/bring/pallas_call | solution.py:511
  41.5 8.7 %all-to-all-done.2 = f32[64,8,128]{2,1,0:T(8,128)S(1)} async-done(((f32[64,8,128]{2,1,0:T(8,128)}), f32[64,8,128]{2,1,0:T(8,128)S(1)}, u32[]{:S(2)}, u32[]{:S(2)}) %all-to-all-start.2) | async-done | bytes 262176 | tf_op jit(solution)/shard_map/all_to_all | solution.py:508
  50.2 3.1 %gradient.1 = f32[4,256,128]{2,1,0:T(8,128)S(1)} custom-call(f32[512,128]{1,0:T(8,128)S(1)} %bitcast.23, f32[2,256,128]{2,1,0:T(8,128)S(1)} %get-tuple-element.23.refs_1_, f32[2,256,128]{2,1,0:T(8,128)S(1)} %get-tuple-element.24.refs_2_, bf16[256,256]{1,0:T(8,128)(2,1)S(1)} %get-tuple-element.25.refs_3_, bf16[256,256]{1,0:T(8,128)(2,1)S(1)} %get-tuple-element.26.refs_4_, ...), custom_call_target="tpu_custom_call" | custom-call | tf_op jit(solution)/shard_map/gradient/pallas_call | solution.py:520
  53.3 2.7 %collective-permute-start = (f32[4,256,128]{2,1,0:T(8,128)S(1)}, f32[4,256,128]{2,1,0:T(8,128)S(1)}, u32[]{:S(2)}, u32[]{:S(2)}) collective-permute-start(f32[4,256,128]{2,1,0:T(8,128)S(1)} %gradient.1), channel_id=1, source_target_pairs={{0,64},{64,0},{1,65},{65,1},{2,66},{66,2},{3,67},{67,3},{4,68},{68... | collective-permute-start | bytes 1572872 | tf_op jit(solution)/shard_map/ppermute | solution.py:535
  56.0 3.6 %depth.1 = f32[2048,128]{1,0:T(8,128)} custom-call(f32[2048,128]{1,0:T(8,128)S(1)} %bitcast.21, f32[2048,128]{1,0:T(8,128)} %bitcast.27, bf16[256,256]{1,0:T(8,128)(2,1)} %constant.112.clone.refs_2_, bf16[256,256]{1,0:T(8,128)(2,1)} %constant.113.clone.refs_3_, bf16[256,256]{1,0:T(8,128)(2,1)} %constant.114.clone.refs_4_, ...), custom_call_target="tpu_custom_call" | custom-call | tf_op jit(solution)/shard_map/depth/pallas_call | solution.py:536
  59.6 4.8 %all-to-all-start.1 = ((f32[64,32,128]{2,1,0:T(8,128)}), f32[64,32,128]{2,1,0:T(8,128)S(1)}, u32[]{:S(2)}, u32[]{:S(2)}) async-start(f32[64,32,128]{2,1,0:T(8,128)} %bitcast.4), calls=%async_computation.1 | async-start | bytes 2097152 | tf_op jit(solution)/shard_map/all_to_all | solution.py:545
  64.5 3.8 %collective-permute-done = f32[4,256,128]{2,1,0:T(8,128)S(1)} collective-permute-done((f32[4,256,128]{2,1,0:T(8,128)S(1)}, f32[4,256,128]{2,1,0:T(8,128)S(1)}, u32[]{:S(2)}, u32[]{:S(2)}) %collective-permute-start) | collective-permute-done | bytes 524320 | tf_op jit(solution)/shard_map/ppermute | solution.py:535
  68.3 0.1 add.95.refs_2_
  68.4 9.5 %collective-permute-start.1 = (f32[4,256,128]{2,1,0:T(8,128)S(1)}, f32[4,256,128]{2,1,0:T(8,128)S(1)}, u32[]{:S(2)}, u32[]{:S(2)}) collective-permute-start(f32[4,256,128]{2,1,0:T(8,128)S(1)} %add.95.refs_2_), channel_id=1, source_target_pairs={{0,1},{1,2},{2,3},{3,4},{4,5},{5,6},{6,7},{7,8},{8,9},{9,10},{10,1... | collective-permute-start | bytes 1572872 | tf_op jit(solution)/shard_map/ppermute | solution.py:559
  77.8 1.9 %collective-permute-start.2 = (f32[4,256,128]{2,1,0:T(8,128)S(1)}, f32[4,256,128]{2,1,0:T(8,128)S(1)}, u32[]{:S(2)}, u32[]{:S(2)}) collective-permute-start(f32[4,256,128]{2,1,0:T(8,128)S(1)} %add.95.refs_2_), channel_id=1, source_target_pairs={{1,0},{2,1},{3,2},{4,3},{5,4},{6,5},{7,6},{8,7},{9,8},{10,9},{11,1... | collective-permute-start | bytes 1572872 | tf_op jit(solution)/shard_map/ppermute | solution.py:560
  79.8 1.1 %again.1 = (bf16[256,256]{1,0:T(8,128)(2,1)S(1)}, bf16[256,256]{1,0:T(8,128)(2,1)S(1)}, bf16[256,256]{1,0:T(8,128)(2,1)S(1)}, bf16[256,256]{1,0:T(8,128)(2,1)S(1)}) custom-call(bf16[256,256]{1,0:T(8,128)(2,1)} %constant.110.clone.refs_0_.refs_2_, bf16[256,256]{1,0:T(8,128)(2,1)} %constant.111.clone.refs_1_.refs_3_, ...), custom_call_target="tpu_custom_call" | custom-call | tf_op jit(solution)/shard_map/again/pallas_call | solution.py:547
  80.9 2.0 %all-to-all-done.1 = f32[64,32,128]{2,1,0:T(8,128)S(1)} async-done(((f32[64,32,128]{2,1,0:T(8,128)}), f32[64,32,128]{2,1,0:T(8,128)S(1)}, u32[]{:S(2)}, u32[]{:S(2)}) %all-to-all-start.1) | async-done | bytes 1048608 | tf_op jit(solution)/shard_map/all_to_all | solution.py:545
  82.9 3.1 %field.1 = f32[2,4,256,128]{3,2,1,0:T(8,128)} custom-call(f32[2048,128]{1,0:T(8,128)S(1)} %bitcast.22, bf16[2,4,256,128]{3,2,1,0:T(8,128)(2,1)} %bitcast.29, bf16[256,256]{1,0:T(8,128)(2,1)S(1)} %get-tuple-element.17.refs_2_, bf16[256,256]{1,0:T(8,128)(2,1)S(1)} %get-tuple-element.18.refs_3_, bf16[256,256]{1,0:T(8,128)(2,1)S(1)} %get-tuple-element.19.refs_4_, ...), custom_call_target="tpu_custom_call" | custom-call | tf_op jit(solution)/shard_map/field/pallas_call | solution.py:562
  86.0 0.0 collective-permute-done.1.refs_1_
  86.0 2.3 %collective-permute-done.2.refs_3_ = f32[4,256,128]{2,1,0:T(8,128)S(1)} collective-permute-done((f32[4,256,128]{2,1,0:T(8,128)S(1)}, f32[4,256,128]{2,1,0:T(8,128)S(1)}, u32[]{:S(2)}, u32[]{:S(2)}) %collective-permute-start.2) | collective-permute-done | bytes 524320 | tf_op jit(solution)/shard_map/ppermute | solution.py:560
  88.3 4.9 %smooth.1 = f32[4,256,128]{2,1,0:T(8,128)} custom-call(s32[1]{0:T(128)} %bitcast.14.refs_0_, f32[4,256,128]{2,1,0:T(8,128)S(1)} %collective-permute-done.1.refs_1_, f32[4,256,128]{2,1,0:T(8,128)S(1)} %add.95.refs_2_, f32[4,256,128]{2,1,0:T(8,128)S(1)} %collective-permute-done.2.refs_3_), custom_call_target="tpu_custom_call" | custom-call | tf_op jit(solution)/shard_map/smooth/pallas_call | solution.py:579
  (7 shorter events, 0.1 us)
Async XLA Ops:
  5.8 28.9 %all-to-all-start = ((f32[64,32,128]{2,1,0:T(8,128)}), f32[64,32,128]{2,1,0:T(8,128)S(1)}, u32[]{:S(2)}, u32[]{:S(2)}) async-start(f32[64,32,128]{2,1,0:T(8,128)} %bitcast.1), calls=%async_computation | async-start | bytes 2097152 | tf_op jit(solution)/shard_map/all_to_all | solution.py:481
  18.1 16.7 %copy-start = (f32[1,2,4,128]{3,2,1,0:T(4,128)S(1)}, f32[1,2,4,128]{3,2,1,0:T(4,128)}, u32[]{:S(2)}) copy-start(f32[1,2,4,128]{3,2,1,0:T(4,128)} %param.21) | copy-start | bytes 12292
  35.6 14.5 %all-to-all-start.2 = ((f32[64,8,128]{2,1,0:T(8,128)}), f32[64,8,128]{2,1,0:T(8,128)S(1)}, u32[]{:S(2)}, u32[]{:S(2)}) async-start(f32[64,8,128]{2,1,0:T(8,128)} %get-tuple-element.22), calls=%async_computation.2 | async-start | bytes 524288 | tf_op jit(solution)/shard_map/all_to_all | solution.py:508
  53.3 15.0 %collective-permute-start = (f32[4,256,128]{2,1,0:T(8,128)S(1)}, f32[4,256,128]{2,1,0:T(8,128)S(1)}, u32[]{:S(2)}, u32[]{:S(2)}) collective-permute-start(f32[4,256,128]{2,1,0:T(8,128)S(1)} %gradient.1), channel_id=1, source_target_pairs={{0,64},{64,0},{1,65},{65,1},{2,66},{66,2},{3,67},{67,3},{4,68},{68... | collective-permute-start | bytes 1572872 | tf_op jit(solution)/shard_map/ppermute | solution.py:535
  59.6 23.3 %all-to-all-start.1 = ((f32[64,32,128]{2,1,0:T(8,128)}), f32[64,32,128]{2,1,0:T(8,128)S(1)}, u32[]{:S(2)}, u32[]{:S(2)}) async-start(f32[64,32,128]{2,1,0:T(8,128)} %bitcast.4), calls=%async_computation.1 | async-start | bytes 2097152 | tf_op jit(solution)/shard_map/all_to_all | solution.py:545
  68.4 17.7 %collective-permute-start.1 = (f32[4,256,128]{2,1,0:T(8,128)S(1)}, f32[4,256,128]{2,1,0:T(8,128)S(1)}, u32[]{:S(2)}, u32[]{:S(2)}) collective-permute-start(f32[4,256,128]{2,1,0:T(8,128)S(1)} %add.95.refs_2_), channel_id=1, source_target_pairs={{0,1},{1,2},{2,3},{3,4},{4,5},{5,6},{6,7},{7,8},{8,9},{9,10},{10,1... | collective-permute-start | bytes 1572872 | tf_op jit(solution)/shard_map/ppermute | solution.py:559
  77.8 10.5 %collective-permute-start.2 = (f32[4,256,128]{2,1,0:T(8,128)S(1)}, f32[4,256,128]{2,1,0:T(8,128)S(1)}, u32[]{:S(2)}, u32[]{:S(2)}) collective-permute-start(f32[4,256,128]{2,1,0:T(8,128)S(1)} %add.95.refs_2_), channel_id=1, source_target_pairs={{1,0},{2,1},{3,2},{4,3},{5,4},{6,5},{7,6},{8,7},{9,8},{10,9},{11,1... | collective-permute-start | bytes 1572872 | tf_op jit(solution)/shard_map/ppermute | solution.py:560

commit v6 on v5

--- a/solution.py
+++ b/solution.py
@@ -152,12 +152,14 @@
                 copy.wait()
         lower, upper = unfold(product((xhv[...], xlv[...]), split(wide)))
         size = slabs // 2
+        flat = stage.at[plane].reshape(slabs * 2 * block, cv.shape[2])
         for part in range(2):
             mirrored = unalign([upper[part][row * size : (row + 1) * size] for row in range(block)])
             for row in range(block):
                 spot = part * block + row
-                stage[plane, :size, spot, :] = lower[part][row * size : (row + 1) * size]
-                stage[plane, size:, spot, :] = mirrored[row]
+                piece = lower[part][row * size : (row + 1) * size]
+                flat[pl.ds(spot, size, stride=2 * block), :] = piece
+                flat[pl.ds(size * 2 * block + spot, size, stride=2 * block), :] = mirrored[row]
         copy = pltpu.make_async_copy(stage.at[plane], out.at[:, plane], out_sems.at[plane])
         copy.start()
         sent.append(copy)
@@ -304,6 +306,14 @@
     fetched = fetch([incident], [iv], sems)
     stride = local * 2 * block
     copies = []
+
+    def finish(plane):
+        for part in range(2):
+            stage[plane, part] += iv[part, plane].astype(f32)
+        copy = pltpu.make_async_copy(stage.at[plane], out.at[:, plane], out_sems.at[plane])
+        copy.start()
+        copies.append(copy)
+
     for plane in range(local):
         starts = [
             [plane * (2 * block) + part * block + row for row in range(block)]
@@ -312,15 +322,15 @@
         wide = gather_rows(volume, starts, slabs, stride)
         wide = product((xh[...], xl[...]), split(wide))
         wide = product(split(wide), (yh[...], yl[...]))
-        if plane == 0:
+        lanes = wide.shape[1] // 2
+        stage[plane, 0] = wide[:, :lanes]
+        stage[plane, 1] = wide[:, lanes:]
+        if plane == 1:
             for copy in fetched:
                 copy.wait()
-        lanes = wide.shape[1] // 2
-        stage[plane, 0] = iv[0, plane].astype(f32) + wide[:, :lanes]
-        stage[plane, 1] = iv[1, plane].astype(f32) + wide[:, lanes:]
-        copy = pltpu.make_async_copy(stage.at[plane], out.at[:, plane], out_sems.at[plane])
-        copy.start()
-        copies.append(copy)
+        if plane > 0:
+            finish(plane - 1)
+    finish(local - 1)
     for copy in copies:
         copy.wait()
 

time: 93.8 us -> 93.4 us (level)
  no operation moved by 1% of the time
where the time goes in v6:
time: 93.4 us; the launch traced here: 92.8 us
  starting transfers between devices  34.5 us (37%)
  waiting for transfers between devices  33.6 us (36%)
  Pallas kernels  22.5 us (24%)
  other arithmetic  1.36 us (1%)
    all_to_all x1, waiting for transfers between devices, shards(): lax.all_to_all(packed.reshape(slabs, chunk, width_y), 'slab', 0, 0, tiled...  16.6 us
    all_to_all x1, starting transfers between devices, shards(): lax.all_to_all(packed.reshape(slabs, chunk, width_y), 'slab', 0, 0, tiled...  10.8 us
    ppermute x1, starting transfers between devices, shards(): before = lax.ppermute(updated, 'slab', up)  9.46 us
    all_to_all x1, waiting for transfers between devices, shards(): gathered = lax.all_to_all(spread, 'slab', 0, 0, tiled=True)  8.65 us
    pallas_call x1, Pallas kernels, shards(): pl.pallas_call(lambda *refs: smooth_kernel(depth, *refs), out_shape=jax.S...  4.92 us
    all_to_all x1, starting transfers between devices, shards(): lax.all_to_all(volume.reshape(slabs, chunk, width_y), 'slab', 0, 0, tiled...  4.84 us
    pallas_call x1, Pallas kernels, shards(): pl.pallas_call(lambda *refs: forward_kernel(block, slabs, *refs), out_sha...  4.75 us
    all_to_all x1, starting transfers between devices, shards(): gathered = lax.all_to_all(spread, 'slab', 0, 0, tiled=True)  4.73 us
  transfers between devices with their start and end apart: 6, of which 5 were waited for; matrix products, arithmetic and copies ran while one was open for 1% of the time, Pallas kernels for 10%

profile of v6, /device:TPU:1, one launch (start us, length us, event | category | flops | bytes accessed | tf_op | source)
XLA Modules:
  0.0 92.8 jit_solution(10353026065157272430)
XLA Ops:
  0.6 4.8 %forward.1 = f32[64,4,8,128]{3,2,1,0:T(8,128)} custom-call(f32[2,4,256,128]{3,2,1,0:T(8,128)} %bitcast.25, f32[4,256,128]{2,1,0:T(8,128)} %refs_8_.1, bf16[256,256]{1,0:T(8,128)(2,1)} %constant.104.clone.refs_2_, bf16[256,256]{1,0:T(8,128)(2,1)} %constant.105.clone.refs_3_, bf16[256,256]{1,0:T(8,128)(2,1)} %constant.106.clone.refs_4_, ...), custom_call_target="tpu_custom_call" | custom-call | tf_op jit(solution)/shard_map/forward/pallas_call | solution.py:472
  5.4 10.8 %all-to-all-start = ((f32[64,32,128]{2,1,0:T(8,128)}), f32[64,32,128]{2,1,0:T(8,128)S(1)}, u32[]{:S(2)}, u32[]{:S(2)}) async-start(f32[64,32,128]{2,1,0:T(8,128)} %bitcast.1), calls=%async_computation | async-start | bytes 2097152 | tf_op jit(solution)/shard_map/all_to_all | solution.py:491
  16.3 0.1 cosine_multiply_fusion.1
  16.5 1.1 %fusion.11 = (f32[1,256,128]{2,1,0:T(8,128)S(1)}, f32[1,256,128]{2,1,0:T(8,128)S(1)}, f32[1,256,128]{2,1,0:T(8,128)S(1)}, f32[1,256,128]{2,1,0:T(8,128)S(1)}) fusion(f32[128]{0:T(128)S(1)} %fusion.36, f32[256]{0:T(256)S(1)} %fusion.33, f32[]{:T(128)S(6)} %convert_element_type.53), kind=kLoop, calls=%fused_computation.15 | loop fusion | flops 458752 | bytes 525828 | tf_op jit(solution)/shard_map/mul | solution.py:436
  17.6 0.0 copy-start
  17.6 16.6 %all-to-all-done = f32[64,32,128]{2,1,0:T(8,128)S(1)} async-done(((f32[64,32,128]{2,1,0:T(8,128)}), f32[64,32,128]{2,1,0:T(8,128)S(1)}, u32[]{:S(2)}, u32[]{:S(2)}) %all-to-all-start) | async-done | bytes 1048608 | tf_op jit(solution)/shard_map/all_to_all | solution.py:491
  34.3 0.0 copy-done
  34.3 0.9 detect.1
  35.2 4.7 %all-to-all-start.2 = ((f32[64,8,128]{2,1,0:T(8,128)}), f32[64,8,128]{2,1,0:T(8,128)S(1)}, u32[]{:S(2)}, u32[]{:S(2)}) async-start(f32[64,8,128]{2,1,0:T(8,128)} %get-tuple-element.22), calls=%async_computation.2 | async-start | bytes 524288 | tf_op jit(solution)/shard_map/all_to_all | solution.py:518
  39.9 1.1 %bring.1 = (bf16[256,256]{1,0:T(8,128)(2,1)S(1)}, bf16[256,256]{1,0:T(8,128)(2,1)S(1)}, bf16[256,256]{1,0:T(8,128)(2,1)S(1)}, bf16[256,256]{1,0:T(8,128)(2,1)S(1)}) custom-call(bf16[256,256]{1,0:T(8,128)(2,1)} %constant.108.clone.refs_2_.refs_0_, bf16[256,256]{1,0:T(8,128)(2,1)} %constant.109.clone.refs_3_.refs_1_, ...), custom_call_target="tpu_custom_call" | custom-call | tf_op jit(solution)/shard_map/bring/pallas_call | solution.py:521
  41.1 8.7 %all-to-all-done.2 = f32[64,8,128]{2,1,0:T(8,128)S(1)} async-done(((f32[64,8,128]{2,1,0:T(8,128)}), f32[64,8,128]{2,1,0:T(8,128)S(1)}, u32[]{:S(2)}, u32[]{:S(2)}) %all-to-all-start.2) | async-done | bytes 262176 | tf_op jit(solution)/shard_map/all_to_all | solution.py:518
  49.7 3.1 %gradient.1 = f32[4,256,128]{2,1,0:T(8,128)S(1)} custom-call(f32[512,128]{1,0:T(8,128)S(1)} %bitcast.23, f32[2,256,128]{2,1,0:T(8,128)S(1)} %get-tuple-element.23.refs_1_, f32[2,256,128]{2,1,0:T(8,128)S(1)} %get-tuple-element.24.refs_2_, bf16[256,256]{1,0:T(8,128)(2,1)S(1)} %get-tuple-element.25.refs_3_, bf16[256,256]{1,0:T(8,128)(2,1)S(1)} %get-tuple-element.26.refs_4_, ...), custom_call_target="tpu_custom_call" | custom-call | tf_op jit(solution)/shard_map/gradient/pallas_call | solution.py:530
  52.9 2.7 %collective-permute-start = (f32[4,256,128]{2,1,0:T(8,128)S(1)}, f32[4,256,128]{2,1,0:T(8,128)S(1)}, u32[]{:S(2)}, u32[]{:S(2)}) collective-permute-start(f32[4,256,128]{2,1,0:T(8,128)S(1)} %gradient.1), channel_id=1, source_target_pairs={{0,64},{64,0},{1,65},{65,1},{2,66},{66,2},{3,67},{67,3},{4,68},{68... | collective-permute-start | bytes 1572872 | tf_op jit(solution)/shard_map/ppermute | solution.py:545
  55.5 3.6 %depth.1 = f32[2048,128]{1,0:T(8,128)} custom-call(f32[2048,128]{1,0:T(8,128)S(1)} %bitcast.21, f32[2048,128]{1,0:T(8,128)} %bitcast.27, bf16[256,256]{1,0:T(8,128)(2,1)} %constant.112.clone.refs_2_, bf16[256,256]{1,0:T(8,128)(2,1)} %constant.113.clone.refs_3_, bf16[256,256]{1,0:T(8,128)(2,1)} %constant.114.clone.refs_4_, ...), custom_call_target="tpu_custom_call" | custom-call | tf_op jit(solution)/shard_map/depth/pallas_call | solution.py:546
  59.2 4.8 %all-to-all-start.1 = ((f32[64,32,128]{2,1,0:T(8,128)}), f32[64,32,128]{2,1,0:T(8,128)S(1)}, u32[]{:S(2)}, u32[]{:S(2)}) async-start(f32[64,32,128]{2,1,0:T(8,128)} %bitcast.4), calls=%async_computation.1 | async-start | bytes 2097152 | tf_op jit(solution)/shard_map/all_to_all | solution.py:555
  64.0 3.8 %collective-permute-done = f32[4,256,128]{2,1,0:T(8,128)S(1)} collective-permute-done((f32[4,256,128]{2,1,0:T(8,128)S(1)}, f32[4,256,128]{2,1,0:T(8,128)S(1)}, u32[]{:S(2)}, u32[]{:S(2)}) %collective-permute-start) | collective-permute-done | bytes 524320 | tf_op jit(solution)/shard_map/ppermute | solution.py:545
  67.9 0.1 add.95.refs_2_
  67.9 9.5 %collective-permute-start.1 = (f32[4,256,128]{2,1,0:T(8,128)S(1)}, f32[4,256,128]{2,1,0:T(8,128)S(1)}, u32[]{:S(2)}, u32[]{:S(2)}) collective-permute-start(f32[4,256,128]{2,1,0:T(8,128)S(1)} %add.95.refs_2_), channel_id=1, source_target_pairs={{0,1},{1,2},{2,3},{3,4},{4,5},{5,6},{6,7},{7,8},{8,9},{9,10},{10,1... | collective-permute-start | bytes 1572872 | tf_op jit(solution)/shard_map/ppermute | solution.py:569
  77.4 1.9 %collective-permute-start.2 = (f32[4,256,128]{2,1,0:T(8,128)S(1)}, f32[4,256,128]{2,1,0:T(8,128)S(1)}, u32[]{:S(2)}, u32[]{:S(2)}) collective-permute-start(f32[4,256,128]{2,1,0:T(8,128)S(1)} %add.95.refs_2_), channel_id=1, source_target_pairs={{1,0},{2,1},{3,2},{4,3},{5,4},{6,5},{7,6},{8,7},{9,8},{10,9},{11,1... | collective-permute-start | bytes 1572872 | tf_op jit(solution)/shard_map/ppermute | solution.py:570
  79.3 1.1 %again.1 = (bf16[256,256]{1,0:T(8,128)(2,1)S(1)}, bf16[256,256]{1,0:T(8,128)(2,1)S(1)}, bf16[256,256]{1,0:T(8,128)(2,1)S(1)}, bf16[256,256]{1,0:T(8,128)(2,1)S(1)}) custom-call(bf16[256,256]{1,0:T(8,128)(2,1)} %constant.110.clone.refs_0_.refs_2_, bf16[256,256]{1,0:T(8,128)(2,1)} %constant.111.clone.refs_1_.refs_3_, ...), custom_call_target="tpu_custom_call" | custom-call | tf_op jit(solution)/shard_map/again/pallas_call | solution.py:557
  80.5 2.0 %all-to-all-done.1 = f32[64,32,128]{2,1,0:T(8,128)S(1)} async-done(((f32[64,32,128]{2,1,0:T(8,128)}), f32[64,32,128]{2,1,0:T(8,128)S(1)}, u32[]{:S(2)}, u32[]{:S(2)}) %all-to-all-start.1) | async-done | bytes 1048608 | tf_op jit(solution)/shard_map/all_to_all | solution.py:555
  82.5 2.9 %field.1 = f32[2,4,256,128]{3,2,1,0:T(8,128)} custom-call(f32[2048,128]{1,0:T(8,128)S(1)} %bitcast.22, bf16[2,4,256,128]{3,2,1,0:T(8,128)(2,1)} %bitcast.29, bf16[256,256]{1,0:T(8,128)(2,1)S(1)} %get-tuple-element.17.refs_2_, bf16[256,256]{1,0:T(8,128)(2,1)S(1)} %get-tuple-element.18.refs_3_, bf16[256,256]{1,0:T(8,128)(2,1)S(1)} %get-tuple-element.19.refs_4_, ...), custom_call_target="tpu_custom_call" | custom-call | tf_op jit(solution)/shard_map/field/pallas_call | solution.py:572
  85.4 0.0 collective-permute-done.1.refs_1_
  85.4 2.5 %collective-permute-done.2.refs_3_ = f32[4,256,128]{2,1,0:T(8,128)S(1)} collective-permute-done((f32[4,256,128]{2,1,0:T(8,128)S(1)}, f32[4,256,128]{2,1,0:T(8,128)S(1)}, u32[]{:S(2)}, u32[]{:S(2)}) %collective-permute-start.2) | collective-permute-done | bytes 524320 | tf_op jit(solution)/shard_map/ppermute | solution.py:570
  87.9 4.9 %smooth.1 = f32[4,256,128]{2,1,0:T(8,128)} custom-call(s32[1]{0:T(128)} %bitcast.14.refs_0_, f32[4,256,128]{2,1,0:T(8,128)S(1)} %collective-permute-done.1.refs_1_, f32[4,256,128]{2,1,0:T(8,128)S(1)} %add.95.refs_2_, f32[4,256,128]{2,1,0:T(8,128)S(1)} %collective-permute-done.2.refs_3_), custom_call_target="tpu_custom_call" | custom-call | tf_op jit(solution)/shard_map/smooth/pallas_call | solution.py:589
  (7 shorter events, 0.1 us)
Async XLA Ops:
  5.4 28.9 %all-to-all-start = ((f32[64,32,128]{2,1,0:T(8,128)}), f32[64,32,128]{2,1,0:T(8,128)S(1)}, u32[]{:S(2)}, u32[]{:S(2)}) async-start(f32[64,32,128]{2,1,0:T(8,128)} %bitcast.1), calls=%async_computation | async-start | bytes 2097152 | tf_op jit(solution)/shard_map/all_to_all | solution.py:491
  17.6 16.7 %copy-start = (f32[1,2,4,128]{3,2,1,0:T(4,128)S(1)}, f32[1,2,4,128]{3,2,1,0:T(4,128)}, u32[]{:S(2)}) copy-start(f32[1,2,4,128]{3,2,1,0:T(4,128)} %param.21) | copy-start | bytes 12292
  35.2 14.5 %all-to-all-start.2 = ((f32[64,8,128]{2,1,0:T(8,128)}), f32[64,8,128]{2,1,0:T(8,128)S(1)}, u32[]{:S(2)}, u32[]{:S(2)}) async-start(f32[64,8,128]{2,1,0:T(8,128)} %get-tuple-element.22), calls=%async_computation.2 | async-start | bytes 524288 | tf_op jit(solution)/shard_map/all_to_all | solution.py:518
  52.9 15.0 %collective-permute-start = (f32[4,256,128]{2,1,0:T(8,128)S(1)}, f32[4,256,128]{2,1,0:T(8,128)S(1)}, u32[]{:S(2)}, u32[]{:S(2)}) collective-permute-start(f32[4,256,128]{2,1,0:T(8,128)S(1)} %gradient.1), channel_id=1, source_target_pairs={{0,64},{64,0},{1,65},{65,1},{2,66},{66,2},{3,67},{67,3},{4,68},{68... | collective-permute-start | bytes 1572872 | tf_op jit(solution)/shard_map/ppermute | solution.py:545
  59.2 23.3 %all-to-all-start.1 = ((f32[64,32,128]{2,1,0:T(8,128)}), f32[64,32,128]{2,1,0:T(8,128)S(1)}, u32[]{:S(2)}, u32[]{:S(2)}) async-start(f32[64,32,128]{2,1,0:T(8,128)} %bitcast.4), calls=%async_computation.1 | async-start | bytes 2097152 | tf_op jit(solution)/shard_map/all_to_all | solution.py:555
  67.9 17.5 %collective-permute-start.1 = (f32[4,256,128]{2,1,0:T(8,128)S(1)}, f32[4,256,128]{2,1,0:T(8,128)S(1)}, u32[]{:S(2)}, u32[]{:S(2)}) collective-permute-start(f32[4,256,128]{2,1,0:T(8,128)S(1)} %add.95.refs_2_), channel_id=1, source_target_pairs={{0,1},{1,2},{2,3},{3,4},{4,5},{5,6},{6,7},{7,8},{8,9},{9,10},{10,1... | collective-permute-start | bytes 1572872 | tf_op jit(solution)/shard_map/ppermute | solution.py:569
  77.4 10.5 %collective-permute-start.2 = (f32[4,256,128]{2,1,0:T(8,128)S(1)}, f32[4,256,128]{2,1,0:T(8,128)S(1)}, u32[]{:S(2)}, u32[]{:S(2)}) collective-permute-start(f32[4,256,128]{2,1,0:T(8,128)S(1)} %add.95.refs_2_), channel_id=1, source_target_pairs={{1,0},{2,1},{3,2},{4,3},{5,4},{6,5},{7,6},{8,7},{9,8},{10,9},{11,1... | collective-permute-start | bytes 1572872 | tf_op jit(solution)/shard_map/ppermute | solution.py:570

commit v7 on v6

--- a/solution.py
+++ b/solution.py
@@ -249,6 +249,7 @@
     cv,
     miss,
     hold,
+    ready,
     sems,
 ):
     local = cv.shape[0]
@@ -266,6 +267,12 @@
     starts = [[part * block + row for row in range(block)] for part in range(2)]
     miss[...] = gather_rows(gathered, starts, slabs, 2 * block) * (1.0 / root_depth)
     hold[...] = prop[...]
+
+    def finish(plane):
+        for copy in copies(plane):
+            copy.wait()
+        terms = fv[plane, 0] * ready[:, :lanes] + fv[plane, 1] * ready[:, lanes:]
+        out[plane] = (0.5 / diffusion) * cv[plane] - (step_size / diffusion) * terms
 
     def body(count, carry):
         plane = local - 1 - count
@@ -278,13 +285,16 @@
         hold[1] = real * step[1] + imag * step[0]
         wide = product((xh[...], xl[...]), split(wide))
         wide = product(split(wide), (yh[...], yl[...]))
-        for copy in copies(plane):
-            copy.wait()
-        terms = fv[plane, 0] * wide[:, :lanes] + fv[plane, 1] * wide[:, lanes:]
-        out[plane] = (0.5 / diffusion) * cv[plane] - (step_size / diffusion) * terms
+
+        @pl.when(count > 0)
+        def _():
+            finish(plane + 1)
+
+        ready[...] = wide
         return carry
 
     lax.fori_loop(0, local, body, 0)
+    finish(0)
 
 
 def field_kernel(
@@ -537,6 +547,7 @@
             pltpu.VMEM((local, width_x, width_y), f32),
             pltpu.VMEM((width_x, 2 * width_y), f32),
             pltpu.VMEM((2, width_x, width_y), f32),
+            pltpu.VMEM((width_x, 2 * width_y), f32),
             sem((2, local)),
         ],
         compiler_params=params(),

time: 93.4 us -> 93.2 us (level)
  no operation moved by 1% of the time
where the time goes in v7:
time: 93.2 us; the launch traced here: 92.6 us
  starting transfers between devices  34.5 us (37%)
  waiting for transfers between devices  33.6 us (36%)
  Pallas kernels  22.3 us (24%)
  other arithmetic  1.36 us (1%)
    all_to_all x1, waiting for transfers between devices, shards(): lax.all_to_all(packed.reshape(slabs, chunk, width_y), 'slab', 0, 0, tiled...  16.6 us
    all_to_all x1, starting transfers between devices, shards(): lax.all_to_all(packed.reshape(slabs, chunk, width_y), 'slab', 0, 0, tiled...  10.8 us
    ppermute x1, starting transfers between devices, shards(): before = lax.ppermute(updated, 'slab', up)  9.46 us
    all_to_all x1, waiting for transfers between devices, shards(): gathered = lax.all_to_all(spread, 'slab', 0, 0, tiled=True)  8.65 us
    pallas_call x1, Pallas kernels, shards(): pl.pallas_call(lambda *refs: smooth_kernel(depth, *refs), out_shape=jax.S...  4.92 us
    all_to_all x1, starting transfers between devices, shards(): lax.all_to_all(volume.reshape(slabs, chunk, width_y), 'slab', 0, 0, tiled...  4.84 us
    pallas_call x1, Pallas kernels, shards(): pl.pallas_call(lambda *refs: forward_kernel(block, slabs, *refs), out_sha...  4.75 us
    all_to_all x1, starting transfers between devices, shards(): gathered = lax.all_to_all(spread, 'slab', 0, 0, tiled=True)  4.73 us
  transfers between devices with their start and end apart: 6, of which 5 were waited for; matrix products, arithmetic and copies ran while one was open for 1% of the time, Pallas kernels for 10%

profile of v7, /device:TPU:1, one launch (start us, length us, event | category | flops | bytes accessed | tf_op | source)
XLA Modules:
  0.0 92.6 jit_solution(2681410915961069470)
XLA Ops:
  0.6 4.8 %forward.1 = f32[64,4,8,128]{3,2,1,0:T(8,128)} custom-call(f32[2,4,256,128]{3,2,1,0:T(8,128)} %bitcast.25, f32[4,256,128]{2,1,0:T(8,128)} %refs_8_.1, bf16[256,256]{1,0:T(8,128)(2,1)} %constant.104.clone.refs_2_, bf16[256,256]{1,0:T(8,128)(2,1)} %constant.105.clone.refs_3_, bf16[256,256]{1,0:T(8,128)(2,1)} %constant.106.clone.refs_4_, ...), custom_call_target="tpu_custom_call" | custom-call | tf_op jit(solution)/shard_map/forward/pallas_call | solution.py:482
  5.4 10.8 %all-to-all-start = ((f32[64,32,128]{2,1,0:T(8,128)}), f32[64,32,128]{2,1,0:T(8,128)S(1)}, u32[]{:S(2)}, u32[]{:S(2)}) async-start(f32[64,32,128]{2,1,0:T(8,128)} %bitcast.1), calls=%async_computation | async-start | bytes 2097152 | tf_op jit(solution)/shard_map/all_to_all | solution.py:501
  16.3 0.1 cosine_multiply_fusion.1
  16.5 1.1 %fusion.11 = (f32[1,256,128]{2,1,0:T(8,128)S(1)}, f32[1,256,128]{2,1,0:T(8,128)S(1)}, f32[1,256,128]{2,1,0:T(8,128)S(1)}, f32[1,256,128]{2,1,0:T(8,128)S(1)}) fusion(f32[128]{0:T(128)S(1)} %fusion.36, f32[256]{0:T(256)S(1)} %fusion.33, f32[]{:T(128)S(6)} %convert_element_type.53), kind=kLoop, calls=%fused_computation.15 | loop fusion | flops 458752 | bytes 525828 | tf_op jit(solution)/shard_map/mul | solution.py:446
  17.6 0.0 copy-start
  17.6 16.6 %all-to-all-done = f32[64,32,128]{2,1,0:T(8,128)S(1)} async-done(((f32[64,32,128]{2,1,0:T(8,128)}), f32[64,32,128]{2,1,0:T(8,128)S(1)}, u32[]{:S(2)}, u32[]{:S(2)}) %all-to-all-start) | async-done | bytes 1048608 | tf_op jit(solution)/shard_map/all_to_all | solution.py:501
  34.3 0.0 copy-done
  34.3 0.9 detect.1
  35.2 4.7 %all-to-all-start.2 = ((f32[64,8,128]{2,1,0:T(8,128)}), f32[64,8,128]{2,1,0:T(8,128)S(1)}, u32[]{:S(2)}, u32[]{:S(2)}) async-start(f32[64,8,128]{2,1,0:T(8,128)} %get-tuple-element.22), calls=%async_computation.2 | async-start | bytes 524288 | tf_op jit(solution)/shard_map/all_to_all | solution.py:528
  39.9 1.1 %bring.1 = (bf16[256,256]{1,0:T(8,128)(2,1)S(1)}, bf16[256,256]{1,0:T(8,128)(2,1)S(1)}, bf16[256,256]{1,0:T(8,128)(2,1)S(1)}, bf16[256,256]{1,0:T(8,128)(2,1)S(1)}) custom-call(bf16[256,256]{1,0:T(8,128)(2,1)} %constant.108.clone.refs_2_.refs_0_, bf16[256,256]{1,0:T(8,128)(2,1)} %constant.109.clone.refs_3_.refs_1_, ...), custom_call_target="tpu_custom_call" | custom-call | tf_op jit(solution)/shard_map/bring/pallas_call | solution.py:531
  41.1 8.7 %all-to-all-done.2 = f32[64,8,128]{2,1,0:T(8,128)S(1)} async-done(((f32[64,8,128]{2,1,0:T(8,128)}), f32[64,8,128]{2,1,0:T(8,128)S(1)}, u32[]{:S(2)}, u32[]{:S(2)}) %all-to-all-start.2) | async-done | bytes 262176 | tf_op jit(solution)/shard_map/all_to_all | solution.py:528
  49.7 2.9 %gradient.1 = f32[4,256,128]{2,1,0:T(8,128)S(1)} custom-call(f32[512,128]{1,0:T(8,128)S(1)} %bitcast.23, f32[2,256,128]{2,1,0:T(8,128)S(1)} %get-tuple-element.23.refs_1_, f32[2,256,128]{2,1,0:T(8,128)S(1)} %get-tuple-element.24.refs_2_, bf16[256,256]{1,0:T(8,128)(2,1)S(1)} %get-tuple-element.25.refs_3_, bf16[256,256]{1,0:T(8,128)(2,1)S(1)} %get-tuple-element.26.refs_4_, ...), custom_call_target="tpu_custom_call" | custom-call | tf_op jit(solution)/shard_map/gradient/pallas_call | solution.py:540
  52.7 2.7 %collective-permute-start = (f32[4,256,128]{2,1,0:T(8,128)S(1)}, f32[4,256,128]{2,1,0:T(8,128)S(1)}, u32[]{:S(2)}, u32[]{:S(2)}) collective-permute-start(f32[4,256,128]{2,1,0:T(8,128)S(1)} %gradient.1), channel_id=1, source_target_pairs={{0,64},{64,0},{1,65},{65,1},{2,66},{66,2},{3,67},{67,3},{4,68},{68... | collective-permute-start | bytes 1572872 | tf_op jit(solution)/shard_map/ppermute | solution.py:556
  55.4 3.6 %depth.1 = f32[2048,128]{1,0:T(8,128)} custom-call(f32[2048,128]{1,0:T(8,128)S(1)} %bitcast.21, f32[2048,128]{1,0:T(8,128)} %bitcast.27, bf16[256,256]{1,0:T(8,128)(2,1)} %constant.112.clone.refs_2_, bf16[256,256]{1,0:T(8,128)(2,1)} %constant.113.clone.refs_3_, bf16[256,256]{1,0:T(8,128)(2,1)} %constant.114.clone.refs_4_, ...), custom_call_target="tpu_custom_call" | custom-call | tf_op jit(solution)/shard_map/depth/pallas_call | solution.py:557
  59.0 4.8 %all-to-all-start.1 = ((f32[64,32,128]{2,1,0:T(8,128)}), f32[64,32,128]{2,1,0:T(8,128)S(1)}, u32[]{:S(2)}, u32[]{:S(2)}) async-start(f32[64,32,128]{2,1,0:T(8,128)} %bitcast.4), calls=%async_computation.1 | async-start | bytes 2097152 | tf_op jit(solution)/shard_map/all_to_all | solution.py:566
  63.8 3.8 %collective-permute-done = f32[4,256,128]{2,1,0:T(8,128)S(1)} collective-permute-done((f32[4,256,128]{2,1,0:T(8,128)S(1)}, f32[4,256,128]{2,1,0:T(8,128)S(1)}, u32[]{:S(2)}, u32[]{:S(2)}) %collective-permute-start) | collective-permute-done | bytes 524320 | tf_op jit(solution)/shard_map/ppermute | solution.py:556
  67.7 0.1 add.95.refs_2_
  67.7 9.5 %collective-permute-start.1 = (f32[4,256,128]{2,1,0:T(8,128)S(1)}, f32[4,256,128]{2,1,0:T(8,128)S(1)}, u32[]{:S(2)}, u32[]{:S(2)}) collective-permute-start(f32[4,256,128]{2,1,0:T(8,128)S(1)} %add.95.refs_2_), channel_id=1, source_target_pairs={{0,1},{1,2},{2,3},{3,4},{4,5},{5,6},{6,7},{7,8},{8,9},{9,10},{10,1... | collective-permute-start | bytes 1572872 | tf_op jit(solution)/shard_map/ppermute | solution.py:580
  77.2 1.9 %collective-permute-start.2 = (f32[4,256,128]{2,1,0:T(8,128)S(1)}, f32[4,256,128]{2,1,0:T(8,128)S(1)}, u32[]{:S(2)}, u32[]{:S(2)}) collective-permute-start(f32[4,256,128]{2,1,0:T(8,128)S(1)} %add.95.refs_2_), channel_id=1, source_target_pairs={{1,0},{2,1},{3,2},{4,3},{5,4},{6,5},{7,6},{8,7},{9,8},{10,9},{11,1... | collective-permute-start | bytes 1572872 | tf_op jit(solution)/shard_map/ppermute | solution.py:581
  79.1 1.1 %again.1 = (bf16[256,256]{1,0:T(8,128)(2,1)S(1)}, bf16[256,256]{1,0:T(8,128)(2,1)S(1)}, bf16[256,256]{1,0:T(8,128)(2,1)S(1)}, bf16[256,256]{1,0:T(8,128)(2,1)S(1)}) custom-call(bf16[256,256]{1,0:T(8,128)(2,1)} %constant.110.clone.refs_0_.refs_2_, bf16[256,256]{1,0:T(8,128)(2,1)} %constant.111.clone.refs_1_.refs_3_, ...), custom_call_target="tpu_custom_call" | custom-call | tf_op jit(solution)/shard_map/again/pallas_call | solution.py:568
  80.3 2.0 %all-to-all-done.1 = f32[64,32,128]{2,1,0:T(8,128)S(1)} async-done(((f32[64,32,128]{2,1,0:T(8,128)}), f32[64,32,128]{2,1,0:T(8,128)S(1)}, u32[]{:S(2)}, u32[]{:S(2)}) %all-to-all-start.1) | async-done | bytes 1048608 | tf_op jit(solution)/shard_map/all_to_all | solution.py:566
  82.3 2.9 %field.1 = f32[2,4,256,128]{3,2,1,0:T(8,128)} custom-call(f32[2048,128]{1,0:T(8,128)S(1)} %bitcast.22, bf16[2,4,256,128]{3,2,1,0:T(8,128)(2,1)} %bitcast.29, bf16[256,256]{1,0:T(8,128)(2,1)S(1)} %get-tuple-element.17.refs_2_, bf16[256,256]{1,0:T(8,128)(2,1)S(1)} %get-tuple-element.18.refs_3_, bf16[256,256]{1,0:T(8,128)(2,1)S(1)} %get-tuple-element.19.refs_4_, ...), custom_call_target="tpu_custom_call" | custom-call | tf_op jit(solution)/shard_map/field/pallas_call | solution.py:583
  85.2 0.0 collective-permute-done.1.refs_1_
  85.2 2.5 %collective-permute-done.2.refs_3_ = f32[4,256,128]{2,1,0:T(8,128)S(1)} collective-permute-done((f32[4,256,128]{2,1,0:T(8,128)S(1)}, f32[4,256,128]{2,1,0:T(8,128)S(1)}, u32[]{:S(2)}, u32[]{:S(2)}) %collective-permute-start.2) | collective-permute-done | bytes 524320 | tf_op jit(solution)/shard_map/ppermute | solution.py:581
  87.7 4.9 %smooth.1 = f32[4,256,128]{2,1,0:T(8,128)} custom-call(s32[1]{0:T(128)} %bitcast.14.refs_0_, f32[4,256,128]{2,1,0:T(8,128)S(1)} %collective-permute-done.1.refs_1_, f32[4,256,128]{2,1,0:T(8,128)S(1)} %add.95.refs_2_, f32[4,256,128]{2,1,0:T(8,128)S(1)} %collective-permute-done.2.refs_3_), custom_call_target="tpu_custom_call" | custom-call | tf_op jit(solution)/shard_map/smooth/pallas_call | solution.py:600
  (7 shorter events, 0.1 us)
Async XLA Ops:
  5.4 28.9 %all-to-all-start = ((f32[64,32,128]{2,1,0:T(8,128)}), f32[64,32,128]{2,1,0:T(8,128)S(1)}, u32[]{:S(2)}, u32[]{:S(2)}) async-start(f32[64,32,128]{2,1,0:T(8,128)} %bitcast.1), calls=%async_computation | async-start | bytes 2097152 | tf_op jit(solution)/shard_map/all_to_all | solution.py:501
  17.6 16.7 %copy-start = (f32[1,2,4,128]{3,2,1,0:T(4,128)S(1)}, f32[1,2,4,128]{3,2,1,0:T(4,128)}, u32[]{:S(2)}) copy-start(f32[1,2,4,128]{3,2,1,0:T(4,128)} %param.21) | copy-start | bytes 12292
  35.2 14.5 %all-to-all-start.2 = ((f32[64,8,128]{2,1,0:T(8,128)}), f32[64,8,128]{2,1,0:T(8,128)S(1)}, u32[]{:S(2)}, u32[]{:S(2)}) async-start(f32[64,8,128]{2,1,0:T(8,128)} %get-tuple-element.22), calls=%async_computation.2 | async-start | bytes 524288 | tf_op jit(solution)/shard_map/all_to_all | solution.py:528
  52.7 15.0 %collective-permute-start = (f32[4,256,128]{2,1,0:T(8,128)S(1)}, f32[4,256,128]{2,1,0:T(8,128)S(1)}, u32[]{:S(2)}, u32[]{:S(2)}) collective-permute-start(f32[4,256,128]{2,1,0:T(8,128)S(1)} %gradient.1), channel_id=1, source_target_pairs={{0,64},{64,0},{1,65},{65,1},{2,66},{66,2},{3,67},{67,3},{4,68},{68... | collective-permute-start | bytes 1572872 | tf_op jit(solution)/shard_map/ppermute | solution.py:556
  59.0 23.3 %all-to-all-start.1 = ((f32[64,32,128]{2,1,0:T(8,128)}), f32[64,32,128]{2,1,0:T(8,128)S(1)}, u32[]{:S(2)}, u32[]{:S(2)}) async-start(f32[64,32,128]{2,1,0:T(8,128)} %bitcast.4), calls=%async_computation.1 | async-start | bytes 2097152 | tf_op jit(solution)/shard_map/all_to_all | solution.py:566
  67.7 17.5 %collective-permute-start.1 = (f32[4,256,128]{2,1,0:T(8,128)S(1)}, f32[4,256,128]{2,1,0:T(8,128)S(1)}, u32[]{:S(2)}, u32[]{:S(2)}) collective-permute-start(f32[4,256,128]{2,1,0:T(8,128)S(1)} %add.95.refs_2_), channel_id=1, source_target_pairs={{0,1},{1,2},{2,3},{3,4},{4,5},{5,6},{6,7},{7,8},{8,9},{9,10},{10,1... | collective-permute-start | bytes 1572872 | tf_op jit(solution)/shard_map/ppermute | solution.py:580
  77.2 10.5 %collective-permute-start.2 = (f32[4,256,128]{2,1,0:T(8,128)S(1)}, f32[4,256,128]{2,1,0:T(8,128)S(1)}, u32[]{:S(2)}, u32[]{:S(2)}) collective-permute-start(f32[4,256,128]{2,1,0:T(8,128)S(1)} %add.95.refs_2_), channel_id=1, source_target_pairs={{1,0},{2,1},{3,2},{4,3},{5,4},{6,5},{7,6},{8,7},{9,8},{10,9},{11,1... | collective-permute-start | bytes 1572872 | tf_op jit(solution)/shard_map/ppermute | solution.py:581
